TPU v7x, 32 devices: a whole 2x2x4 slice. The times are simulated.
32 devices in a mesh: band: 4 (over y, x), domain: 8 (over z, core).
Axes of the slice: x: 2, y: 2, z: 4, core: 2. Of those that a mesh axis runs over, the one named last changes fastest.
Arguments:
- orbitals: float32 [6144, 512], P('domain', 'band'), may hold values from -6 to 6
- potential: float32 [6144], P('domain'), may hold values from -1 to 1
- occupation: float32 [512], P('band'), may hold values from 0 to 0.0068359375, as said below
- cell_matrix: bfloat16 [343, 343], replicated, may hold values from -1 to 2, as said below
- cell_nodes: int32 [32, 343], P('domain'), may hold values from 0 to 936, as said below
- face_order: int32 [8, 169], P('domain'), may hold values from 0 to 168, as said below
- pois_matrix: float32 [729, 729], replicated, may hold values from -1 to 2, as said below
- pois_nodes: int32 [16, 729], P('domain'), may hold values from 0 to 848, as said below
- pois_face: int32 [8, 81], P('domain'), may hold values from 0 to 80, as said below
- screening: float32 [6144], P('domain'), may hold values from 0.5 to 2
- block_owner: int32 [8, 8], P('domain'), may hold values from 0 to 7, as said below
Outputs:
- filtered: float32 [6144, 512], P('domain', 'band')
- hartree: float32 [6144], P('domain')
Inputs may be any that keep to these rules, and one draw needn't show every extreme that they name: `occupation`: positive weights. `cell_matrix`: symmetric. `pois_matrix`: symmetric. `cell_nodes`: cell c (counted from 0 within its domain) uses the local nodes (c * 234 + k) mod 937 for k < 343, in a drawn order. `pois_nodes`: cell c (counted from 0 within its domain) uses the local nodes (c * 424 + k) mod 849 for k < 729, in a drawn order. `face_order`: each row is a permutation. `pois_face`: each row is a permutation. `block_owner`: each row is a permutation.
All inputs are finite; a program needn't handle non-finite values.
Results may differ from a plain program's by a relative error of at most 0.0065.
The roundings to bfloat16 on the way count: a program that leaves them out, or rounds other values in their place, can miss the bound.
Values may be sent and summed in bfloat16 or wider, within the bound.
No kernel may reach another device: no remote copies, remote signals or barrier semaphores. Data moves between devices by JAX's collectives and lax.ppermute only.
A program may use at most 64 MiB of HBM per device.

v0:
```python
import functools

import jax
import jax.numpy as jnp
from jax import lax
from jax.experimental import pallas as pl
from jax.experimental.pallas import tpu as pltpu
from jax.sharding import PartitionSpec as P

filter_center = 1.8
filter_half = 2.7
solve_center = 3.25
solve_half = 2.75
solve_ratio = solve_center / solve_half
weight_zero = 1.0 / solve_ratio
weight_one = 1.0 / (2.0 * solve_ratio - weight_zero)
weight_two = 1.0 / (2.0 * solve_ratio - weight_one)

BF = jnp.bfloat16
F32 = jnp.float32
I32 = jnp.int32
LANES = 128
SUBLANES = 8


def up_to(n, m):
    return -(-n // m) * m


def from_behind(array, axis, by):
    length = lax.axis_size(axis)
    return lax.ppermute(array, axis, [(i, (i + by) % length) for i in range(length)])


class Window:
    def __init__(self, start, npc, own, nloc):
        end = start + npc
        self.lo = start // 16 * 16
        self.hi = min(up_to(min(end, own), 16), own)
        self.touches = end > own
        self.low = up_to(max(0, end - nloc), 16)
        self.rows = self.hi - self.lo + self.low


class Geometry:
    def __init__(self, own, share, cells, npc):
        self.own, self.share, self.cells, self.npc = own, share, cells, npc
        nloc = own + share
        stride = nloc // cells
        self.sp = up_to(share, 16)
        self.npl = up_to(npc, LANES)
        self.windows = [Window(c * stride, npc, own, nloc) for c in range(cells)]
        self.touching = [c for c in range(cells) if self.windows[c].touches]
        self.dn_lo = min(self.windows[c].lo for c in self.touching)
        self.low = max(w.low for w in self.windows)
        self.dn_rows = own - self.dn_lo + self.low
        self.table_rows = up_to(cells, SUBLANES)
        self.table_lanes = up_to(npc, LANES)
        self.table_tiles = self.table_lanes // LANES


def dot(a, b):
    return lax.dot_general(a, b, (((1,), (0,)), ((), ())), preferred_element_type=F32)


def dot_t(a, b):
    return lax.dot_general(a, b, (((1,), (1,)), ((), ())), preferred_element_type=F32)


def vmem_call(kernel, out_shape, scratch=(), in_specs=None, out_specs=None, cost=None):
    kwargs = {}
    if in_specs is not None:
        kwargs["in_specs"] = in_specs
    if out_specs is not None:
        kwargs["out_specs"] = out_specs
    return pl.pallas_call(
        kernel,
        out_shape=out_shape,
        scratch_shapes=list(scratch),
        cost_estimate=cost,
        compiler_params=pltpu.CompilerParams(vmem_limit_bytes=12 * 1024 * 1024),
        **kwargs,
    )


def in_hbm(*arrays):
    return [pltpu.with_memory_space_constraint(a, pltpu.HBM) for a in arrays]


def sds(shape, dtype):
    return jax.ShapeDtypeStruct(shape, dtype)


def one_hot_rows(count, first, nodes):
    ids = lax.broadcasted_iota(I32, (count, nodes.shape[1]), 0) + first
    return jnp.where(ids == nodes, 1.0, 0.0).astype(BF)


def place_table(geo, nodes_ref, face_ref, table, faces):
    table[...] = jnp.full(table.shape, -1, I32)
    table[0 : geo.cells, 0 : geo.npc] = nodes_ref[...]
    faces[...] = jnp.zeros(faces.shape, I32)
    faces[0:1, 0 : geo.share] = face_ref[...]
    for t in range(geo.table_tiles):
        lanes = slice(t * LANES, (t + 1) * LANES)
        nodes = table[:, lanes]
        beyond = nodes - geo.own
        at = jnp.bitwise_and(beyond, LANES - 1)
        which = jnp.right_shift(beyond, 7)
        for f in range(faces.shape[1] // LANES):
            row = jnp.broadcast_to(faces[0:1, f * LANES : (f + 1) * LANES], nodes.shape)
            nodes = jnp.where(which == f, lanes_of(row, at) + geo.own, nodes)
        table[:, lanes] = nodes


def place_matrix(geo, matrix_ref, matrix_pad):
    matrix_pad[...] = jnp.zeros(matrix_pad.shape, F32)
    matrix_pad[0 : geo.npc, 0 : geo.npc] = matrix_ref[...].astype(F32)
    return matrix_pad[...].astype(BF)


def table_scratch(geo):
    return pltpu.VMEM((geo.table_rows, geo.table_lanes), I32)


def matrix_scratch(geo):
    return pltpu.VMEM((geo.npl, geo.npl), F32)


def nodes_of(geo, table, c):
    return table[c : c + 1, 0 : geo.npl]


def owned_picks(geo, c, nodes):
    w = geo.windows[c]
    picks = one_hot_rows(w.hi - w.lo, w.lo, nodes)
    if w.low:
        picks = jnp.concatenate([picks, one_hot_rows(w.low, 0, nodes)], axis=0)
    return picks


def upper_picks(geo, nodes):
    return one_hot_rows(geo.sp, geo.own, nodes)


def own_matrices_kernel(geo, *refs):
    table, matrix_ref, pot_ref = refs[:3]
    outs, matrix_pad = refs[3:-1], refs[-1]
    matrix = place_matrix(geo, matrix_ref, matrix_pad)
    for c in range(geo.cells):
        nodes = nodes_of(geo, table, c)
        own = owned_picks(geo, c, nodes)
        left = dot(own, matrix).astype(BF)
        outs[c][...] = dot_t(left, own).astype(BF)
        if c in geo.touching:
            at = geo.cells + geo.touching.index(c)
            upper = upper_picks(geo, nodes)
            outs[at][...] = dot_t(left, upper).astype(BF)
            left = dot(upper, matrix).astype(BF)
            outs[at + len(geo.touching)][...] = dot_t(left, own).astype(BF)
    column = outs[-1]
    for r in range(geo.own // LANES):
        row = jnp.broadcast_to(pot_ref[r : r + 1, :], (LANES, LANES))
        column[r * LANES : (r + 1) * LANES, :] = row.T


def own_matrices(geo, table, cell_matrix, lines):
    shapes = [sds((w.rows, w.rows), BF) for w in geo.windows]
    shapes += [sds((geo.windows[c].rows, geo.sp), BF) for c in geo.touching]
    shapes += [sds((geo.sp, geo.windows[c].rows), BF) for c in geo.touching]
    shapes += [sds((geo.own, LANES), F32)]
    outs = vmem_call(
        functools.partial(own_matrices_kernel, geo),
        shapes,
        [matrix_scratch(geo)],
        cost=cost_of(2.0),
    )(table, cell_matrix, lines)
    n, m = geo.cells, geo.cells + len(geo.touching)
    return outs[:n], outs[n:m], outs[m:-1], outs[-1]


def build_behind(geo, sent_ref, matrix_ref, table, matrix_pad, behinds, uppers):
    for t in range(geo.table_tiles):
        at = geo.dn_rows + 2 * t * geo.table_rows
        digits = sent_ref[at : at + 2 * geo.table_rows, :].astype(F32)
        value = digits[: geo.table_rows] * LANES + digits[geo.table_rows :] - 1.0
        table[:, t * LANES : (t + 1) * LANES] = value.astype(I32)
    matrix = place_matrix(geo, matrix_ref, matrix_pad)
    for at, c in enumerate(geo.touching):
        nodes = nodes_of(geo, table, c)
        upper = upper_picks(geo, nodes)
        left = dot(upper, matrix).astype(BF)
        behinds[at][...] = dot_t(left, owned_picks(geo, c, nodes)).astype(BF)
        uppers[at][...] = dot_t(left, upper).astype(BF)


def cost_of(us):
    return pl.CostEstimate(flops=0, bytes_accessed=int(us * 3.0e6), transcendentals=0)


def write_rows(geo, y_ref, dn_ref, up_ref):
    top = geo.own - geo.dn_lo
    dn_ref[0:top, :] = y_ref[geo.dn_lo : geo.own, :].astype(BF)
    dn_ref[top : top + geo.low, :] = y_ref[0 : geo.low, :].astype(BF)
    up_ref[...] = y_ref[0 : geo.sp, :].astype(BF)


def window_rows(geo, c, y_ref):
    w = geo.windows[c]
    rows = y_ref[w.lo : w.hi, :].astype(BF)
    if w.low:
        rows = jnp.concatenate([rows, y_ref[0 : w.low, :].astype(BF)], axis=0)
    return rows


def is_even():
    return jnp.bitwise_and(lax.axis_index("domain"), 1) == 0


def write_sends(geo, y_ref, reaches, near_ref, far_ref):
    total = None
    for at, c in enumerate(geo.touching):
        term = dot(reaches[at][...], window_rows(geo, c, y_ref))
        total = term if total is None else total + term
    rows = y_ref[0 : geo.sp, :]
    even = is_even()
    near_ref[...] = jnp.where(even, total, rows).astype(BF)
    far_ref[...] = jnp.where(even, rows, total).astype(BF)


def send_shapes(geo, columns):
    return [sds((geo.sp, columns), BF), sds((geo.sp, columns), BF)]


def fetch(pairs, sems):
    copies = [pltpu.make_async_copy(src, dst, sems.at[i]) for i, (src, dst) in enumerate(pairs)]
    for copy in copies:
        copy.start()
    return copies


def pack_kernel(geo, extra, y_hbm, nodes_hbm, face_hbm, *refs):
    sources, refs = refs[:extra], refs[extra:]
    dn_ref, up_ref, y, table = refs[:4]
    kept, (nodes, face, faces, sems) = refs[4 : 4 + extra], refs[4 + extra :]
    cuts = sorted({0, max(geo.sp, geo.low), geo.dn_lo, geo.own})
    spans = list(zip(cuts[:-1], cuts[1:]))
    pairs = [(nodes_hbm, nodes), (face_hbm, face)]
    pairs += [(y_hbm.at[pl.ds(a, b - a)], y.at[pl.ds(a, b - a)]) for a, b in spans]
    pairs += list(zip(sources, kept))
    copies = fetch(pairs, sems)
    copies[0].wait()
    copies[1].wait()
    place_table(geo, nodes, face, table, faces)
    for t in range(geo.table_tiles):
        at = geo.dn_rows + 2 * t * geo.table_rows
        value = table[:, t * LANES : (t + 1) * LANES] + 1
        high = jnp.right_shift(value, 7).astype(F32)
        low = jnp.bitwise_and(value, LANES - 1).astype(F32)
        digits = jnp.concatenate([high, low], axis=0).astype(BF)
        dn_ref[at : at + 2 * geo.table_rows, :] = digits
    for copy in copies[2:]:
        copy.wait()
    write_rows(geo, y, dn_ref, up_ref)


def pack(geo, y, cell_nodes, face_order, *others):
    up = sds((geo.sp, y.shape[1]), BF)
    rows = geo.dn_rows + 2 * geo.table_rows * geo.table_tiles
    dn, up, y, table, *others = vmem_call(
        functools.partial(pack_kernel, geo, len(others)),
        [
            sds((rows, y.shape[1]), BF),
            up,
            sds(y.shape, F32),
            sds((geo.table_rows, geo.table_lanes), I32),
            *[sds(a.shape, a.dtype) for a in others],
        ],
        [
            pltpu.VMEM(cell_nodes.shape, I32),
            pltpu.VMEM(face_order.shape, I32),
            pltpu.VMEM((1, up_to(geo.share, LANES)), I32),
            pltpu.SemaphoreType.DMA((5 + len(others),)),
        ],
        in_specs=[pl.BlockSpec(memory_space=pltpu.HBM)] * (3 + len(others)),
        cost=cost_of(1.0),
    )(*in_hbm(y, cell_nodes, face_order, *others))
    return (dn, up), y, table, others


def owned_part_kernel(geo, scale, has_prev, has_field, has_upper, *refs):
    refs = list(refs)
    base_ref = refs.pop()
    y_ref = refs.pop(0)
    prev_ref = refs.pop(0) if has_prev else None
    pot_ref = refs.pop(0)
    field_ref = refs.pop(0) if has_field else None
    mats = [refs.pop(0) for _ in range(geo.cells)]
    y = y_ref[...]
    factor = pot_ref[...]
    if has_field:
        factor = factor + field_ref[...]
    value = ((factor - filter_center) * scale) * y
    if has_prev:
        value = value - prev_ref[...]
    base_ref[...] = value
    x = y.astype(BF)
    for c in range(geo.cells):
        w = geo.windows[c]
        own = w.hi - w.lo
        rows = x[w.lo : w.hi, :]
        if w.low:
            rows = jnp.concatenate([rows, x[0 : w.low, :]], axis=0)
        product = dot(mats[c][...], rows) * scale
        base_ref[w.lo : w.hi, :] += product[:own]
        if w.low:
            base_ref[0 : w.low, :] += product[own:]
    if has_upper:
        for upper in refs:
            base_ref[0 : geo.sp, :] += dot(upper[...], x[0 : geo.sp, :]) * scale


def owned_part(geo, scale, y, prev, pot, field, mats, uppers):
    args = [y] + ([prev] if prev is not None else []) + [pot]
    args += [field] if field is not None else []
    args += list(mats) + list(uppers)
    return vmem_call(
        functools.partial(
            owned_part_kernel, geo, scale, prev is not None, field is not None, bool(uppers)
        ),
        sds(y.shape, F32),
        cost=cost_of(2.0),
    )(*args)


def add_upper(geo, scale, y_ref, h_up, crosses):
    for at, c in enumerate(geo.touching):
        w = geo.windows[c]
        own = w.hi - w.lo
        product = dot(crosses[at][...], h_up) * scale
        y_ref[w.lo : w.hi, :] += product[:own]
        if w.low:
            y_ref[0 : w.low, :] += product[own:]


def add_rows(geo, scale, y_ref, h_dn, behinds, uppers, own_up):
    total = None
    for at, c in enumerate(geo.touching):
        w = geo.windows[c]
        first = w.lo - geo.dn_lo
        term = dot(behinds[at][...], h_dn[first : first + w.rows, :])
        term = term + dot(uppers[at][...], own_up)
        total = term if total is None else total + term
    y_ref[0 : geo.sp, :] += total * scale


def add_halo(geo, scale, y_ref, near_ref, far_ref, crosses):
    near, far = near_ref[...].astype(F32), far_ref[...].astype(F32)
    even = is_even()
    y_ref[0 : geo.sp, :] += jnp.where(even, far, near) * scale
    add_upper(geo, scale, y_ref, jnp.where(even, near, far).astype(BF), crosses)


def write_density(y_ref, occ_ref, table_ref, part_rows, dens_ref):
    parts = dens_ref.shape[0]
    own = y_ref.shape[0]
    y = y_ref[...]
    terms = y * y * occ_ref[...]
    high = terms.astype(BF)
    low = (terms - high.astype(F32)).astype(BF)
    ones = jnp.ones((SUBLANES, terms.shape[1]), BF)
    summed = dot_t(ones, high) + dot_t(ones, low)
    dens_ref[:, 0, 0:own] = jnp.broadcast_to(summed[0:1, :], (parts, own))
    band = lax.axis_index("band")
    for r in range(part_rows):
        row = table_ref[band, r : r + 1, :]
        dens_ref[:, 0, own + r * LANES : own + (r + 1) * LANES] = jnp.broadcast_to(row, (parts, LANES))


def first_finish_kernel(geo, scale, *refs):
    n = len(geo.touching)
    base_ref, up_ref, dn_ref, own_up_ref, matrix_ref = refs[:5]
    crosses, reaches, refs = refs[5 : 5 + n], refs[5 + n : 5 + 2 * n], refs[5 + 2 * n :]
    y_ref, near_out, far_out = refs[:3]
    uppers, behinds = refs[3 : 3 + n], refs[3 + n : 3 + 2 * n]
    build_behind(geo, dn_ref, matrix_ref, *refs[-2:], behinds, uppers)
    y_ref[...] = base_ref[...]
    add_upper(geo, scale, y_ref, up_ref[...], crosses)
    add_rows(geo, scale, y_ref, dn_ref[...], behinds, uppers, own_up_ref[...])
    write_sends(geo, y_ref, reaches, near_out, far_out)


def first_finish(geo, scale, base, halo, own_up, matrix, crosses, reaches):
    shapes = [sds(base.shape, F32), *send_shapes(geo, base.shape[1])]
    shapes += [sds((geo.sp, geo.sp), BF) for _ in geo.touching]
    y, near, far, *uppers = vmem_call(
        functools.partial(first_finish_kernel, geo, scale),
        shapes,
        [
            *[pltpu.VMEM((geo.sp, geo.windows[c].rows), BF) for c in geo.touching],
            table_scratch(geo),
            matrix_scratch(geo),
        ],
        cost=cost_of(1.5),
    )(base, halo[0], halo[1], own_up, matrix, *crosses, *reaches)
    return y, (near, far), uppers


def finish_kernel(geo, scale, mode, part_rows, *refs):
    refs = list(refs)
    n = len(geo.touching)
    base_ref, near_ref, far_ref = refs[:3]
    refs = refs[3:]
    crosses, refs = refs[:n], refs[n:]
    halo = (near_ref, far_ref, crosses)
    if mode == "last":
        finish_last(geo, scale, base_ref, halo, *refs)
        return
    reaches, refs = refs[:n], refs[n:]
    if mode == "density":
        occ_ref, table_ref = refs.pop(0), refs.pop(0)
    if mode == "field":
        column_ref, before_ref = refs.pop(0), refs.pop(0)
    y_ref = refs.pop(0)
    if mode == "field":
        y_ref[...] = base_ref[...] + (column_ref[...] * scale) * before_ref[...]
    else:
        y_ref[...] = base_ref[...]
    add_halo(geo, scale, y_ref, *halo)
    if mode == "density":
        _, _, out_hbm, dens, sem = refs
        write_density(y_ref, occ_ref, table_ref, part_rows, dens)
        copy = pltpu.make_async_copy(dens, out_hbm, sem)
        copy.start()
    write_sends(geo, y_ref, reaches, refs[0], refs[1])
    if mode == "density":
        copy.wait()


def finish_last(geo, scale, base_ref, halo, *refs):
    extras = (len(refs) - 3) // 2
    sources, out_hbm, targets = refs[:extras], refs[extras], refs[extras + 1 : -2]
    y_ref, sems = refs[-2:]
    top = max(geo.sp, geo.low)
    inner = pl.ds(top, geo.dn_lo - top)
    copies = fetch([(base_ref.at[inner], out_hbm.at[inner]), *zip(sources, targets)], sems)
    edges = [(0, top), (geo.dn_lo, geo.own)]
    for a, b in edges:
        y_ref[a:b, :] = base_ref[a:b, :]
    add_halo(geo, scale, y_ref, *halo)
    for i, (a, b) in enumerate(edges):
        edge = pl.ds(a, b - a)
        copy = pltpu.make_async_copy(y_ref.at[edge], out_hbm.at[edge], sems.at[1 + extras + i])
        copy.start()
        copies.append(copy)
    for copy in copies:
        copy.wait()


def finish(geo, scale, base, halo, crosses, reaches=(), density=None, field=None, last=None):
    columns = base.shape[1]
    args = [base, halo[0], halo[1], *crosses, *reaches]
    mode, part_rows = "plain", 0
    shapes = [sds(base.shape, F32)]
    scratch = []
    vmem, hbm = pl.BlockSpec(memory_space=pltpu.VMEM), pl.BlockSpec(memory_space=pltpu.HBM)
    out_specs = [vmem, vmem, vmem]
    if last is not None:
        mode = "last"
        args += last
        shapes += [sds(a.shape, a.dtype) for a in last]
        out_specs = [hbm] * len(shapes)
        scratch = [pltpu.VMEM(base.shape, F32), pltpu.SemaphoreType.DMA((3 + len(last),))]
    else:
        shapes += send_shapes(geo, columns)
    if field is not None:
        mode = "field"
        args += list(field)
    if density is not None:
        mode = "density"
        fg, weights, table = density
        part_rows = fg.part_rows
        args += [weights, table]
        spread = (fg.bands * fg.domains, 1, fg.width)
        shapes.append(sds(spread, F32))
        out_specs.append(hbm)
        scratch = [pltpu.VMEM(spread, F32), pltpu.SemaphoreType.DMA(())]
    return vmem_call(
        functools.partial(finish_kernel, geo, scale, mode, part_rows),
        shapes,
        scratch,
        out_specs=out_specs,
        cost=cost_of(1.0),
    )(*args)


class FieldGeometry:
    def __init__(self, bands, domains, own, share, cells, npc):
        self.bands, self.domains, self.own, self.share = bands, domains, own, share
        self.cells, self.npc = cells, npc
        self.block = own // domains
        self.rows = up_to(npc, LANES) // LANES
        self.lines = own // LANES
        self.tiles = self.lines + 1
        nloc = own + share
        self.touched = []
        for c in range(cells):
            nodes = [(c * (nloc // cells) + k) % nloc for k in range(npc)]
            self.touched.append(sorted({node // LANES for node in nodes}))
        self.at_inverse = cells * self.rows
        self.at_face = self.at_inverse + cells * self.tiles
        self.at_screen = up_to(self.at_face + 2, 2) // 2
        self.part_rows = -(-(self.at_screen + self.lines) // bands)
        self.table_rows = up_to(self.part_rows * bands, SUBLANES)
        self.width = own + self.part_rows * LANES
        self.size = self.rows * LANES
        self.at_owner_lane = LANES - domains
        self.fits = (
            domains == SUBLANES
            and own % (domains * SUBLANES) == 0
            and own % LANES == 0
            and self.block <= LANES
            and share <= self.at_owner_lane
            and max(npc, nloc) < CODE_BASE - 1
        )


CODE_BASE = 2048
CODE_BITS = 11


def pieces(length, blocks):
    found = []
    for j in range(blocks):
        done = 0
        while done < length:
            at = j * length + done
            count = min(length - done, LANES - at % LANES)
            found.append((at // LANES, at % LANES, j, done, count))
            done += count
    return found


def column_of(row):
    return jnp.broadcast_to(row, (LANES, LANES)).T


def inverse_row(columns, first):
    sub = lax.broadcasted_iota(I32, (LANES, LANES), 0)
    target = (lax.broadcasted_iota(I32, (LANES, LANES), 1) + first).astype(F32)
    found = jnp.zeros((LANES, LANES), F32)
    for r, column in enumerate(columns):
        found = jnp.where(column == target, (sub + (r * LANES + 1)).astype(F32), found)
    return jnp.sum(found, axis=0, keepdims=True) - 1.0


def field_tables_kernel(fg, *refs):
    nodes_ref, face_ref, owner_ref, screen_ref = refs[:4]
    table_ref, pad, one, spare, packed = refs[5:]
    one[...] = jnp.full(one.shape, -1.0, F32)
    spare[...] = jnp.full(spare.shape, -1.0, F32)
    pad[...] = jnp.full(pad.shape, -1, I32)
    pad[0 : fg.cells, 0 : fg.npc] = nodes_ref[...]
    for c in range(fg.cells):
        columns = []
        for r in range(fg.rows):
            code = pad[c : c + 1, r * LANES : (r + 1) * LANES].astype(F32)
            one[c * fg.rows + r : c * fg.rows + r + 1, :] = code
            columns.append(column_of(code))
        for t in fg.touched[c]:
            at = fg.at_inverse + c * fg.tiles + t
            one[at : at + 1, :] = inverse_row(columns, t * LANES)
    lane = fg.at_owner_lane
    spare[0:1, 0 : fg.share] = face_ref[...].astype(F32)
    spare[1:2, 0 : fg.domains] = owner_ref[...].astype(F32)
    at = fg.at_face
    one[at : at + 1, :] = spare[0:1, :]
    one[at : at + 1, lane:LANES] = owner_ref[...].astype(F32)
    back = inverse_row([column_of(spare[0:1, :])], 0)
    home = inverse_row([column_of(spare[1:2, :])], -lane)
    lanes = lax.broadcasted_iota(I32, (1, LANES), 1)
    one[at + 1 : at + 2, :] = jnp.where(lanes < lane, back, home)
    packed[...] = jnp.zeros(packed.shape, F32)
    half = fg.at_screen
    packed[0:half, :] = (one[0:half, :] + 1.0) + (one[half : 2 * half, :] + 1.0) * CODE_BASE
    packed[half : half + fg.lines, :] = screen_ref[...]
    for b in range(fg.bands):
        table_ref[b, 0 : fg.part_rows, :] = packed[b * fg.part_rows : (b + 1) * fg.part_rows, :]


def field_tables(fg, pois_nodes, pois_face, block_owner, lines, after):
    specs = [pl.BlockSpec(memory_space=pltpu.VMEM)] * 4 + [pl.BlockSpec(memory_space=pl.ANY)]
    return vmem_call(
        functools.partial(field_tables_kernel, fg),
        sds((fg.bands, up_to(fg.part_rows, SUBLANES), LANES), F32),
        [
            pltpu.VMEM((up_to(fg.cells, SUBLANES), fg.size), I32),
            pltpu.VMEM((up_to(2 * fg.at_screen, SUBLANES), LANES), F32),
            pltpu.VMEM((SUBLANES, LANES), F32),
            pltpu.VMEM((fg.table_rows, LANES), F32),
        ],
        in_specs=specs,
        cost=cost_of(1.0),
    )(pois_nodes, pois_face, block_owner, lines, after)


def lanes_of(values, index):
    return jnp.take_along_axis(values, index, axis=1, mode="promise_in_bounds")


def decode(fg, got_ref, codes):
    domains, half, own = fg.domains, fg.at_screen, fg.own

    def tile(at):
        band, row = at // fg.part_rows, at % fg.part_rows
        first = own + row * LANES
        return got_ref[band * domains : (band + 1) * domains, 0, first : first + LANES]

    for at in range(half):
        both = tile(at).astype(I32)
        codes[at] = jnp.bitwise_and(both, CODE_BASE - 1) - 1
        codes[half + at] = jnp.right_shift(both, CODE_BITS) - 1
    screens = [tile(half + g) for g in range(fg.lines)]
    lane = lax.broadcasted_iota(I32, (domains, LANES), 1)
    first, last = fg.at_owner_lane, LANES
    owners = codes[fg.at_face].astype(F32).T[first:last, :]
    inverse = codes[fg.at_face + 1].astype(F32).T[first:last, :]
    back = jnp.where(lane < fg.share, codes[fg.at_face + 1], -1)
    codes[fg.at_face + 1] = pltpu.roll(back, 1, 0)
    places = []
    for q in range(domains):
        block = jnp.broadcast_to(inverse[:, q : q + 1], (domains, LANES)).astype(I32)
        places.append(block * fg.block + lane)
    here = lax.axis_index("domain")
    narrow = lax.broadcasted_iota(I32, (domains, domains), 1)
    mine = jnp.sum(jnp.where(narrow == here, owners, 0.0), axis=1, keepdims=True)
    return places, jnp.broadcast_to(mine, (domains, LANES)).astype(I32), screens


def rows_of(values, index):
    return jnp.take_along_axis(values, index, axis=0, mode="promise_in_bounds")


def lookup(sources, code):
    lane = jnp.bitwise_and(code, LANES - 1)
    which = jnp.right_shift(code, 7)
    total = jnp.zeros(code.shape, F32)
    for b, values in sources:
        total = jnp.where(which == b, lanes_of(values, lane), total)
    return total


def field_source(fg, got_ref, places):
    domains = fg.domains
    density = []
    for g in range(fg.lines):
        at = slice(g * LANES, (g + 1) * LANES)
        total = got_ref[0:domains, 0, at]
        for b in range(1, fg.bands):
            total = total + got_ref[b * domains : (b + 1) * domains, 0, at]
        density.append(total)
    lane = lax.broadcasted_iota(I32, (domains, LANES), 1)
    source = [None] * fg.lines
    for q in range(domains):
        spread = [jnp.broadcast_to(d[q : q + 1, :], (domains, LANES)) for d in density]
        block = lookup(list(enumerate(spread)), places[q])
        for row, start, j, offset, count in pieces(fg.block, domains):
            if j == q:
                moved = pltpu.roll(block, (start - offset) % LANES, 1)
                inside = (lane >= start) & (lane < start + count)
                before = 0.0 if source[row] is None else source[row]
                source[row] = jnp.where(inside, moved, before)
    return source


def field_solve(fg, source, codes, screen, matrix_ref, high_ref, low_ref, rows, copies):
    domains, cells = fg.domains, fg.cells

    def operator(field):
        ahead = pltpu.roll(field[0], domains - 1, 0)
        local = list(field) + [lookup([(0, ahead)], codes[fg.at_face])]
        for r in range(fg.rows):
            for c in range(cells):
                sources = [(t, local[t]) for t in fg.touched[c]]
                rows[c * domains : (c + 1) * domains, r * LANES : (r + 1) * LANES] = lookup(sources, codes[c * fg.rows + r])
            if copies:
                copies.pop(0).wait()
                span = slice(r * LANES, min((r + 1) * LANES, fg.npc))
                full = matrix_ref[span, :]
                top = full.astype(BF)
                high_ref[span, :] = top
                low_ref[span, :] = (full - top.astype(F32)).astype(BF)
        picked = rows[:, 0 : fg.npc]
        high = picked.astype(BF)
        low = (picked - high.astype(F32)).astype(BF)
        both = dot(jnp.concatenate([high, low], axis=0), high_ref[...])
        half_rows = cells * domains
        rows[:, 0 : fg.npc] = both[:half_rows] + (both[half_rows:] + dot(high, low_ref[...]))
        out = [None] * fg.tiles
        for c in range(cells):
            sources = [
                (r, rows[c * domains : (c + 1) * domains, r * LANES : (r + 1) * LANES])
                for r in range(fg.rows)
            ]
            for t in fg.touched[c]:
                term = lookup(sources, codes[fg.at_inverse + c * fg.tiles + t])
                out[t] = term if out[t] is None else out[t] + term
        arriving = pltpu.roll(out[fg.lines], 1, 0)
        out[0] = out[0] + lookup([(0, arriving)], codes[fg.at_face + 1])
        return [screen[g] * field[g] + out[g] for g in range(fg.lines)]

    step_one = [s * (1.0 / solve_center) for s in source]
    applied = operator(step_one)
    residual = [s - a for s, a in zip(source, applied)]
    a1, b1 = weight_one * weight_zero, 2.0 * weight_one / solve_half
    step_two = [a1 * e + b1 * r for e, r in zip(step_one, residual)]
    applied = operator(step_two)
    residual = [r - a for r, a in zip(residual, applied)]
    a2, b2 = weight_two * weight_one, 2.0 * weight_two / solve_half
    step_three = [a2 * e + b2 * r for e, r in zip(step_two, residual)]
    return [(x + y) + z for x, y, z in zip(step_one, step_two, step_three)]


def field_kernel(fg, got_ref, matrix_hbm, column_ref, hartree_ref, codes, rows, mine, matrix_ref, high_ref, low_ref, sems):
    spans = [pl.ds(r * LANES, min(LANES, fg.npc - r * LANES)) for r in range(fg.rows)]
    copies = fetch([(matrix_hbm.at[span], matrix_ref.at[span]) for span in spans], sems)
    places, owner, screens = decode(fg, got_ref, codes)
    source = field_source(fg, got_ref, places)
    solved = field_solve(fg, source, codes, screens, matrix_ref, high_ref, low_ref, rows, copies)
    lane = lax.broadcasted_iota(I32, (fg.domains, LANES), 1)
    block = lookup(list(enumerate(solved)), lane + lax.axis_index("domain") * fg.block)
    mine[...] = rows_of(block, owner)
    for j in range(fg.domains):
        column = column_of(mine[j : j + 1, :])
        column_ref[j * fg.block : (j + 1) * fg.block, :] = column[0 : fg.block, :]
    for row, start, j, offset, count in pieces(fg.block, fg.domains):
        hartree_ref[row : row + 1, start : start + count] = mine[j : j + 1, offset : offset + count]


def field_step(fg, got, matrix):
    tile = (fg.domains, LANES)
    return vmem_call(
        functools.partial(field_kernel, fg),
        [sds((fg.own, LANES), F32), sds((fg.lines, LANES), F32)],
        [
            pltpu.VMEM((2 * fg.at_screen, *tile), I32),
            pltpu.VMEM((fg.cells * fg.domains, fg.size), F32),
            pltpu.VMEM(tile, F32),
            pltpu.VMEM(matrix.shape, F32),
            pltpu.VMEM(matrix.shape, BF),
            pltpu.VMEM(matrix.shape, BF),
            pltpu.SemaphoreType.DMA((fg.rows,)),
        ],
        in_specs=[pl.BlockSpec(memory_space=pltpu.VMEM), pl.BlockSpec(memory_space=pltpu.HBM)],
        cost=cost_of(4.0),
    )(got, *in_hbm(matrix))


def assembled(owned_rows, face_row, terms):
    owned_count = owned_rows.shape[0]
    shared = face_row.shape[0]
    coming = jnp.take(from_behind(owned_rows[:shared], "domain", -1), face_row, axis=0)
    partial_value = terms(jnp.concatenate([owned_rows, coming], axis=0))
    upper_rows = partial_value[owned_count:]
    ordered = jnp.zeros_like(upper_rows).at[face_row].set(upper_rows)
    arrived = from_behind(ordered, "domain", 1)
    return partial_value[:owned_count].at[:shared].add(arrived)


def field_terms(local_rows, pois_matrix, node_ids):
    cell_vals = jnp.take(local_rows, node_ids, axis=0)
    product = jnp.einsum(
        "pq,cq->cp",
        pois_matrix,
        cell_vals,
        precision=lax.Precision.HIGHEST,
        preferred_element_type=F32,
    )
    return jnp.zeros(local_rows.shape, F32).at[node_ids.reshape(-1)].add(product.reshape(-1))


def reshuffle(blocks):
    return lax.all_to_all(blocks, "domain", split_axis=0, concat_axis=0, tiled=True)


def distributed_field(y, occupation, owner_row, pois_matrix, pois_nodes, field_face, screening):
    owned_count = y.shape[0]
    domains = lax.axis_size("domain")
    block_len = owned_count // domains
    partial_value = jnp.dot(
        y * y, occupation, precision=lax.Precision.HIGHEST, preferred_element_type=F32
    )
    summed = lax.psum(partial_value, "band")
    arranged = (
        jnp.zeros((domains, block_len), F32)
        .at[owner_row]
        .set(summed.reshape(domains, block_len))
    )
    source = reshuffle(arranged).reshape(owned_count)

    def field_operator(vector):
        return (
            assembled(
                vector, field_face, lambda local: field_terms(local, pois_matrix, pois_nodes)
            )
            + screening * vector
        )

    step_one = source / solve_center
    residual = source - field_operator(step_one)
    step_two = weight_one * weight_zero * step_one + 2.0 * weight_one / solve_half * residual
    residual = residual - field_operator(step_two)
    step_three = weight_two * weight_one * step_two + 2.0 * weight_two / solve_half * residual
    solved = step_one + step_two + step_three
    returned = reshuffle(solved.reshape(domains, block_len))
    return jnp.take(returned, owner_row, axis=0).reshape(owned_count)


def exchange(sends):
    dn, up = sends
    h_dn = from_behind(dn, "domain", 1)
    h_up = from_behind(up, "domain", -1)
    return h_up, h_dn


def on_device(
    orbitals,
    potential,
    occupation,
    cell_matrix,
    cell_nodes,
    face_order,
    pois_matrix,
    pois_nodes,
    pois_face,
    screening,
    block_owner,
):
    domains = lax.axis_size("domain")
    bands = lax.axis_size("band")
    own, columns = orbitals.shape
    geo = Geometry(own, face_order.shape[1], cell_nodes.shape[0], cell_nodes.shape[1])
    fg = FieldGeometry(bands, domains, own, pois_face.shape[1], pois_nodes.shape[0], pois_nodes.shape[1])
    first, later = 1.0 / filter_half, 2.0 / filter_half

    others = [cell_matrix, potential.reshape(own // LANES, LANES)]
    if fg.fits:
        others += [pois_nodes, pois_face, block_owner, screening.reshape(own // LANES, LANES)]
        others.append(occupation.reshape(1, columns))
    sends, y0, nodes, (matrix, lines, *others) = pack(geo, orbitals, cell_nodes, face_order, *others)
    halo = exchange(sends)
    mats, crosses, reaches, pot = own_matrices(geo, nodes, matrix, lines)
    base = owned_part(geo, first, y0, None, pot, None, mats, ())
    y1, sends1, uppers = first_finish(
        geo, first, base, halo, sends[1], matrix, crosses, reaches
    )

    halo = swap(sends1)
    base = owned_part(geo, later, y1, y0, pot, None, mats, uppers)
    if fg.fits:
        *others, weights = others
        table = field_tables(fg, *others, base)
    y2, *sends2 = finish(geo, later, base, halo, crosses, reaches)

    halo = swap(sends2)
    base = owned_part(geo, later, y2, y1, pot, None, mats, uppers)
    if fg.fits:
        y3, dn, up, spread = finish(
            geo, later, base, halo, crosses, reaches, density=(fg, weights, table)
        )
        dens = lax.all_to_all(spread, ("band", "domain"), 0, 0, tiled=True)
        halo = swap((dn, up))
        base = owned_part(geo, first, y3, None, pot, None, mats, uppers)
        column, packed = field_step(fg, dens, pois_matrix)
        z1, *sends4 = finish(geo, first, base, halo, crosses, reaches, field=(column, y3))
    else:
        y3, *sends3 = finish(geo, later, base, halo, crosses, reaches)
        halo = swap(sends3)
        hartree = distributed_field(
            y3, occupation, block_owner[0], pois_matrix, pois_nodes, pois_face[0], screening
        )
        column = jnp.broadcast_to(hartree[:, None], (own, LANES))
        base = owned_part(geo, first, y3, None, pot, column, mats, uppers)
        z1, *sends4 = finish(geo, first, base, halo, crosses, reaches)

    halo = swap(sends4)
    base = owned_part(geo, later, z1, y3, pot, column, mats, uppers)
    last = [packed] if fg.fits else []
    filtered, *rest = finish(geo, later, base, halo, crosses, last=last)
    if fg.fits:
        hartree = rest[0].reshape(own)
    return filtered, hartree


def swap(sends):
    length = lax.axis_size("domain")
    near, far = sends
    turns = [(i, (i + 1) % length if i % 2 else (i - 1) % length) for i in range(length)]
    far = lax.ppermute(far, "domain", turns)
    near = lax.ppermute(near, "domain", [(i, i ^ 1) for i in range(length)])
    return near, far


def solution(mesh):
    return jax.shard_map(
        on_device,
        mesh=mesh,
        in_specs=(
            P("domain", "band"),
            P("domain"),
            P("band"),
            P(),
            P("domain", None),
            P("domain", None),
            P(),
            P("domain", None),
            P("domain", None),
            P("domain"),
            P("domain", None),
        ),
        out_specs=(P("domain", "band"), P("domain")),
        check_vma=False,
    )
```

profile of v0, /device:TPU:0, one launch (start us, length us, event | category | flops | bytes accessed | tf_op | source)
XLA Modules:
  0.0 48.4 jit_solution(4101265996804552227)
XLA Ops:
  0.6 1.3 %shard_map.122 = (bf16[464,128]{1,0:T(8,128)(2,1)S(1)}, bf16[176,128]{1,0:T(8,128)(2,1)S(1)}, f32[768,128]{1,0:T(8,128)S(1)}, s32[8,384]{1,0:T(8,128)S(1)}, bf16...) custom-call(f32[768,128]{1,0:T(8,128)} %y_hbm.1, ...), custom_call_target="tpu_custom_call" | custom-call | bytes 3000000 | tf_op jit(solution)/shard_map/pallas_call | solution.py:270
  1.9 0.5 %collective-permute-start.1 = (bf16[464,128]{1,0:T(8,128)(2,1)S(1)}, bf16[464,128]{1,0:T(8,128)(2,1)S(1)}, u32[]{:S(2)}, u32[]{:S(2)}) collective-permute-start(bf16[464,128]{1,0:T(8,128)(2,1)S(1)} %get-tuple-element.51), channel_id=1, source_target_pairs={{0,1},{1,2},{2,3},{3,4},{4,5},{5,6},{6,7},{7,0},{8,9},{9,10},{10,1... | collective-permute-start | bytes 356360 | tf_op jit(solution)/shard_map/ppermute | solution.py:32
  2.5 4.1 %collective-permute-start = (bf16[176,128]{1,0:T(8,128)(2,1)S(1)}, bf16[176,128]{1,0:T(8,128)(2,1)S(1)}, u32[]{:S(2)}, u32[]{:S(2)}) collective-permute-start(bf16[176,128]{1,0:T(8,128)(2,1)S(1)} %get-tuple-element.50.refs_3_), channel_id=1, source_target_pairs={{0,7},{1,0},{2,1},{3,2},{4,3},{5,4},{6,5},{7,6},{8,15},{9,8},{10,9... | collective-permute-start | bytes 135176 | tf_op jit(solution)/shard_map/ppermute | solution.py:32
  6.6 2.3 %shard_map.123 = (bf16[352,352]{1,0:T(8,128)(2,1)S(1)}, bf16[368,368]{1,0:T(8,128)(2,1)S(1)}, bf16[304,304]{1,0:T(8,128)(2,1)S(1)}, bf16[192,192]{1,0:T(8,128)(2...) custom-call(s32[8,384]{1,0:T(8,128)S(1)} %get-tuple-element.42.refs_, ...), custom_call_target="tpu_custom_call" | custom-call | bytes 6000000 | tf_op jit(solution)/shard_map/pallas_call | solution.py:172
  8.9 0.4 shard_map.124.refs_0_
  9.3 0.0 collective-permute-done.refs_1_
  9.3 0.0 collective-permute-done.1.refs_2_
  9.3 1.2 %shard_map.125 = (f32[768,128]{1,0:T(8,128)S(1)}, bf16[176,128]{1,0:T(8,128)(2,1)S(1)}, bf16[176,128]{1,0:T(8,128)(2,1)S(1)}, bf16[176,176]{1,0:T(8,128)(2,1)S(1)}, bf16[176,176]{1,0:T(8,128)(2,1)S(1)}) custom-call(f32[768,128]{1,0:T(8,128)S(1)} %shard_map.124.refs_0_, bf16[176,128]{1,0:T(8,128)(2,1)S(1)} %collective-permute-done.refs_1_, ...), custom_call_target="tpu_custom_call" | custom-call | bytes 4500000 | tf_op jit(solution)/shard_map/pallas_call | solution.py:396
  10.6 0.1 collective-permute-start.2
  10.7 2.6 %collective-permute-start.3 = (bf16[176,128]{1,0:T(8,128)(2,1)S(1)}, bf16[176,128]{1,0:T(8,128)(2,1)S(1)}, u32[]{:S(2)}, u32[]{:S(2)}) collective-permute-start(bf16[176,128]{1,0:T(8,128)(2,1)S(1)} %get-tuple-element.60), channel_id=1, source_target_pairs={{0,7},{1,2},{2,1},{3,4},{4,3},{5,6},{6,5},{7,0},{8,15},{9,10},{10,... | collective-permute-start | bytes 135176 | tf_op jit(solution)/shard_map/ppermute | solution.py:899
  13.2 0.5 %shard_map.126.refs_0_.refs_4_ = f32[768,128]{1,0:T(8,128)S(1)} custom-call(f32[768,128]{1,0:T(8,128)S(1)} %get-tuple-element.56.refs_0_.refs_1_, f32[768,128]{1,0:T(8,128)S(1)} %get-tuple-element.41.refs_0_.refs_1_, f32[768,128]{1,0:T(8,128)S(1)} %get-tuple-element.45.refs_1_.refs_2_, bf16[352,352]{1,0:T(8,128)(2,1)S(1)} %get-tuple-element.46.refs_2_.refs_3_.refs_4_, ...), custom_call_target="tpu_custom_call" | custom-call | bytes 6000000 | tf_op jit(solution)/shard_map/pallas_call | solution.py:327
  13.7 0.0 collective-permute-done.2.refs_1_
  13.8 2.4 %collective-permute-done.3.refs_2_ = bf16[176,128]{1,0:T(8,128)(2,1)S(1)} collective-permute-done((bf16[176,128]{1,0:T(8,128)(2,1)S(1)}, bf16[176,128]{1,0:T(8,128)(2,1)S(1)}, u32[]{:S(2)}, u32[]{:S(2)}) %collective-permute-start.3) | collective-permute-done | bytes 45088 | tf_op jit(solution)/shard_map/ppermute | solution.py:899
  16.2 0.5 shard_map.127
  16.7 0.1 collective-permute-start.4
  16.8 2.4 %collective-permute-start.5 = (bf16[176,128]{1,0:T(8,128)(2,1)S(1)}, bf16[176,128]{1,0:T(8,128)(2,1)S(1)}, u32[]{:S(2)}, u32[]{:S(2)}) collective-permute-start(bf16[176,128]{1,0:T(8,128)(2,1)S(1)} %get-tuple-element.63), channel_id=1, source_target_pairs={{0,7},{1,2},{2,1},{3,4},{4,3},{5,6},{6,5},{7,0},{8,15},{9,10},{10,... | collective-permute-start | bytes 135176 | tf_op jit(solution)/shard_map/ppermute | solution.py:899
  19.1 0.5 %shard_map.129.refs_8_ = f32[4,8,128]{2,1,0:T(8,128)S(1)} custom-call(s32[2,729]{1,0:T(2,128)S(1)} %get-tuple-element.65.refs_0_, s32[1,81]{1,0:T(1,128)S(1)} %get-tuple-element.66.refs_1_, s32[1,8]{1,0:T(1,128)S(1)} %get-tuple-element.67.refs_2_, f32[6,128]{1,0:T(8,128)S(1)} %get-tuple-element.68.refs_3_, f32[768,128]{1,0:T(8,128)S(1)} %shard_map.126.refs_0_.refs_4_), custom_call_target="tpu_custom_call" | custom-call | bytes 3000000 | tf_op jit(solution)/shard_map/pallas_call | solution.py:593
  19.7 0.5 %shard_map.128.refs_0_ = f32[768,128]{1,0:T(8,128)S(1)} custom-call(f32[768,128]{1,0:T(8,128)S(1)} %get-tuple-element.61.refs_0_, f32[768,128]{1,0:T(8,128)S(1)} %get-tuple-element.56.refs_0_.refs_1_, f32[768,128]{1,0:T(8,128)S(1)} %get-tuple-element.45.refs_1_.refs_2_, bf16[352,352]{1,0:T(8,128)(2,1)S(1)} %get-tuple-element.46.refs_2_.refs_3_.refs_4_, ...), custom_call_target="tpu_custom_call" | custom-call | bytes 6000000 | tf_op jit(solution)/shard_map/pallas_call | solution.py:327
  20.2 0.0 collective-permute-done.4.refs_1_
  20.2 1.9 %collective-permute-done.5.refs_2_ = bf16[176,128]{1,0:T(8,128)(2,1)S(1)} collective-permute-done((bf16[176,128]{1,0:T(8,128)(2,1)S(1)}, bf16[176,128]{1,0:T(8,128)(2,1)S(1)}, u32[]{:S(2)}, u32[]{:S(2)}) %collective-permute-start.5) | collective-permute-done | bytes 45088 | tf_op jit(solution)/shard_map/ppermute | solution.py:899
  22.1 1.2 %shard_map.130 = (f32[768,128]{1,0:T(8,128)S(1)}, bf16[176,128]{1,0:T(8,128)(2,1)S(1)}, bf16[176,128]{1,0:T(8,128)(2,1)S(1)}, f32[32,1,1408]{2,1,0:T(1,128)}) custom-call(f32[768,128]{1,0:T(8,128)S(1)} %shard_map.128.refs_0_, bf16[176,128]{1,0:T(8,128)(2,1)S(1)} %collective-permute-done.4.refs_1_, bf16[176,128]{1,0:T(8,128)(2,1)S(1)} %collective-permute-done.5.refs_2_, ...), custom_call_target="tpu_custom_call" | custom-call | bytes 3000000 | tf_op jit(solution)/shard_map/pallas_call | solution.py:488
  23.3 5.0 %all-to-all-start = ((f32[32,1,1408]{2,1,0:T(1,128)}), f32[32,1,1408]{2,1,0:T(1,128)S(1)}, u32[]{:S(2)}, u32[]{:S(2)}) async-start(f32[32,1,1408]{2,1,0:T(1,128)} %get-tuple-element.72), calls=%async_computation | async-start | bytes 360448 | tf_op jit(solution)/shard_map/all_to_all | solution.py:871
  28.3 0.3 collective-permute-start.6
  28.6 3.5 %collective-permute-start.7 = (bf16[176,128]{1,0:T(8,128)(2,1)S(1)}, bf16[176,128]{1,0:T(8,128)(2,1)S(1)}, u32[]{:S(2)}, u32[]{:S(2)}) collective-permute-start(bf16[176,128]{1,0:T(8,128)(2,1)S(1)} %get-tuple-element.71), channel_id=1, source_target_pairs={{0,7},{1,2},{2,1},{3,4},{4,3},{5,6},{6,5},{7,0},{8,15},{9,10},{10,... | collective-permute-start | bytes 135176 | tf_op jit(solution)/shard_map/ppermute | solution.py:899
  32.1 0.5 shard_map.131.refs_0_
  32.6 4.4 %all-to-all-done.got_ref = f32[32,1,1408]{2,1,0:T(1,128)S(1)} async-done(((f32[32,1,1408]{2,1,0:T(1,128)}), f32[32,1,1408]{2,1,0:T(1,128)S(1)}, u32[]{:S(2)}, u32[]{:S(2)}) %all-to-all-start) | async-done | bytes 180256 | tf_op jit(solution)/shard_map/all_to_all | solution.py:871
  37.0 3.6 %shard_map.132 = (f32[768,128]{1,0:T(8,128)S(1)}, f32[6,128]{1,0:T(8,128)S(1)}) custom-call(f32[32,1,1408]{2,1,0:T(1,128)S(1)} %all-to-all-done.got_ref, f32[729,729]{1,0:T(8,128)} %matrix_hbm.1), custom_call_target="tpu_custom_call" | custom-call | bytes 12000000 | tf_op jit(solution)/shard_map/pallas_call | solution.py:742
  40.5 0.0 collective-permute-done.6.refs_1_
  40.5 0.0 collective-permute-done.7.refs_2_
  40.6 0.5 %shard_map.133 = (f32[768,128]{1,0:T(8,128)S(1)}, bf16[176,128]{1,0:T(8,128)(2,1)S(1)}, bf16[176,128]{1,0:T(8,128)(2,1)S(1)}) custom-call(f32[768,128]{1,0:T(8,128)S(1)} %shard_map.131.refs_0_, bf16[176,128]{1,0:T(8,128)(2,1)S(1)} %collective-permute-done.6.refs_1_, bf16[176,128]{1,0:T(8,128)(2,1)S(1)} %collective-permute-done.7.refs_2_, ...), custom_call_target="tpu_custom_call" | custom-call | bytes 3000000 | tf_op jit(solution)/shard_map/pallas_call | solution.py:488
  41.0 1.1 %collective-permute-start.8 = (bf16[176,128]{1,0:T(8,128)(2,1)S(1)}, bf16[176,128]{1,0:T(8,128)(2,1)S(1)}, u32[]{:S(2)}, u32[]{:S(2)}) collective-permute-start(bf16[176,128]{1,0:T(8,128)(2,1)S(1)} %get-tuple-element.75), channel_id=1, source_target_pairs={{0,1},{1,0},{2,3},{3,2},{4,5},{5,4},{6,7},{7,6},{8,9},{9,8},{10,11... | collective-permute-start | bytes 135176 | tf_op jit(solution)/shard_map/ppermute | solution.py:900
  42.2 0.4 collective-permute-start.9
  42.5 0.5 %shard_map.134.refs_0_ = f32[768,128]{1,0:T(8,128)S(1)} custom-call(f32[768,128]{1,0:T(8,128)S(1)} %get-tuple-element.74.refs_0_, f32[768,128]{1,0:T(8,128)S(1)} %get-tuple-element.69.refs_0_.refs_8_.refs_1_, f32[768,128]{1,0:T(8,128)S(1)} %get-tuple-element.45.refs_1_.refs_2_, f32[768,128]{1,0:T(8,128)S(1)} %get-tuple-element.73.refs_7_.refs_3_, ...), custom_call_target="tpu_custom_call" | custom-call | bytes 6000000 | tf_op jit(solution)/shard_map/pallas_call | solution.py:327
  43.1 0.0 collective-permute-done.8.refs_1_
  43.1 4.4 %collective-permute-done.9.refs_2_ = bf16[176,128]{1,0:T(8,128)(2,1)S(1)} collective-permute-done((bf16[176,128]{1,0:T(8,128)(2,1)S(1)}, bf16[176,128]{1,0:T(8,128)(2,1)S(1)}, u32[]{:S(2)}, u32[]{:S(2)}) %collective-permute-start.9) | collective-permute-done | bytes 45088 | tf_op jit(solution)/shard_map/ppermute | solution.py:899
  47.5 1.0 %shard_map.135 = (f32[768,128]{1,0:T(8,128)}, f32[6,128]{1,0:T(8,128)}) custom-call(f32[768,128]{1,0:T(8,128)S(1)} %shard_map.134.refs_0_, bf16[176,128]{1,0:T(8,128)(2,1)S(1)} %collective-permute-done.8.refs_1_, bf16[176,128]{1,0:T(8,128)(2,1)S(1)} %collective-permute-done.9.refs_2_, bf16[304,176]{1,0:T(8,128)(2,1)S(1)} %get-tuple-element.52.refs_5_.refs_3_, ...), custom_call_target="tpu_custom_call" | custom-call | bytes 3000000 | tf_op jit(solution)/shard_map/pallas_call | solution.py:488
Async XLA Ops:
  1.9 7.4 %collective-permute-start.1 = (bf16[464,128]{1,0:T(8,128)(2,1)S(1)}, bf16[464,128]{1,0:T(8,128)(2,1)S(1)}, u32[]{:S(2)}, u32[]{:S(2)}) collective-permute-start(bf16[464,128]{1,0:T(8,128)(2,1)S(1)} %get-tuple-element.51), channel_id=1, source_target_pairs={{0,1},{1,2},{2,3},{3,4},{4,5},{5,6},{6,7},{7,0},{8,9},{9,10},{10,1... | collective-permute-start | bytes 356360 | tf_op jit(solution)/shard_map/ppermute | solution.py:32
  2.5 6.8 %collective-permute-start = (bf16[176,128]{1,0:T(8,128)(2,1)S(1)}, bf16[176,128]{1,0:T(8,128)(2,1)S(1)}, u32[]{:S(2)}, u32[]{:S(2)}) collective-permute-start(bf16[176,128]{1,0:T(8,128)(2,1)S(1)} %get-tuple-element.50.refs_3_), channel_id=1, source_target_pairs={{0,7},{1,0},{2,1},{3,2},{4,3},{5,4},{6,5},{7,6},{8,15},{9,8},{10,9... | collective-permute-start | bytes 135176 | tf_op jit(solution)/shard_map/ppermute | solution.py:32
  10.6 3.2 %collective-permute-start.2 = (bf16[176,128]{1,0:T(8,128)(2,1)S(1)}, bf16[176,128]{1,0:T(8,128)(2,1)S(1)}, u32[]{:S(2)}, u32[]{:S(2)}) collective-permute-start(bf16[176,128]{1,0:T(8,128)(2,1)S(1)} %get-tuple-element.59), channel_id=1, source_target_pairs={{0,1},{1,0},{2,3},{3,2},{4,5},{5,4},{6,7},{7,6},{8,9},{9,8},{10,11... | collective-permute-start | bytes 135176 | tf_op jit(solution)/shard_map/ppermute | solution.py:900
  10.7 5.5 %collective-permute-start.3 = (bf16[176,128]{1,0:T(8,128)(2,1)S(1)}, bf16[176,128]{1,0:T(8,128)(2,1)S(1)}, u32[]{:S(2)}, u32[]{:S(2)}) collective-permute-start(bf16[176,128]{1,0:T(8,128)(2,1)S(1)} %get-tuple-element.60), channel_id=1, source_target_pairs={{0,7},{1,2},{2,1},{3,4},{4,3},{5,6},{6,5},{7,0},{8,15},{9,10},{10,... | collective-permute-start | bytes 135176 | tf_op jit(solution)/shard_map/ppermute | solution.py:899
  16.7 3.5 %collective-permute-start.4 = (bf16[176,128]{1,0:T(8,128)(2,1)S(1)}, bf16[176,128]{1,0:T(8,128)(2,1)S(1)}, u32[]{:S(2)}, u32[]{:S(2)}) collective-permute-start(bf16[176,128]{1,0:T(8,128)(2,1)S(1)} %get-tuple-element.62), channel_id=1, source_target_pairs={{0,1},{1,0},{2,3},{3,2},{4,5},{5,4},{6,7},{7,6},{8,9},{9,8},{10,11... | collective-permute-start | bytes 135176 | tf_op jit(solution)/shard_map/ppermute | solution.py:900
  16.8 5.3 %collective-permute-start.5 = (bf16[176,128]{1,0:T(8,128)(2,1)S(1)}, bf16[176,128]{1,0:T(8,128)(2,1)S(1)}, u32[]{:S(2)}, u32[]{:S(2)}) collective-permute-start(bf16[176,128]{1,0:T(8,128)(2,1)S(1)} %get-tuple-element.63), channel_id=1, source_target_pairs={{0,7},{1,2},{2,1},{3,4},{4,3},{5,6},{6,5},{7,0},{8,15},{9,10},{10,... | collective-permute-start | bytes 135176 | tf_op jit(solution)/shard_map/ppermute | solution.py:899
  23.3 13.7 %all-to-all-start = ((f32[32,1,1408]{2,1,0:T(1,128)}), f32[32,1,1408]{2,1,0:T(1,128)S(1)}, u32[]{:S(2)}, u32[]{:S(2)}) async-start(f32[32,1,1408]{2,1,0:T(1,128)} %get-tuple-element.72), calls=%async_computation | async-start | bytes 360448 | tf_op jit(solution)/shard_map/all_to_all | solution.py:871
  28.3 12.2 %collective-permute-start.6 = (bf16[176,128]{1,0:T(8,128)(2,1)S(1)}, bf16[176,128]{1,0:T(8,128)(2,1)S(1)}, u32[]{:S(2)}, u32[]{:S(2)}) collective-permute-start(bf16[176,128]{1,0:T(8,128)(2,1)S(1)} %get-tuple-element.70), channel_id=1, source_target_pairs={{0,1},{1,0},{2,3},{3,2},{4,5},{5,4},{6,7},{7,6},{8,9},{9,8},{10,11... | collective-permute-start | bytes 135176 | tf_op jit(solution)/shard_map/ppermute | solution.py:900
  28.6 11.9 %collective-permute-start.7 = (bf16[176,128]{1,0:T(8,128)(2,1)S(1)}, bf16[176,128]{1,0:T(8,128)(2,1)S(1)}, u32[]{:S(2)}, u32[]{:S(2)}) collective-permute-start(bf16[176,128]{1,0:T(8,128)(2,1)S(1)} %get-tuple-element.71), channel_id=1, source_target_pairs={{0,7},{1,2},{2,1},{3,4},{4,3},{5,6},{6,5},{7,0},{8,15},{9,10},{10,... | collective-permute-start | bytes 135176 | tf_op jit(solution)/shard_map/ppermute | solution.py:899
  41.0 2.0 %collective-permute-start.8 = (bf16[176,128]{1,0:T(8,128)(2,1)S(1)}, bf16[176,128]{1,0:T(8,128)(2,1)S(1)}, u32[]{:S(2)}, u32[]{:S(2)}) collective-permute-start(bf16[176,128]{1,0:T(8,128)(2,1)S(1)} %get-tuple-element.75), channel_id=1, source_target_pairs={{0,1},{1,0},{2,3},{3,2},{4,5},{5,4},{6,7},{7,6},{8,9},{9,8},{10,11... | collective-permute-start | bytes 135176 | tf_op jit(solution)/shard_map/ppermute | solution.py:900
  42.2 5.3 %collective-permute-start.9 = (bf16[176,128]{1,0:T(8,128)(2,1)S(1)}, bf16[176,128]{1,0:T(8,128)(2,1)S(1)}, u32[]{:S(2)}, u32[]{:S(2)}) collective-permute-start(bf16[176,128]{1,0:T(8,128)(2,1)S(1)} %get-tuple-element.76), channel_id=1, source_target_pairs={{0,7},{1,2},{2,1},{3,4},{4,3},{5,6},{6,5},{7,0},{8,15},{9,10},{10,... | collective-permute-start | bytes 135176 | tf_op jit(solution)/shard_map/ppermute | solution.py:899
where the time goes:
time: 48.7 us; the launch traced here: 48.4 us
  starting transfers between devices  20.1 us (41%)
  Pallas kernels  14.4 us (30%)
  waiting for transfers between devices  13.2 us (27%)
  between operations  0.8 us (2%)
    ppermute x4, starting transfers between devices, swap(): far = lax.ppermute(far, 'domain', turns)  8.81 us
    ppermute x4, waiting for transfers between devices, swap(): far = lax.ppermute(far, 'domain', turns)  8.75 us
    all_to_all x1, starting transfers between devices, on_device(): dens = lax.all_to_all(spread, ('band', 'domain'), 0, 0, tiled=True)  5 us
    ppermute x2, starting transfers between devices, from_behind(): lax.ppermute(array, axis, [(i, (i + by) % length) for i in range(length)])  4.64 us
    all_to_all x1, waiting for transfers between devices, on_device(): dens = lax.all_to_all(spread, ('band', 'domain'), 0, 0, tiled=True)  4.39 us
    pallas_call x1, Pallas kernels, field_step(): vmem_call(functools.partial(field_kernel, fg), [sds((fg.own, LANES), F32)...  3.56 us
    pallas_call x4, Pallas kernels, finish(): vmem_call(functools.partial(finish_kernel, geo, scale, mode, part_rows),...  3.11 us
    pallas_call x5, Pallas kernels, owned_part(): vmem_call(functools.partial(owned_part_kernel, geo, scale, prev is not No...  2.41 us
  transfers between devices with their start and end apart: 11, of which 4 were waited for; matrix products, arithmetic and copies ran while one was open for 0% of the time, Pallas kernels for 18%

commit v1 on v0

--- a/solution.py
+++ b/solution.py
@@ -377,33 +377,41 @@
         dens_ref[:, 0, own + r * LANES : own + (r + 1) * LANES] = jnp.broadcast_to(row, (parts, LANES))
 
 
+def behind_kernel(geo, sent_ref, matrix_ref, *refs):
+    n = len(geo.touching)
+    build_behind(geo, sent_ref, matrix_ref, *refs[2 * n :], refs[:n], refs[n : 2 * n])
+
+
+def behind_matrices(geo, sent, matrix):
+    shapes = [sds((geo.sp, geo.windows[c].rows), BF) for c in geo.touching]
+    shapes += [sds((geo.sp, geo.sp), BF) for _ in geo.touching]
+    outs = vmem_call(
+        functools.partial(behind_kernel, geo),
+        shapes,
+        [table_scratch(geo), matrix_scratch(geo)],
+        cost=cost_of(1.0),
+    )(sent, matrix)
+    return outs[: len(geo.touching)], outs[len(geo.touching) :]
+
+
 def first_finish_kernel(geo, scale, *refs):
     n = len(geo.touching)
-    base_ref, up_ref, dn_ref, own_up_ref, matrix_ref = refs[:5]
-    crosses, reaches, refs = refs[5 : 5 + n], refs[5 + n : 5 + 2 * n], refs[5 + 2 * n :]
-    y_ref, near_out, far_out = refs[:3]
-    uppers, behinds = refs[3 : 3 + n], refs[3 + n : 3 + 2 * n]
-    build_behind(geo, dn_ref, matrix_ref, *refs[-2:], behinds, uppers)
+    base_ref, up_ref, dn_ref, own_up_ref = refs[:4]
+    crosses, reaches, behinds, uppers = (refs[4 + i * n : 4 + (i + 1) * n] for i in range(4))
+    y_ref, near_out, far_out = refs[4 + 4 * n :]
     y_ref[...] = base_ref[...]
     add_upper(geo, scale, y_ref, up_ref[...], crosses)
     add_rows(geo, scale, y_ref, dn_ref[...], behinds, uppers, own_up_ref[...])
     write_sends(geo, y_ref, reaches, near_out, far_out)
 
 
-def first_finish(geo, scale, base, halo, own_up, matrix, crosses, reaches):
-    shapes = [sds(base.shape, F32), *send_shapes(geo, base.shape[1])]
-    shapes += [sds((geo.sp, geo.sp), BF) for _ in geo.touching]
-    y, near, far, *uppers = vmem_call(
+def first_finish(geo, scale, base, halo, own_up, crosses, reaches, behinds, uppers):
+    y, near, far = vmem_call(
         functools.partial(first_finish_kernel, geo, scale),
-        shapes,
-        [
-            *[pltpu.VMEM((geo.sp, geo.windows[c].rows), BF) for c in geo.touching],
-            table_scratch(geo),
-            matrix_scratch(geo),
-        ],
-        cost=cost_of(1.5),
-    )(base, halo[0], halo[1], own_up, matrix, *crosses, *reaches)
-    return y, (near, far), uppers
+        [sds(base.shape, F32), *send_shapes(geo, base.shape[1])],
+        cost=cost_of(0.5),
+    )(base, halo[0], halo[1], own_up, *crosses, *reaches, *behinds, *uppers)
+    return y, (near, far)
 
 
 def finish_kernel(geo, scale, mode, part_rows, *refs):
@@ -419,13 +427,8 @@
     reaches, refs = refs[:n], refs[n:]
     if mode == "density":
         occ_ref, table_ref = refs.pop(0), refs.pop(0)
-    if mode == "field":
-        column_ref, before_ref = refs.pop(0), refs.pop(0)
     y_ref = refs.pop(0)
-    if mode == "field":
-        y_ref[...] = base_ref[...] + (column_ref[...] * scale) * before_ref[...]
-    else:
-        y_ref[...] = base_ref[...]
+    y_ref[...] = base_ref[...]
     add_halo(geo, scale, y_ref, *halo)
     if mode == "density":
         _, _, out_hbm, dens, sem = refs
@@ -457,7 +460,7 @@
         copy.wait()
 
 
-def finish(geo, scale, base, halo, crosses, reaches=(), density=None, field=None, last=None):
+def finish(geo, scale, base, halo, crosses, reaches=(), density=None, last=None):
     columns = base.shape[1]
     args = [base, halo[0], halo[1], *crosses, *reaches]
     mode, part_rows = "plain", 0
@@ -473,9 +476,6 @@
         scratch = [pltpu.VMEM(base.shape, F32), pltpu.SemaphoreType.DMA((3 + len(last),))]
     else:
         shapes += send_shapes(geo, columns)
-    if field is not None:
-        mode = "field"
-        args += list(field)
     if density is not None:
         mode = "density"
         fg, weights, table = density
@@ -721,9 +721,15 @@
     return [(x + y) + z for x, y, z in zip(step_one, step_two, step_three)]
 
 
-def field_kernel(fg, got_ref, matrix_hbm, column_ref, hartree_ref, codes, rows, mine, matrix_ref, high_ref, low_ref, sems):
+def field_kernel(geo, fg, scale, got_ref, matrix_hbm, base_ref, near_ref, far_ref, y_ref, *refs):
+    n = len(geo.touching)
+    crosses, reaches, refs = refs[:n], refs[n : 2 * n], refs[2 * n :]
+    z_ref, near_out, far_out, column_ref, hartree_ref = refs[:5]
+    codes, rows, mine, matrix_ref, high_ref, low_ref, sems = refs[5:]
     spans = [pl.ds(r * LANES, min(LANES, fg.npc - r * LANES)) for r in range(fg.rows)]
     copies = fetch([(matrix_hbm.at[span], matrix_ref.at[span]) for span in spans], sems)
+    z_ref[...] = base_ref[...]
+    add_halo(geo, scale, z_ref, near_ref, far_ref, crosses)
     places, owner, screens = decode(fg, got_ref, codes)
     source = field_source(fg, got_ref, places)
     solved = field_solve(fg, source, codes, screens, matrix_ref, high_ref, low_ref, rows, copies)
@@ -731,17 +737,29 @@
     block = lookup(list(enumerate(solved)), lane + lax.axis_index("domain") * fg.block)
     mine[...] = rows_of(block, owner)
     for j in range(fg.domains):
-        column = column_of(mine[j : j + 1, :])
-        column_ref[j * fg.block : (j + 1) * fg.block, :] = column[0 : fg.block, :]
+        at = slice(j * fg.block, (j + 1) * fg.block)
+        column = column_of(mine[j : j + 1, :])[0 : fg.block, :]
+        column_ref[at, :] = column
+        z_ref[at, :] += (column * scale) * y_ref[at, :]
+    write_sends(geo, z_ref, reaches, near_out, far_out)
     for row, start, j, offset, count in pieces(fg.block, fg.domains):
         hartree_ref[row : row + 1, start : start + count] = mine[j : j + 1, offset : offset + count]
 
 
-def field_step(fg, got, matrix):
+def field_step(geo, fg, scale, got, matrix, base, halo, y, crosses, reaches):
     tile = (fg.domains, LANES)
-    return vmem_call(
-        functools.partial(field_kernel, fg),
-        [sds((fg.own, LANES), F32), sds((fg.lines, LANES), F32)],
+    vmem = pl.BlockSpec(memory_space=pltpu.VMEM)
+    args = [got, *in_hbm(matrix), base, *halo, y, *crosses, *reaches]
+    specs = [vmem] * len(args)
+    specs[1] = pl.BlockSpec(memory_space=pltpu.HBM)
+    z, near, far, column, lines = vmem_call(
+        functools.partial(field_kernel, geo, fg, scale),
+        [
+            sds(y.shape, F32),
+            *send_shapes(geo, y.shape[1]),
+            sds((fg.own, LANES), F32),
+            sds((fg.lines, LANES), F32),
+        ],
         [
             pltpu.VMEM((2 * fg.at_screen, *tile), I32),
             pltpu.VMEM((fg.cells * fg.domains, fg.size), F32),
@@ -751,9 +769,10 @@
             pltpu.VMEM(matrix.shape, BF),
             pltpu.SemaphoreType.DMA((fg.rows,)),
         ],
-        in_specs=[pl.BlockSpec(memory_space=pltpu.VMEM), pl.BlockSpec(memory_space=pltpu.HBM)],
+        in_specs=specs,
         cost=cost_of(4.0),
-    )(got, *in_hbm(matrix))
+    )(*args)
+    return z, (near, far), column, lines
 
 
 def assembled(owned_rows, face_row, terms):
@@ -851,8 +870,9 @@
     halo = exchange(sends)
     mats, crosses, reaches, pot = own_matrices(geo, nodes, matrix, lines)
     base = owned_part(geo, first, y0, None, pot, None, mats, ())
-    y1, sends1, uppers = first_finish(
-        geo, first, base, halo, sends[1], matrix, crosses, reaches
+    behinds, uppers = behind_matrices(geo, halo[1], matrix)
+    y1, sends1 = first_finish(
+        geo, first, base, halo, sends[1], crosses, reaches, behinds, uppers
     )
 
     halo = swap(sends1)
@@ -871,8 +891,9 @@
         dens = lax.all_to_all(spread, ("band", "domain"), 0, 0, tiled=True)
         halo = swap((dn, up))
         base = owned_part(geo, first, y3, None, pot, None, mats, uppers)
-        column, packed = field_step(fg, dens, pois_matrix)
-        z1, *sends4 = finish(geo, first, base, halo, crosses, reaches, field=(column, y3))
+        z1, sends4, column, packed = field_step(
+            geo, fg, first, dens, pois_matrix, base, halo, y3, crosses, reaches
+        )
     else:
         y3, *sends3 = finish(geo, later, base, halo, crosses, reaches)
         halo = swap(sends3)

time: 48.7 us -> 48.2 us (0.990)
  starting transfers between devices: 20.1 us -> 19.3 us
    ppermute x4, waiting for transfers between devices: 8.75 us -> 12.5 us  [swap(): far = lax.ppermute(far, 'domain', turns)]
    all_to_all x1, waiting for transfers between devices: 4.39 us -> 0.69 us  [on_device(): dens = lax.all_to_all(spread, ('band', 'domain'), 0, 0, tiled=True)]
    pallas_call x2 -> x3, Pallas kernels: 4.8 us -> 5.52 us  [the longest x1 4.12 us: field_step(): vmem_call(functools.partial(field_kernel, geo, fg, scale), [sds(y.shape,...]
    pallas_call x4 -> x3, Pallas kernels: 3.11 us -> 2.61 us  [finish(): vmem_call(functools.partial(finish_kernel, geo, scale, mode, part_rows),...]
  transfers between devices with their start and end apart: 11 -> 11, of which waited for: 4 -> 5; matrix products, arithmetic and copies ran while one was open for 0% -> 0% of each run, Pallas kernels for 18% -> 12%
where the time goes in v1:
time: 48.2 us; the launch traced here: 47.9 us
  starting transfers between devices  19.3 us (40%)
  Pallas kernels  14.6 us (30%)
  waiting for transfers between devices  13.2 us (27%)
  between operations  0.8 us (2%)
    ppermute x4, waiting for transfers between devices, swap(): far = lax.ppermute(far, 'domain', turns)  12.5 us
    ppermute x4, starting transfers between devices, swap(): far = lax.ppermute(far, 'domain', turns)  8.54 us
    ppermute x2, starting transfers between devices, from_behind(): lax.ppermute(array, axis, [(i, (i + by) % length) for i in range(length)])  4.64 us
    all_to_all x1, starting transfers between devices, on_device(): dens = lax.all_to_all(spread, ('band', 'domain'), 0, 0, tiled=True)  4.54 us
    pallas_call x1, Pallas kernels, field_step(): vmem_call(functools.partial(field_kernel, geo, fg, scale), [sds(y.shape,...  4.12 us
    pallas_call x3, Pallas kernels, finish(): vmem_call(functools.partial(finish_kernel, geo, scale, mode, part_rows),...  2.61 us
    pallas_call x5, Pallas kernels, owned_part(): vmem_call(functools.partial(owned_part_kernel, geo, scale, prev is not No...  2.42 us
    pallas_call x1, Pallas kernels, own_matrices(): vmem_call(functools.partial(own_matrices_kernel, geo), shapes, [matrix_sc...  2.25 us
  transfers between devices with their start and end apart: 11, of which 5 were waited for; matrix products, arithmetic and copies ran while one was open for 0% of the time, Pallas kernels for 12%

profile of v1, /device:TPU:0, one launch (start us, length us, event | category | flops | bytes accessed | tf_op | source)
XLA Modules:
  0.0 47.9 jit_solution(4182949300494805821)
XLA Ops:
  0.6 1.3 %shard_map.122 = (bf16[464,128]{1,0:T(8,128)(2,1)S(1)}, bf16[176,128]{1,0:T(8,128)(2,1)S(1)}, f32[768,128]{1,0:T(8,128)S(1)}, s32[8,384]{1,0:T(8,128)S(1)}, bf16...) custom-call(f32[768,128]{1,0:T(8,128)} %y_hbm.1, ...), custom_call_target="tpu_custom_call" | custom-call | bytes 3000000 | tf_op jit(solution)/shard_map/pallas_call | solution.py:270
  1.9 0.5 %collective-permute-start.1 = (bf16[464,128]{1,0:T(8,128)(2,1)S(1)}, bf16[464,128]{1,0:T(8,128)(2,1)S(1)}, u32[]{:S(2)}, u32[]{:S(2)}) collective-permute-start(bf16[464,128]{1,0:T(8,128)(2,1)S(1)} %get-tuple-element.53), channel_id=1, source_target_pairs={{0,1},{1,2},{2,3},{3,4},{4,5},{5,6},{6,7},{7,0},{8,9},{9,10},{10,1... | collective-permute-start | bytes 356360 | tf_op jit(solution)/shard_map/ppermute | solution.py:32
  2.5 4.1 %collective-permute-start = (bf16[176,128]{1,0:T(8,128)(2,1)S(1)}, bf16[176,128]{1,0:T(8,128)(2,1)S(1)}, u32[]{:S(2)}, u32[]{:S(2)}) collective-permute-start(bf16[176,128]{1,0:T(8,128)(2,1)S(1)} %get-tuple-element.52.refs_3_), channel_id=1, source_target_pairs={{0,7},{1,0},{2,1},{3,2},{4,3},{5,4},{6,5},{7,6},{8,15},{9,8},{10,9... | collective-permute-start | bytes 135176 | tf_op jit(solution)/shard_map/ppermute | solution.py:32
  6.6 2.3 %shard_map.123 = (bf16[352,352]{1,0:T(8,128)(2,1)S(1)}, bf16[368,368]{1,0:T(8,128)(2,1)S(1)}, bf16[304,304]{1,0:T(8,128)(2,1)S(1)}, bf16[192,192]{1,0:T(8,128)(2...) custom-call(s32[8,384]{1,0:T(8,128)S(1)} %get-tuple-element.44.refs_, ...), custom_call_target="tpu_custom_call" | custom-call | bytes 6000000 | tf_op jit(solution)/shard_map/pallas_call | solution.py:172
  8.8 0.4 shard_map.124.refs_0_
  9.3 0.0 collective-permute-done.1.sent_ref.refs_2_
  9.3 0.7 %shard_map.125 = (bf16[176,304]{1,0:T(8,128)(2,1)S(1)}, bf16[176,192]{1,0:T(8,128)(2,1)S(1)}, bf16[176,176]{1,0:T(8,128)(2,1)S(1)}, bf16[176,176]{1,0:T(8,128)(2,1)S(1)}) custom-call(bf16[464,128]{1,0:T(8,128)(2,1)S(1)} %collective-permute-done.1.sent_ref.refs_2_, bf16[343,343]{1,0:T(8,128)(2,1)S(1)} %get-tuple-element.45.refs_1_.matrix_ref), custom_call_target="tpu_custom_call" | custom-call | bytes 3000000 | tf_op jit(solution)/shard_map/pallas_call | solution.py:388
  10.0 0.0 collective-permute-done.refs_1_
  10.1 0.7 %shard_map.126 = (f32[768,128]{1,0:T(8,128)S(1)}, bf16[176,128]{1,0:T(8,128)(2,1)S(1)}, bf16[176,128]{1,0:T(8,128)(2,1)S(1)}) custom-call(f32[768,128]{1,0:T(8,128)S(1)} %shard_map.124.refs_0_, bf16[176,128]{1,0:T(8,128)(2,1)S(1)} %collective-permute-done.refs_1_, bf16[464,128]{1,0:T(8,128)(2,1)S(1)} %collective-permute-done.1.sent_ref.refs_2_, ...), custom_call_target="tpu_custom_call" | custom-call | bytes 1500000 | tf_op jit(solution)/shard_map/pallas_call | solution.py:409
  10.7 0.1 collective-permute-start.2
  10.8 2.3 %collective-permute-start.3 = (bf16[176,128]{1,0:T(8,128)(2,1)S(1)}, bf16[176,128]{1,0:T(8,128)(2,1)S(1)}, u32[]{:S(2)}, u32[]{:S(2)}) collective-permute-start(bf16[176,128]{1,0:T(8,128)(2,1)S(1)} %get-tuple-element.64), channel_id=1, source_target_pairs={{0,7},{1,2},{2,1},{3,4},{4,3},{5,6},{6,5},{7,0},{8,15},{9,10},{10,... | collective-permute-start | bytes 135176 | tf_op jit(solution)/shard_map/ppermute | solution.py:920
  13.1 0.5 %shard_map.127.refs_0_.refs_4_ = f32[768,128]{1,0:T(8,128)S(1)} custom-call(f32[768,128]{1,0:T(8,128)S(1)} %get-tuple-element.62.refs_0_.refs_1_, f32[768,128]{1,0:T(8,128)S(1)} %get-tuple-element.43.refs_0_.refs_1_, f32[768,128]{1,0:T(8,128)S(1)} %get-tuple-element.47.refs_1_.refs_2_, bf16[352,352]{1,0:T(8,128)(2,1)S(1)} %get-tuple-element.48.refs_2_.refs_3_.refs_4_, ...), custom_call_target="tpu_custom_call" | custom-call | bytes 6000000 | tf_op jit(solution)/shard_map/pallas_call | solution.py:327
  13.6 0.0 collective-permute-done.2.refs_1_
  13.7 2.5 %collective-permute-done.3.refs_2_ = bf16[176,128]{1,0:T(8,128)(2,1)S(1)} collective-permute-done((bf16[176,128]{1,0:T(8,128)(2,1)S(1)}, bf16[176,128]{1,0:T(8,128)(2,1)S(1)}, u32[]{:S(2)}, u32[]{:S(2)}) %collective-permute-start.3) | collective-permute-done | bytes 45088 | tf_op jit(solution)/shard_map/ppermute | solution.py:920
  16.1 0.5 shard_map.128
  16.6 0.1 collective-permute-start.4
  16.7 2.3 %collective-permute-start.5 = (bf16[176,128]{1,0:T(8,128)(2,1)S(1)}, bf16[176,128]{1,0:T(8,128)(2,1)S(1)}, u32[]{:S(2)}, u32[]{:S(2)}) collective-permute-start(bf16[176,128]{1,0:T(8,128)(2,1)S(1)} %get-tuple-element.67), channel_id=1, source_target_pairs={{0,7},{1,2},{2,1},{3,4},{4,3},{5,6},{6,5},{7,0},{8,15},{9,10},{10,... | collective-permute-start | bytes 135176 | tf_op jit(solution)/shard_map/ppermute | solution.py:920
  19.0 0.5 %shard_map.130.refs_8_ = f32[4,8,128]{2,1,0:T(8,128)S(1)} custom-call(s32[2,729]{1,0:T(2,128)S(1)} %get-tuple-element.69.refs_0_, s32[1,81]{1,0:T(1,128)S(1)} %get-tuple-element.70.refs_1_, s32[1,8]{1,0:T(1,128)S(1)} %get-tuple-element.71.refs_2_, f32[6,128]{1,0:T(8,128)S(1)} %get-tuple-element.72.refs_3_, f32[768,128]{1,0:T(8,128)S(1)} %shard_map.127.refs_0_.refs_4_), custom_call_target="tpu_custom_call" | custom-call | bytes 3000000 | tf_op jit(solution)/shard_map/pallas_call | solution.py:593
  19.6 0.5 %shard_map.129.refs_0_ = f32[768,128]{1,0:T(8,128)S(1)} custom-call(f32[768,128]{1,0:T(8,128)S(1)} %get-tuple-element.65.refs_0_, f32[768,128]{1,0:T(8,128)S(1)} %get-tuple-element.62.refs_0_.refs_1_, f32[768,128]{1,0:T(8,128)S(1)} %get-tuple-element.47.refs_1_.refs_2_, bf16[352,352]{1,0:T(8,128)(2,1)S(1)} %get-tuple-element.48.refs_2_.refs_3_.refs_4_, ...), custom_call_target="tpu_custom_call" | custom-call | bytes 6000000 | tf_op jit(solution)/shard_map/pallas_call | solution.py:327
  20.1 0.0 collective-permute-done.4.refs_1_
  20.1 2.0 %collective-permute-done.5.refs_2_ = bf16[176,128]{1,0:T(8,128)(2,1)S(1)} collective-permute-done((bf16[176,128]{1,0:T(8,128)(2,1)S(1)}, bf16[176,128]{1,0:T(8,128)(2,1)S(1)}, u32[]{:S(2)}, u32[]{:S(2)}) %collective-permute-start.5) | collective-permute-done | bytes 45088 | tf_op jit(solution)/shard_map/ppermute | solution.py:920
  22.0 1.2 %shard_map.131 = (f32[768,128]{1,0:T(8,128)S(1)}, bf16[176,128]{1,0:T(8,128)(2,1)S(1)}, bf16[176,128]{1,0:T(8,128)(2,1)S(1)}, f32[32,1,1408]{2,1,0:T(1,128)}) custom-call(f32[768,128]{1,0:T(8,128)S(1)} %shard_map.129.refs_0_, bf16[176,128]{1,0:T(8,128)(2,1)S(1)} %collective-permute-done.4.refs_1_, bf16[176,128]{1,0:T(8,128)(2,1)S(1)} %collective-permute-done.5.refs_2_, ...), custom_call_target="tpu_custom_call" | custom-call | bytes 3000000 | tf_op jit(solution)/shard_map/pallas_call | solution.py:488
  23.2 4.5 %all-to-all-start = ((f32[32,1,1408]{2,1,0:T(1,128)}), f32[32,1,1408]{2,1,0:T(1,128)S(1)}, u32[]{:S(2)}, u32[]{:S(2)}) async-start(f32[32,1,1408]{2,1,0:T(1,128)} %get-tuple-element.73), calls=%async_computation | async-start | bytes 360448 | tf_op jit(solution)/shard_map/all_to_all | solution.py:891
  27.8 0.3 collective-permute-start.6
  28.1 3.5 %collective-permute-start.7 = (bf16[176,128]{1,0:T(8,128)(2,1)S(1)}, bf16[176,128]{1,0:T(8,128)(2,1)S(1)}, u32[]{:S(2)}, u32[]{:S(2)}) collective-permute-start(bf16[176,128]{1,0:T(8,128)(2,1)S(1)} %get-tuple-element.76), channel_id=1, source_target_pairs={{0,7},{1,2},{2,1},{3,4},{4,3},{5,6},{6,5},{7,0},{8,15},{9,10},{10,... | collective-permute-start | bytes 135176 | tf_op jit(solution)/shard_map/ppermute | solution.py:920
  31.6 0.5 %shard_map.132.base_ref = f32[768,128]{1,0:T(8,128)S(1)} custom-call(f32[768,128]{1,0:T(8,128)S(1)} %get-tuple-element.74.refs_0_.y_ref.refs_1_, f32[768,128]{1,0:T(8,128)S(1)} %get-tuple-element.47.refs_1_.refs_2_, bf16[352,352]{1,0:T(8,128)(2,1)S(1)} %get-tuple-element.48.refs_2_.refs_3_.refs_4_, ...), custom_call_target="tpu_custom_call" | custom-call | bytes 6000000 | tf_op jit(solution)/shard_map/pallas_call | solution.py:327
  32.0 0.0 collective-permute-done.6.near_ref
  32.1 3.7 %collective-permute-done.7.far_ref = bf16[176,128]{1,0:T(8,128)(2,1)S(1)} collective-permute-done((bf16[176,128]{1,0:T(8,128)(2,1)S(1)}, bf16[176,128]{1,0:T(8,128)(2,1)S(1)}, u32[]{:S(2)}, u32[]{:S(2)}) %collective-permute-start.7) | collective-permute-done | bytes 45088 | tf_op jit(solution)/shard_map/ppermute | solution.py:920
  35.7 0.7 %all-to-all-done.got_ref = f32[32,1,1408]{2,1,0:T(1,128)S(1)} async-done(((f32[32,1,1408]{2,1,0:T(1,128)}), f32[32,1,1408]{2,1,0:T(1,128)S(1)}, u32[]{:S(2)}, u32[]{:S(2)}) %all-to-all-start) | async-done | bytes 180256 | tf_op jit(solution)/shard_map/all_to_all | solution.py:891
  36.4 4.1 %shard_map.133 = (f32[768,128]{1,0:T(8,128)S(1)}, bf16[176,128]{1,0:T(8,128)(2,1)S(1)}, bf16[176,128]{1,0:T(8,128)(2,1)S(1)}, f32[768,128]{1,0:T(8,128)S(1)}, f32[6,128]{1,0:T(8,128)S(1)}) custom-call(f32[32,1,1408]{2,1,0:T(1,128)S(1)} %all-to-all-done.got_ref, f32[729,729]{1,0:T(8,128)} %matrix_hbm.1, f32[768,128]{1,0:T(8,128)S(1)} %shard_map.132.base_ref, ...), custom_call_target="tpu_custom_call" | custom-call | bytes 12000000 | tf_op jit(solution)/shard_map/pallas_call | solution.py:755
  40.6 1.1 %collective-permute-start.8 = (bf16[176,128]{1,0:T(8,128)(2,1)S(1)}, bf16[176,128]{1,0:T(8,128)(2,1)S(1)}, u32[]{:S(2)}, u32[]{:S(2)}) collective-permute-start(bf16[176,128]{1,0:T(8,128)(2,1)S(1)} %get-tuple-element.79), channel_id=1, source_target_pairs={{0,1},{1,0},{2,3},{3,2},{4,5},{5,4},{6,7},{7,6},{8,9},{9,8},{10,11... | collective-permute-start | bytes 135176 | tf_op jit(solution)/shard_map/ppermute | solution.py:921
  41.7 0.4 collective-permute-start.9
  42.1 0.5 %shard_map.134.refs_0_ = f32[768,128]{1,0:T(8,128)S(1)} custom-call(f32[768,128]{1,0:T(8,128)S(1)} %get-tuple-element.77.refs_0_, f32[768,128]{1,0:T(8,128)S(1)} %get-tuple-element.74.refs_0_.y_ref.refs_1_, f32[768,128]{1,0:T(8,128)S(1)} %get-tuple-element.47.refs_1_.refs_2_, f32[768,128]{1,0:T(8,128)S(1)} %get-tuple-element.78.refs_3_, ...), custom_call_target="tpu_custom_call" | custom-call | bytes 6000000 | tf_op jit(solution)/shard_map/pallas_call | solution.py:327
  42.6 0.0 collective-permute-done.8.refs_1_
  42.6 4.4 %collective-permute-done.9.refs_2_ = bf16[176,128]{1,0:T(8,128)(2,1)S(1)} collective-permute-done((bf16[176,128]{1,0:T(8,128)(2,1)S(1)}, bf16[176,128]{1,0:T(8,128)(2,1)S(1)}, u32[]{:S(2)}, u32[]{:S(2)}) %collective-permute-start.9) | collective-permute-done | bytes 45088 | tf_op jit(solution)/shard_map/ppermute | solution.py:920
  47.0 1.0 %shard_map.135 = (f32[768,128]{1,0:T(8,128)}, f32[6,128]{1,0:T(8,128)}) custom-call(f32[768,128]{1,0:T(8,128)S(1)} %shard_map.134.refs_0_, bf16[176,128]{1,0:T(8,128)(2,1)S(1)} %collective-permute-done.8.refs_1_, bf16[176,128]{1,0:T(8,128)(2,1)S(1)} %collective-permute-done.9.refs_2_, bf16[304,176]{1,0:T(8,128)(2,1)S(1)} %get-tuple-element.54.refs_4_.refs_3_.refs_0_, ...), custom_call_target="tpu_custom_call" | custom-call | bytes 3000000 | tf_op jit(solution)/shard_map/pallas_call | solution.py:488
Async XLA Ops:
  1.9 7.3 %collective-permute-start.1 = (bf16[464,128]{1,0:T(8,128)(2,1)S(1)}, bf16[464,128]{1,0:T(8,128)(2,1)S(1)}, u32[]{:S(2)}, u32[]{:S(2)}) collective-permute-start(bf16[464,128]{1,0:T(8,128)(2,1)S(1)} %get-tuple-element.53), channel_id=1, source_target_pairs={{0,1},{1,2},{2,3},{3,4},{4,5},{5,6},{6,7},{7,0},{8,9},{9,10},{10,1... | collective-permute-start | bytes 356360 | tf_op jit(solution)/shard_map/ppermute | solution.py:32
  2.5 7.6 %collective-permute-start = (bf16[176,128]{1,0:T(8,128)(2,1)S(1)}, bf16[176,128]{1,0:T(8,128)(2,1)S(1)}, u32[]{:S(2)}, u32[]{:S(2)}) collective-permute-start(bf16[176,128]{1,0:T(8,128)(2,1)S(1)} %get-tuple-element.52.refs_3_), channel_id=1, source_target_pairs={{0,7},{1,0},{2,1},{3,2},{4,3},{5,4},{6,5},{7,6},{8,15},{9,8},{10,9... | collective-permute-start | bytes 135176 | tf_op jit(solution)/shard_map/ppermute | solution.py:32
  10.7 2.9 %collective-permute-start.2 = (bf16[176,128]{1,0:T(8,128)(2,1)S(1)}, bf16[176,128]{1,0:T(8,128)(2,1)S(1)}, u32[]{:S(2)}, u32[]{:S(2)}) collective-permute-start(bf16[176,128]{1,0:T(8,128)(2,1)S(1)} %get-tuple-element.63), channel_id=1, source_target_pairs={{0,1},{1,0},{2,3},{3,2},{4,5},{5,4},{6,7},{7,6},{8,9},{9,8},{10,11... | collective-permute-start | bytes 135176 | tf_op jit(solution)/shard_map/ppermute | solution.py:921
  10.8 5.3 %collective-permute-start.3 = (bf16[176,128]{1,0:T(8,128)(2,1)S(1)}, bf16[176,128]{1,0:T(8,128)(2,1)S(1)}, u32[]{:S(2)}, u32[]{:S(2)}) collective-permute-start(bf16[176,128]{1,0:T(8,128)(2,1)S(1)} %get-tuple-element.64), channel_id=1, source_target_pairs={{0,7},{1,2},{2,1},{3,4},{4,3},{5,6},{6,5},{7,0},{8,15},{9,10},{10,... | collective-permute-start | bytes 135176 | tf_op jit(solution)/shard_map/ppermute | solution.py:920
  16.6 3.4 %collective-permute-start.4 = (bf16[176,128]{1,0:T(8,128)(2,1)S(1)}, bf16[176,128]{1,0:T(8,128)(2,1)S(1)}, u32[]{:S(2)}, u32[]{:S(2)}) collective-permute-start(bf16[176,128]{1,0:T(8,128)(2,1)S(1)} %get-tuple-element.66), channel_id=1, source_target_pairs={{0,1},{1,0},{2,3},{3,2},{4,5},{5,4},{6,7},{7,6},{8,9},{9,8},{10,11... | collective-permute-start | bytes 135176 | tf_op jit(solution)/shard_map/ppermute | solution.py:921
  16.7 5.3 %collective-permute-start.5 = (bf16[176,128]{1,0:T(8,128)(2,1)S(1)}, bf16[176,128]{1,0:T(8,128)(2,1)S(1)}, u32[]{:S(2)}, u32[]{:S(2)}) collective-permute-start(bf16[176,128]{1,0:T(8,128)(2,1)S(1)} %get-tuple-element.67), channel_id=1, source_target_pairs={{0,7},{1,2},{2,1},{3,4},{4,3},{5,6},{6,5},{7,0},{8,15},{9,10},{10,... | collective-permute-start | bytes 135176 | tf_op jit(solution)/shard_map/ppermute | solution.py:920
  23.2 13.2 %all-to-all-start = ((f32[32,1,1408]{2,1,0:T(1,128)}), f32[32,1,1408]{2,1,0:T(1,128)S(1)}, u32[]{:S(2)}, u32[]{:S(2)}) async-start(f32[32,1,1408]{2,1,0:T(1,128)} %get-tuple-element.73), calls=%async_computation | async-start | bytes 360448 | tf_op jit(solution)/shard_map/all_to_all | solution.py:891
  27.8 4.3 %collective-permute-start.6 = (bf16[176,128]{1,0:T(8,128)(2,1)S(1)}, bf16[176,128]{1,0:T(8,128)(2,1)S(1)}, u32[]{:S(2)}, u32[]{:S(2)}) collective-permute-start(bf16[176,128]{1,0:T(8,128)(2,1)S(1)} %get-tuple-element.75), channel_id=1, source_target_pairs={{0,1},{1,0},{2,3},{3,2},{4,5},{5,4},{6,7},{7,6},{8,9},{9,8},{10,11... | collective-permute-start | bytes 135176 | tf_op jit(solution)/shard_map/ppermute | solution.py:921
  28.1 7.7 %collective-permute-start.7 = (bf16[176,128]{1,0:T(8,128)(2,1)S(1)}, bf16[176,128]{1,0:T(8,128)(2,1)S(1)}, u32[]{:S(2)}, u32[]{:S(2)}) collective-permute-start(bf16[176,128]{1,0:T(8,128)(2,1)S(1)} %get-tuple-element.76), channel_id=1, source_target_pairs={{0,7},{1,2},{2,1},{3,4},{4,3},{5,6},{6,5},{7,0},{8,15},{9,10},{10,... | collective-permute-start | bytes 135176 | tf_op jit(solution)/shard_map/ppermute | solution.py:920
  40.6 2.0 %collective-permute-start.8 = (bf16[176,128]{1,0:T(8,128)(2,1)S(1)}, bf16[176,128]{1,0:T(8,128)(2,1)S(1)}, u32[]{:S(2)}, u32[]{:S(2)}) collective-permute-start(bf16[176,128]{1,0:T(8,128)(2,1)S(1)} %get-tuple-element.79), channel_id=1, source_target_pairs={{0,1},{1,0},{2,3},{3,2},{4,5},{5,4},{6,7},{7,6},{8,9},{9,8},{10,11... | collective-permute-start | bytes 135176 | tf_op jit(solution)/shard_map/ppermute | solution.py:921
  41.7 5.3 %collective-permute-start.9 = (bf16[176,128]{1,0:T(8,128)(2,1)S(1)}, bf16[176,128]{1,0:T(8,128)(2,1)S(1)}, u32[]{:S(2)}, u32[]{:S(2)}) collective-permute-start(bf16[176,128]{1,0:T(8,128)(2,1)S(1)} %get-tuple-element.80), channel_id=1, source_target_pairs={{0,7},{1,2},{2,1},{3,4},{4,3},{5,6},{6,5},{7,0},{8,15},{9,10},{10,... | collective-permute-start | bytes 135176 | tf_op jit(solution)/shard_map/ppermute | solution.py:920

commit v2 on v1

--- a/solution.py
+++ b/solution.py
@@ -377,40 +377,44 @@
         dens_ref[:, 0, own + r * LANES : own + (r + 1) * LANES] = jnp.broadcast_to(row, (parts, LANES))
 
 
-def behind_kernel(geo, sent_ref, matrix_ref, *refs):
+def behind_kernel(geo, scale, sent_ref, matrix_ref, base_ref, own_up_ref, *refs):
     n = len(geo.touching)
-    build_behind(geo, sent_ref, matrix_ref, *refs[2 * n :], refs[:n], refs[n : 2 * n])
-
-
-def behind_matrices(geo, sent, matrix):
-    shapes = [sds((geo.sp, geo.windows[c].rows), BF) for c in geo.touching]
-    shapes += [sds((geo.sp, geo.sp), BF) for _ in geo.touching]
-    outs = vmem_call(
-        functools.partial(behind_kernel, geo),
-        shapes,
-        [table_scratch(geo), matrix_scratch(geo)],
+    uppers, out_ref, behinds, rest = refs[:n], refs[n], refs[n + 1 : 2 * n + 1], refs[2 * n + 1 :]
+    build_behind(geo, sent_ref, matrix_ref, *rest, behinds, uppers)
+    out_ref[...] = base_ref[...]
+    add_rows(geo, scale, out_ref, sent_ref[...], behinds, uppers, own_up_ref[...])
+
+
+def behind_sums(geo, scale, sent, matrix, base, own_up):
+    *uppers, base = vmem_call(
+        functools.partial(behind_kernel, geo, scale),
+        [sds((geo.sp, geo.sp), BF) for _ in geo.touching] + [sds(base.shape, F32)],
+        [
+            *[pltpu.VMEM((geo.sp, geo.windows[c].rows), BF) for c in geo.touching],
+            table_scratch(geo),
+            matrix_scratch(geo),
+        ],
         cost=cost_of(1.0),
-    )(sent, matrix)
-    return outs[: len(geo.touching)], outs[len(geo.touching) :]
+    )(sent, matrix, base, own_up)
+    return uppers, base
 
 
 def first_finish_kernel(geo, scale, *refs):
     n = len(geo.touching)
-    base_ref, up_ref, dn_ref, own_up_ref = refs[:4]
-    crosses, reaches, behinds, uppers = (refs[4 + i * n : 4 + (i + 1) * n] for i in range(4))
-    y_ref, near_out, far_out = refs[4 + 4 * n :]
+    base_ref, up_ref = refs[:2]
+    crosses, reaches = refs[2 : 2 + n], refs[2 + n : 2 + 2 * n]
+    y_ref, near_out, far_out = refs[2 + 2 * n :]
     y_ref[...] = base_ref[...]
     add_upper(geo, scale, y_ref, up_ref[...], crosses)
-    add_rows(geo, scale, y_ref, dn_ref[...], behinds, uppers, own_up_ref[...])
     write_sends(geo, y_ref, reaches, near_out, far_out)
 
 
-def first_finish(geo, scale, base, halo, own_up, crosses, reaches, behinds, uppers):
+def first_finish(geo, scale, base, h_up, crosses, reaches):
     y, near, far = vmem_call(
         functools.partial(first_finish_kernel, geo, scale),
         [sds(base.shape, F32), *send_shapes(geo, base.shape[1])],
         cost=cost_of(0.5),
-    )(base, halo[0], halo[1], own_up, *crosses, *reaches, *behinds, *uppers)
+    )(base, h_up, *crosses, *reaches)
     return y, (near, far)
 
 
@@ -673,7 +677,7 @@
     return source
 
 
-def field_solve(fg, source, codes, screen, matrix_ref, high_ref, low_ref, rows, copies):
+def field_solve(fg, source, codes, screen, matrix_ref, weight_ref, rows, copies):
     domains, cells = fg.domains, fg.cells
 
     def operator(field):
@@ -686,16 +690,13 @@
             if copies:
                 copies.pop(0).wait()
                 span = slice(r * LANES, min((r + 1) * LANES, fg.npc))
-                full = matrix_ref[span, :]
-                top = full.astype(BF)
-                high_ref[span, :] = top
-                low_ref[span, :] = (full - top.astype(F32)).astype(BF)
+                weight_ref[span, :] = matrix_ref[span, :].astype(BF)
         picked = rows[:, 0 : fg.npc]
         high = picked.astype(BF)
         low = (picked - high.astype(F32)).astype(BF)
-        both = dot(jnp.concatenate([high, low], axis=0), high_ref[...])
+        both = dot(jnp.concatenate([high, low], axis=0), weight_ref[...])
         half_rows = cells * domains
-        rows[:, 0 : fg.npc] = both[:half_rows] + (both[half_rows:] + dot(high, low_ref[...]))
+        rows[:, 0 : fg.npc] = both[:half_rows] + both[half_rows:]
         out = [None] * fg.tiles
         for c in range(cells):
             sources = [
@@ -725,14 +726,14 @@
     n = len(geo.touching)
     crosses, reaches, refs = refs[:n], refs[n : 2 * n], refs[2 * n :]
     z_ref, near_out, far_out, column_ref, hartree_ref = refs[:5]
-    codes, rows, mine, matrix_ref, high_ref, low_ref, sems = refs[5:]
+    codes, rows, mine, matrix_ref, weight_ref, sems = refs[5:]
     spans = [pl.ds(r * LANES, min(LANES, fg.npc - r * LANES)) for r in range(fg.rows)]
     copies = fetch([(matrix_hbm.at[span], matrix_ref.at[span]) for span in spans], sems)
     z_ref[...] = base_ref[...]
     add_halo(geo, scale, z_ref, near_ref, far_ref, crosses)
     places, owner, screens = decode(fg, got_ref, codes)
     source = field_source(fg, got_ref, places)
-    solved = field_solve(fg, source, codes, screens, matrix_ref, high_ref, low_ref, rows, copies)
+    solved = field_solve(fg, source, codes, screens, matrix_ref, weight_ref, rows, copies)
     lane = lax.broadcasted_iota(I32, (fg.domains, LANES), 1)
     block = lookup(list(enumerate(solved)), lane + lax.axis_index("domain") * fg.block)
     mine[...] = rows_of(block, owner)
@@ -766,7 +767,6 @@
             pltpu.VMEM(tile, F32),
             pltpu.VMEM(matrix.shape, F32),
             pltpu.VMEM(matrix.shape, BF),
-            pltpu.VMEM(matrix.shape, BF),
             pltpu.SemaphoreType.DMA((fg.rows,)),
         ],
         in_specs=specs,
@@ -870,10 +870,8 @@
     halo = exchange(sends)
     mats, crosses, reaches, pot = own_matrices(geo, nodes, matrix, lines)
     base = owned_part(geo, first, y0, None, pot, None, mats, ())
-    behinds, uppers = behind_matrices(geo, halo[1], matrix)
-    y1, sends1 = first_finish(
-        geo, first, base, halo, sends[1], crosses, reaches, behinds, uppers
-    )
+    uppers, base = behind_sums(geo, first, halo[1], matrix, base, sends[1])
+    y1, sends1 = first_finish(geo, first, base, halo[0], crosses, reaches)
 
     halo = swap(sends1)
     base = owned_part(geo, later, y1, y0, pot, None, mats, uppers)

time: 48.2 us -> 47.8 us (level)
  transfers between devices with their start and end apart: 11 -> 11, of which waited for: 5 -> 5; matrix products, arithmetic and copies ran while one was open for 0% -> 0% of each run, Pallas kernels for 12% -> 13%
where the time goes in v2:
time: 47.8 us; the launch traced here: 47.6 us
  starting transfers between devices  19.3 us (40%)
  Pallas kernels  14.3 us (30%)
  waiting for transfers between devices  13.2 us (28%)
  between operations  0.8 us (2%)
    ppermute x4, waiting for transfers between devices, swap(): far = lax.ppermute(far, 'domain', turns)  12.5 us
    ppermute x4, starting transfers between devices, swap(): far = lax.ppermute(far, 'domain', turns)  8.54 us
    ppermute x2, starting transfers between devices, from_behind(): lax.ppermute(array, axis, [(i, (i + by) % length) for i in range(length)])  4.64 us
    all_to_all x1, starting transfers between devices, on_device(): dens = lax.all_to_all(spread, ('band', 'domain'), 0, 0, tiled=True)  4.53 us
    pallas_call x1, Pallas kernels, field_step(): vmem_call(functools.partial(field_kernel, geo, fg, scale), [sds(y.shape,...  3.74 us
    pallas_call x3, Pallas kernels, finish(): vmem_call(functools.partial(finish_kernel, geo, scale, mode, part_rows),...  2.6 us
    pallas_call x5, Pallas kernels, owned_part(): vmem_call(functools.partial(owned_part_kernel, geo, scale, prev is not No...  2.42 us
    pallas_call x1, Pallas kernels, own_matrices(): vmem_call(functools.partial(own_matrices_kernel, geo), shapes, [matrix_sc...  2.25 us
  transfers between devices with their start and end apart: 11, of which 5 were waited for; matrix products, arithmetic and copies ran while one was open for 0% of the time, Pallas kernels for 13%

profile of v2, /device:TPU:0, one launch (start us, length us, event | category | flops | bytes accessed | tf_op | source)
XLA Modules:
  0.0 47.6 jit_solution(7874656344597349388)
XLA Ops:
  0.6 1.3 %shard_map.122 = (bf16[464,128]{1,0:T(8,128)(2,1)S(1)}, bf16[176,128]{1,0:T(8,128)(2,1)S(1)}, f32[768,128]{1,0:T(8,128)S(1)}, s32[8,384]{1,0:T(8,128)S(1)}, bf16...) custom-call(f32[768,128]{1,0:T(8,128)} %y_hbm.1, ...), custom_call_target="tpu_custom_call" | custom-call | bytes 3000000 | tf_op jit(solution)/shard_map/pallas_call | solution.py:270
  1.9 0.5 %collective-permute-start = (bf16[464,128]{1,0:T(8,128)(2,1)S(1)}, bf16[464,128]{1,0:T(8,128)(2,1)S(1)}, u32[]{:S(2)}, u32[]{:S(2)}) collective-permute-start(bf16[464,128]{1,0:T(8,128)(2,1)S(1)} %get-tuple-element.42), channel_id=1, source_target_pairs={{0,1},{1,2},{2,3},{3,4},{4,5},{5,6},{6,7},{7,0},{8,9},{9,10},{10,1... | collective-permute-start | bytes 356360 | tf_op jit(solution)/shard_map/ppermute | solution.py:32
  2.5 4.1 %collective-permute-start.1 = (bf16[176,128]{1,0:T(8,128)(2,1)S(1)}, bf16[176,128]{1,0:T(8,128)(2,1)S(1)}, u32[]{:S(2)}, u32[]{:S(2)}) collective-permute-start(bf16[176,128]{1,0:T(8,128)(2,1)S(1)} %get-tuple-element.52.own_up_ref), channel_id=1, source_target_pairs={{0,7},{1,0},{2,1},{3,2},{4,3},{5,4},{6,5},{7,6},{8,15},{9,8},{10,9... | collective-permute-start | bytes 135176 | tf_op jit(solution)/shard_map/ppermute | solution.py:32
  6.6 2.3 %shard_map.123 = (bf16[352,352]{1,0:T(8,128)(2,1)S(1)}, bf16[368,368]{1,0:T(8,128)(2,1)S(1)}, bf16[304,304]{1,0:T(8,128)(2,1)S(1)}, bf16[192,192]{1,0:T(8,128)(2...) custom-call(s32[8,384]{1,0:T(8,128)S(1)} %get-tuple-element.45.refs_, ...), custom_call_target="tpu_custom_call" | custom-call | bytes 6000000 | tf_op jit(solution)/shard_map/pallas_call | solution.py:172
  8.8 0.4 shard_map.124.base_ref
  9.3 0.0 collective-permute-done.sent_ref
  9.3 1.0 %shard_map.125 = (bf16[176,176]{1,0:T(8,128)(2,1)S(1)}, bf16[176,176]{1,0:T(8,128)(2,1)S(1)}, f32[768,128]{1,0:T(8,128)S(1)}) custom-call(bf16[464,128]{1,0:T(8,128)(2,1)S(1)} %collective-permute-done.sent_ref, bf16[343,343]{1,0:T(8,128)(2,1)S(1)} %get-tuple-element.43.refs_1_.matrix_ref, f32[768,128]{1,0:T(8,128)S(1)} %shard_map.124.base_ref, ...), custom_call_target="tpu_custom_call" | custom-call | bytes 3000000 | tf_op jit(solution)/shard_map/pallas_call | solution.py:389
  10.3 0.0 collective-permute-done.1.refs_1_
  10.3 0.5 shard_map.126
  10.8 0.1 collective-permute-start.2
  10.8 2.3 %collective-permute-start.3 = (bf16[176,128]{1,0:T(8,128)(2,1)S(1)}, bf16[176,128]{1,0:T(8,128)(2,1)S(1)}, u32[]{:S(2)}, u32[]{:S(2)}) collective-permute-start(bf16[176,128]{1,0:T(8,128)(2,1)S(1)} %get-tuple-element.62), channel_id=1, source_target_pairs={{0,7},{1,2},{2,1},{3,4},{4,3},{5,6},{6,5},{7,0},{8,15},{9,10},{10,... | collective-permute-start | bytes 135176 | tf_op jit(solution)/shard_map/ppermute | solution.py:918
  13.2 0.5 %shard_map.127.refs_0_.refs_4_ = f32[768,128]{1,0:T(8,128)S(1)} custom-call(f32[768,128]{1,0:T(8,128)S(1)} %get-tuple-element.58.refs_0_.refs_1_, f32[768,128]{1,0:T(8,128)S(1)} %get-tuple-element.44.refs_0_.refs_1_, f32[768,128]{1,0:T(8,128)S(1)} %get-tuple-element.47.refs_1_.refs_2_, bf16[352,352]{1,0:T(8,128)(2,1)S(1)} %get-tuple-element.48.refs_2_.refs_3_.refs_4_, ...), custom_call_target="tpu_custom_call" | custom-call | bytes 6000000 | tf_op jit(solution)/shard_map/pallas_call | solution.py:327
  13.7 0.0 collective-permute-done.2.refs_1_
  13.7 2.5 %collective-permute-done.3.refs_2_ = bf16[176,128]{1,0:T(8,128)(2,1)S(1)} collective-permute-done((bf16[176,128]{1,0:T(8,128)(2,1)S(1)}, bf16[176,128]{1,0:T(8,128)(2,1)S(1)}, u32[]{:S(2)}, u32[]{:S(2)}) %collective-permute-start.3) | collective-permute-done | bytes 45088 | tf_op jit(solution)/shard_map/ppermute | solution.py:918
  16.2 0.5 shard_map.128
  16.6 0.1 collective-permute-start.4
  16.7 2.3 %collective-permute-start.5 = (bf16[176,128]{1,0:T(8,128)(2,1)S(1)}, bf16[176,128]{1,0:T(8,128)(2,1)S(1)}, u32[]{:S(2)}, u32[]{:S(2)}) collective-permute-start(bf16[176,128]{1,0:T(8,128)(2,1)S(1)} %get-tuple-element.65), channel_id=1, source_target_pairs={{0,7},{1,2},{2,1},{3,4},{4,3},{5,6},{6,5},{7,0},{8,15},{9,10},{10,... | collective-permute-start | bytes 135176 | tf_op jit(solution)/shard_map/ppermute | solution.py:918
  19.1 0.5 %shard_map.130.refs_8_ = f32[4,8,128]{2,1,0:T(8,128)S(1)} custom-call(s32[2,729]{1,0:T(2,128)S(1)} %get-tuple-element.67.refs_0_, s32[1,81]{1,0:T(1,128)S(1)} %get-tuple-element.68.refs_1_, s32[1,8]{1,0:T(1,128)S(1)} %get-tuple-element.69.refs_2_, f32[6,128]{1,0:T(8,128)S(1)} %get-tuple-element.70.refs_3_, f32[768,128]{1,0:T(8,128)S(1)} %shard_map.127.refs_0_.refs_4_), custom_call_target="tpu_custom_call" | custom-call | bytes 3000000 | tf_op jit(solution)/shard_map/pallas_call | solution.py:597
  19.6 0.5 %shard_map.129.refs_0_ = f32[768,128]{1,0:T(8,128)S(1)} custom-call(f32[768,128]{1,0:T(8,128)S(1)} %get-tuple-element.63.refs_0_, f32[768,128]{1,0:T(8,128)S(1)} %get-tuple-element.58.refs_0_.refs_1_, f32[768,128]{1,0:T(8,128)S(1)} %get-tuple-element.47.refs_1_.refs_2_, bf16[352,352]{1,0:T(8,128)(2,1)S(1)} %get-tuple-element.48.refs_2_.refs_3_.refs_4_, ...), custom_call_target="tpu_custom_call" | custom-call | bytes 6000000 | tf_op jit(solution)/shard_map/pallas_call | solution.py:327
  20.1 0.0 collective-permute-done.4.refs_1_
  20.1 2.0 %collective-permute-done.5.refs_2_ = bf16[176,128]{1,0:T(8,128)(2,1)S(1)} collective-permute-done((bf16[176,128]{1,0:T(8,128)(2,1)S(1)}, bf16[176,128]{1,0:T(8,128)(2,1)S(1)}, u32[]{:S(2)}, u32[]{:S(2)}) %collective-permute-start.5) | collective-permute-done | bytes 45088 | tf_op jit(solution)/shard_map/ppermute | solution.py:918
  22.1 1.2 %shard_map.131 = (f32[768,128]{1,0:T(8,128)S(1)}, bf16[176,128]{1,0:T(8,128)(2,1)S(1)}, bf16[176,128]{1,0:T(8,128)(2,1)S(1)}, f32[32,1,1408]{2,1,0:T(1,128)}) custom-call(f32[768,128]{1,0:T(8,128)S(1)} %shard_map.129.refs_0_, bf16[176,128]{1,0:T(8,128)(2,1)S(1)} %collective-permute-done.4.refs_1_, bf16[176,128]{1,0:T(8,128)(2,1)S(1)} %collective-permute-done.5.refs_2_, ...), custom_call_target="tpu_custom_call" | custom-call | bytes 3000000 | tf_op jit(solution)/shard_map/pallas_call | solution.py:492
  23.2 4.5 %all-to-all-start = ((f32[32,1,1408]{2,1,0:T(1,128)}), f32[32,1,1408]{2,1,0:T(1,128)S(1)}, u32[]{:S(2)}, u32[]{:S(2)}) async-start(f32[32,1,1408]{2,1,0:T(1,128)} %get-tuple-element.71), calls=%async_computation | async-start | bytes 360448 | tf_op jit(solution)/shard_map/all_to_all | solution.py:889
  27.8 0.3 collective-permute-start.6
  28.1 3.5 %collective-permute-start.7 = (bf16[176,128]{1,0:T(8,128)(2,1)S(1)}, bf16[176,128]{1,0:T(8,128)(2,1)S(1)}, u32[]{:S(2)}, u32[]{:S(2)}) collective-permute-start(bf16[176,128]{1,0:T(8,128)(2,1)S(1)} %get-tuple-element.74), channel_id=1, source_target_pairs={{0,7},{1,2},{2,1},{3,4},{4,3},{5,6},{6,5},{7,0},{8,15},{9,10},{10,... | collective-permute-start | bytes 135176 | tf_op jit(solution)/shard_map/ppermute | solution.py:918
  31.6 0.5 %shard_map.132.base_ref = f32[768,128]{1,0:T(8,128)S(1)} custom-call(f32[768,128]{1,0:T(8,128)S(1)} %get-tuple-element.72.refs_0_.y_ref.refs_1_, f32[768,128]{1,0:T(8,128)S(1)} %get-tuple-element.47.refs_1_.refs_2_, bf16[352,352]{1,0:T(8,128)(2,1)S(1)} %get-tuple-element.48.refs_2_.refs_3_.refs_4_, ...), custom_call_target="tpu_custom_call" | custom-call | bytes 6000000 | tf_op jit(solution)/shard_map/pallas_call | solution.py:327
  32.1 0.0 collective-permute-done.6.near_ref
  32.1 3.7 %collective-permute-done.7.far_ref = bf16[176,128]{1,0:T(8,128)(2,1)S(1)} collective-permute-done((bf16[176,128]{1,0:T(8,128)(2,1)S(1)}, bf16[176,128]{1,0:T(8,128)(2,1)S(1)}, u32[]{:S(2)}, u32[]{:S(2)}) %collective-permute-start.7) | collective-permute-done | bytes 45088 | tf_op jit(solution)/shard_map/ppermute | solution.py:918
  35.8 0.7 %all-to-all-done.got_ref = f32[32,1,1408]{2,1,0:T(1,128)S(1)} async-done(((f32[32,1,1408]{2,1,0:T(1,128)}), f32[32,1,1408]{2,1,0:T(1,128)S(1)}, u32[]{:S(2)}, u32[]{:S(2)}) %all-to-all-start) | async-done | bytes 180256 | tf_op jit(solution)/shard_map/all_to_all | solution.py:889
  36.5 3.7 %shard_map.133 = (f32[768,128]{1,0:T(8,128)S(1)}, bf16[176,128]{1,0:T(8,128)(2,1)S(1)}, bf16[176,128]{1,0:T(8,128)(2,1)S(1)}, f32[768,128]{1,0:T(8,128)S(1)}, f32[6,128]{1,0:T(8,128)S(1)}) custom-call(f32[32,1,1408]{2,1,0:T(1,128)S(1)} %all-to-all-done.got_ref, f32[729,729]{1,0:T(8,128)} %matrix_hbm.1, f32[768,128]{1,0:T(8,128)S(1)} %shard_map.132.base_ref, ...), custom_call_target="tpu_custom_call" | custom-call | bytes 12000000 | tf_op jit(solution)/shard_map/pallas_call | solution.py:756
  40.2 1.1 %collective-permute-start.8 = (bf16[176,128]{1,0:T(8,128)(2,1)S(1)}, bf16[176,128]{1,0:T(8,128)(2,1)S(1)}, u32[]{:S(2)}, u32[]{:S(2)}) collective-permute-start(bf16[176,128]{1,0:T(8,128)(2,1)S(1)} %get-tuple-element.77), channel_id=1, source_target_pairs={{0,1},{1,0},{2,3},{3,2},{4,5},{5,4},{6,7},{7,6},{8,9},{9,8},{10,11... | collective-permute-start | bytes 135176 | tf_op jit(solution)/shard_map/ppermute | solution.py:919
  41.3 0.4 collective-permute-start.9
  41.7 0.5 %shard_map.134.refs_0_ = f32[768,128]{1,0:T(8,128)S(1)} custom-call(f32[768,128]{1,0:T(8,128)S(1)} %get-tuple-element.75.refs_0_, f32[768,128]{1,0:T(8,128)S(1)} %get-tuple-element.72.refs_0_.y_ref.refs_1_, f32[768,128]{1,0:T(8,128)S(1)} %get-tuple-element.47.refs_1_.refs_2_, f32[768,128]{1,0:T(8,128)S(1)} %get-tuple-element.76.refs_3_, ...), custom_call_target="tpu_custom_call" | custom-call | bytes 6000000 | tf_op jit(solution)/shard_map/pallas_call | solution.py:327
  42.2 0.0 collective-permute-done.8.refs_1_
  42.2 4.4 %collective-permute-done.9.refs_2_ = bf16[176,128]{1,0:T(8,128)(2,1)S(1)} collective-permute-done((bf16[176,128]{1,0:T(8,128)(2,1)S(1)}, bf16[176,128]{1,0:T(8,128)(2,1)S(1)}, u32[]{:S(2)}, u32[]{:S(2)}) %collective-permute-start.9) | collective-permute-done | bytes 45088 | tf_op jit(solution)/shard_map/ppermute | solution.py:918
  46.6 1.0 %shard_map.135 = (f32[768,128]{1,0:T(8,128)}, f32[6,128]{1,0:T(8,128)}) custom-call(f32[768,128]{1,0:T(8,128)S(1)} %shard_map.134.refs_0_, bf16[176,128]{1,0:T(8,128)(2,1)S(1)} %collective-permute-done.8.refs_1_, bf16[176,128]{1,0:T(8,128)(2,1)S(1)} %collective-permute-done.9.refs_2_, bf16[304,176]{1,0:T(8,128)(2,1)S(1)} %get-tuple-element.54.refs_2_.refs_3_.refs_0_, ...), custom_call_target="tpu_custom_call" | custom-call | bytes 3000000 | tf_op jit(solution)/shard_map/pallas_call | solution.py:492
Async XLA Ops:
  1.9 7.3 %collective-permute-start = (bf16[464,128]{1,0:T(8,128)(2,1)S(1)}, bf16[464,128]{1,0:T(8,128)(2,1)S(1)}, u32[]{:S(2)}, u32[]{:S(2)}) collective-permute-start(bf16[464,128]{1,0:T(8,128)(2,1)S(1)} %get-tuple-element.42), channel_id=1, source_target_pairs={{0,1},{1,2},{2,3},{3,4},{4,5},{5,6},{6,7},{7,0},{8,9},{9,10},{10,1... | collective-permute-start | bytes 356360 | tf_op jit(solution)/shard_map/ppermute | solution.py:32
  2.5 7.8 %collective-permute-start.1 = (bf16[176,128]{1,0:T(8,128)(2,1)S(1)}, bf16[176,128]{1,0:T(8,128)(2,1)S(1)}, u32[]{:S(2)}, u32[]{:S(2)}) collective-permute-start(bf16[176,128]{1,0:T(8,128)(2,1)S(1)} %get-tuple-element.52.own_up_ref), channel_id=1, source_target_pairs={{0,7},{1,0},{2,1},{3,2},{4,3},{5,4},{6,5},{7,6},{8,15},{9,8},{10,9... | collective-permute-start | bytes 135176 | tf_op jit(solution)/shard_map/ppermute | solution.py:32
  10.8 2.9 %collective-permute-start.2 = (bf16[176,128]{1,0:T(8,128)(2,1)S(1)}, bf16[176,128]{1,0:T(8,128)(2,1)S(1)}, u32[]{:S(2)}, u32[]{:S(2)}) collective-permute-start(bf16[176,128]{1,0:T(8,128)(2,1)S(1)} %get-tuple-element.61), channel_id=1, source_target_pairs={{0,1},{1,0},{2,3},{3,2},{4,5},{5,4},{6,7},{7,6},{8,9},{9,8},{10,11... | collective-permute-start | bytes 135176 | tf_op jit(solution)/shard_map/ppermute | solution.py:919
  10.8 5.3 %collective-permute-start.3 = (bf16[176,128]{1,0:T(8,128)(2,1)S(1)}, bf16[176,128]{1,0:T(8,128)(2,1)S(1)}, u32[]{:S(2)}, u32[]{:S(2)}) collective-permute-start(bf16[176,128]{1,0:T(8,128)(2,1)S(1)} %get-tuple-element.62), channel_id=1, source_target_pairs={{0,7},{1,2},{2,1},{3,4},{4,3},{5,6},{6,5},{7,0},{8,15},{9,10},{10,... | collective-permute-start | bytes 135176 | tf_op jit(solution)/shard_map/ppermute | solution.py:918
  16.6 3.5 %collective-permute-start.4 = (bf16[176,128]{1,0:T(8,128)(2,1)S(1)}, bf16[176,128]{1,0:T(8,128)(2,1)S(1)}, u32[]{:S(2)}, u32[]{:S(2)}) collective-permute-start(bf16[176,128]{1,0:T(8,128)(2,1)S(1)} %get-tuple-element.64), channel_id=1, source_target_pairs={{0,1},{1,0},{2,3},{3,2},{4,5},{5,4},{6,7},{7,6},{8,9},{9,8},{10,11... | collective-permute-start | bytes 135176 | tf_op jit(solution)/shard_map/ppermute | solution.py:919
  16.7 5.3 %collective-permute-start.5 = (bf16[176,128]{1,0:T(8,128)(2,1)S(1)}, bf16[176,128]{1,0:T(8,128)(2,1)S(1)}, u32[]{:S(2)}, u32[]{:S(2)}) collective-permute-start(bf16[176,128]{1,0:T(8,128)(2,1)S(1)} %get-tuple-element.65), channel_id=1, source_target_pairs={{0,7},{1,2},{2,1},{3,4},{4,3},{5,6},{6,5},{7,0},{8,15},{9,10},{10,... | collective-permute-start | bytes 135176 | tf_op jit(solution)/shard_map/ppermute | solution.py:918
  23.2 13.2 %all-to-all-start = ((f32[32,1,1408]{2,1,0:T(1,128)}), f32[32,1,1408]{2,1,0:T(1,128)S(1)}, u32[]{:S(2)}, u32[]{:S(2)}) async-start(f32[32,1,1408]{2,1,0:T(1,128)} %get-tuple-element.71), calls=%async_computation | async-start | bytes 360448 | tf_op jit(solution)/shard_map/all_to_all | solution.py:889
  27.8 4.3 %collective-permute-start.6 = (bf16[176,128]{1,0:T(8,128)(2,1)S(1)}, bf16[176,128]{1,0:T(8,128)(2,1)S(1)}, u32[]{:S(2)}, u32[]{:S(2)}) collective-permute-start(bf16[176,128]{1,0:T(8,128)(2,1)S(1)} %get-tuple-element.73), channel_id=1, source_target_pairs={{0,1},{1,0},{2,3},{3,2},{4,5},{5,4},{6,7},{7,6},{8,9},{9,8},{10,11... | collective-permute-start | bytes 135176 | tf_op jit(solution)/shard_map/ppermute | solution.py:919
  28.1 7.7 %collective-permute-start.7 = (bf16[176,128]{1,0:T(8,128)(2,1)S(1)}, bf16[176,128]{1,0:T(8,128)(2,1)S(1)}, u32[]{:S(2)}, u32[]{:S(2)}) collective-permute-start(bf16[176,128]{1,0:T(8,128)(2,1)S(1)} %get-tuple-element.74), channel_id=1, source_target_pairs={{0,7},{1,2},{2,1},{3,4},{4,3},{5,6},{6,5},{7,0},{8,15},{9,10},{10,... | collective-permute-start | bytes 135176 | tf_op jit(solution)/shard_map/ppermute | solution.py:918
  40.2 2.0 %collective-permute-start.8 = (bf16[176,128]{1,0:T(8,128)(2,1)S(1)}, bf16[176,128]{1,0:T(8,128)(2,1)S(1)}, u32[]{:S(2)}, u32[]{:S(2)}) collective-permute-start(bf16[176,128]{1,0:T(8,128)(2,1)S(1)} %get-tuple-element.77), channel_id=1, source_target_pairs={{0,1},{1,0},{2,3},{3,2},{4,5},{5,4},{6,7},{7,6},{8,9},{9,8},{10,11... | collective-permute-start | bytes 135176 | tf_op jit(solution)/shard_map/ppermute | solution.py:919
  41.3 5.3 %collective-permute-start.9 = (bf16[176,128]{1,0:T(8,128)(2,1)S(1)}, bf16[176,128]{1,0:T(8,128)(2,1)S(1)}, u32[]{:S(2)}, u32[]{:S(2)}) collective-permute-start(bf16[176,128]{1,0:T(8,128)(2,1)S(1)} %get-tuple-element.78), channel_id=1, source_target_pairs={{0,7},{1,2},{2,1},{3,4},{4,3},{5,6},{6,5},{7,0},{8,15},{9,10},{10,... | collective-permute-start | bytes 135176 | tf_op jit(solution)/shard_map/ppermute | solution.py:918

commit v3 on v2

--- a/solution.py
+++ b/solution.py
@@ -612,13 +612,16 @@
     return jnp.take_along_axis(values, index, axis=1, mode="promise_in_bounds")
 
 
+def got_tile(fg, got_ref, band, line):
+    lines = fg.width // LANES
+    return got_ref[pl.ds(band * fg.domains * lines + line, fg.domains, stride=lines), :]
+
+
 def decode(fg, got_ref, codes):
-    domains, half, own = fg.domains, fg.at_screen, fg.own
+    domains, half = fg.domains, fg.at_screen
 
     def tile(at):
-        band, row = at // fg.part_rows, at % fg.part_rows
-        first = own + row * LANES
-        return got_ref[band * domains : (band + 1) * domains, 0, first : first + LANES]
+        return got_tile(fg, got_ref, at // fg.part_rows, fg.lines + at % fg.part_rows)
 
     for at in range(half):
         both = tile(at).astype(I32)
@@ -658,10 +661,9 @@
     domains = fg.domains
     density = []
     for g in range(fg.lines):
-        at = slice(g * LANES, (g + 1) * LANES)
-        total = got_ref[0:domains, 0, at]
+        total = got_tile(fg, got_ref, 0, g)
         for b in range(1, fg.bands):
-            total = total + got_ref[b * domains : (b + 1) * domains, 0, at]
+            total = total + got_tile(fg, got_ref, b, g)
         density.append(total)
     lane = lax.broadcasted_iota(I32, (domains, LANES), 1)
     source = [None] * fg.lines
@@ -677,7 +679,7 @@
     return source
 
 
-def field_solve(fg, source, codes, screen, matrix_ref, weight_ref, rows, copies):
+def field_solve(fg, source, codes, screen, matrix_ref, high_ref, low_ref, rows, copies):
     domains, cells = fg.domains, fg.cells
 
     def operator(field):
@@ -690,13 +692,16 @@
             if copies:
                 copies.pop(0).wait()
                 span = slice(r * LANES, min((r + 1) * LANES, fg.npc))
-                weight_ref[span, :] = matrix_ref[span, :].astype(BF)
+                full = matrix_ref[span, :]
+                top = full.astype(BF)
+                high_ref[span, :] = top
+                low_ref[span, :] = (full - top.astype(F32)).astype(BF)
         picked = rows[:, 0 : fg.npc]
         high = picked.astype(BF)
         low = (picked - high.astype(F32)).astype(BF)
-        both = dot(jnp.concatenate([high, low], axis=0), weight_ref[...])
+        both = dot(jnp.concatenate([high, low], axis=0), high_ref[...])
         half_rows = cells * domains
-        rows[:, 0 : fg.npc] = both[:half_rows] + both[half_rows:]
+        rows[:, 0 : fg.npc] = both[:half_rows] + (both[half_rows:] + dot(high, low_ref[...]))
         out = [None] * fg.tiles
         for c in range(cells):
             sources = [
@@ -726,14 +731,14 @@
     n = len(geo.touching)
     crosses, reaches, refs = refs[:n], refs[n : 2 * n], refs[2 * n :]
     z_ref, near_out, far_out, column_ref, hartree_ref = refs[:5]
-    codes, rows, mine, matrix_ref, weight_ref, sems = refs[5:]
+    codes, rows, mine, matrix_ref, high_ref, low_ref, sems = refs[5:]
     spans = [pl.ds(r * LANES, min(LANES, fg.npc - r * LANES)) for r in range(fg.rows)]
     copies = fetch([(matrix_hbm.at[span], matrix_ref.at[span]) for span in spans], sems)
     z_ref[...] = base_ref[...]
     add_halo(geo, scale, z_ref, near_ref, far_ref, crosses)
     places, owner, screens = decode(fg, got_ref, codes)
     source = field_source(fg, got_ref, places)
-    solved = field_solve(fg, source, codes, screens, matrix_ref, weight_ref, rows, copies)
+    solved = field_solve(fg, source, codes, screens, matrix_ref, high_ref, low_ref, rows, copies)
     lane = lax.broadcasted_iota(I32, (fg.domains, LANES), 1)
     block = lookup(list(enumerate(solved)), lane + lax.axis_index("domain") * fg.block)
     mine[...] = rows_of(block, owner)
@@ -750,6 +755,7 @@
 def field_step(geo, fg, scale, got, matrix, base, halo, y, crosses, reaches):
     tile = (fg.domains, LANES)
     vmem = pl.BlockSpec(memory_space=pltpu.VMEM)
+    got = got.reshape(got.shape[0] * fg.width // LANES, LANES)
     args = [got, *in_hbm(matrix), base, *halo, y, *crosses, *reaches]
     specs = [vmem] * len(args)
     specs[1] = pl.BlockSpec(memory_space=pltpu.HBM)
@@ -766,6 +772,7 @@
             pltpu.VMEM((fg.cells * fg.domains, fg.size), F32),
             pltpu.VMEM(tile, F32),
             pltpu.VMEM(matrix.shape, F32),
+            pltpu.VMEM(matrix.shape, BF),
             pltpu.VMEM(matrix.shape, BF),
             pltpu.SemaphoreType.DMA((fg.rows,)),
         ],

time: 47.8 us -> 47.9 us (level)
  no operation moved by 1% of the time
where the time goes in v3:
time: 47.9 us; the launch traced here: 47.7 us
  starting transfers between devices  19.3 us (40%)
  Pallas kernels  14.4 us (30%)
  waiting for transfers between devices  13.2 us (28%)
  between operations  0.8 us (2%)
    ppermute x4, waiting for transfers between devices, swap(): far = lax.ppermute(far, 'domain', turns)  12.5 us
    ppermute x4, starting transfers between devices, swap(): far = lax.ppermute(far, 'domain', turns)  8.54 us
    ppermute x2, starting transfers between devices, from_behind(): lax.ppermute(array, axis, [(i, (i + by) % length) for i in range(length)])  4.64 us
    all_to_all x1, starting transfers between devices, on_device(): dens = lax.all_to_all(spread, ('band', 'domain'), 0, 0, tiled=True)  4.53 us
    pallas_call x1, Pallas kernels, field_step(): vmem_call(functools.partial(field_kernel, geo, fg, scale), [sds(y.shape,...  3.83 us
    pallas_call x3, Pallas kernels, finish(): vmem_call(functools.partial(finish_kernel, geo, scale, mode, part_rows),...  2.61 us
    pallas_call x5, Pallas kernels, owned_part(): vmem_call(functools.partial(owned_part_kernel, geo, scale, prev is not No...  2.42 us
    pallas_call x1, Pallas kernels, own_matrices(): vmem_call(functools.partial(own_matrices_kernel, geo), shapes, [matrix_sc...  2.25 us
  transfers between devices with their start and end apart: 11, of which 5 were waited for; matrix products, arithmetic and copies ran while one was open for 0% of the time, Pallas kernels for 13%

profile of v3, /device:TPU:0, one launch (start us, length us, event | category | flops | bytes accessed | tf_op | source)
XLA Modules:
  0.0 47.7 jit_solution(6136838164824703069)
XLA Ops:
  0.6 1.3 %shard_map.122 = (bf16[464,128]{1,0:T(8,128)(2,1)S(1)}, bf16[176,128]{1,0:T(8,128)(2,1)S(1)}, f32[768,128]{1,0:T(8,128)S(1)}, s32[8,384]{1,0:T(8,128)S(1)}, bf16...) custom-call(f32[768,128]{1,0:T(8,128)} %y_hbm.1, ...), custom_call_target="tpu_custom_call" | custom-call | bytes 3000000 | tf_op jit(solution)/shard_map/pallas_call | solution.py:270
  1.9 0.5 %collective-permute-start = (bf16[464,128]{1,0:T(8,128)(2,1)S(1)}, bf16[464,128]{1,0:T(8,128)(2,1)S(1)}, u32[]{:S(2)}, u32[]{:S(2)}) collective-permute-start(bf16[464,128]{1,0:T(8,128)(2,1)S(1)} %get-tuple-element.42), channel_id=1, source_target_pairs={{0,1},{1,2},{2,3},{3,4},{4,5},{5,6},{6,7},{7,0},{8,9},{9,10},{10,1... | collective-permute-start | bytes 356360 | tf_op jit(solution)/shard_map/ppermute | solution.py:32
  2.5 4.1 %collective-permute-start.1 = (bf16[176,128]{1,0:T(8,128)(2,1)S(1)}, bf16[176,128]{1,0:T(8,128)(2,1)S(1)}, u32[]{:S(2)}, u32[]{:S(2)}) collective-permute-start(bf16[176,128]{1,0:T(8,128)(2,1)S(1)} %get-tuple-element.52.own_up_ref), channel_id=1, source_target_pairs={{0,7},{1,0},{2,1},{3,2},{4,3},{5,4},{6,5},{7,6},{8,15},{9,8},{10,9... | collective-permute-start | bytes 135176 | tf_op jit(solution)/shard_map/ppermute | solution.py:32
  6.6 2.3 %shard_map.123 = (bf16[352,352]{1,0:T(8,128)(2,1)S(1)}, bf16[368,368]{1,0:T(8,128)(2,1)S(1)}, bf16[304,304]{1,0:T(8,128)(2,1)S(1)}, bf16[192,192]{1,0:T(8,128)(2...) custom-call(s32[8,384]{1,0:T(8,128)S(1)} %get-tuple-element.45.refs_, ...), custom_call_target="tpu_custom_call" | custom-call | bytes 6000000 | tf_op jit(solution)/shard_map/pallas_call | solution.py:172
  8.8 0.4 shard_map.124.base_ref
  9.3 0.0 collective-permute-done.sent_ref
  9.3 1.0 %shard_map.125 = (bf16[176,176]{1,0:T(8,128)(2,1)S(1)}, bf16[176,176]{1,0:T(8,128)(2,1)S(1)}, f32[768,128]{1,0:T(8,128)S(1)}) custom-call(bf16[464,128]{1,0:T(8,128)(2,1)S(1)} %collective-permute-done.sent_ref, bf16[343,343]{1,0:T(8,128)(2,1)S(1)} %get-tuple-element.43.refs_1_.matrix_ref, f32[768,128]{1,0:T(8,128)S(1)} %shard_map.124.base_ref, ...), custom_call_target="tpu_custom_call" | custom-call | bytes 3000000 | tf_op jit(solution)/shard_map/pallas_call | solution.py:389
  10.3 0.0 collective-permute-done.1.refs_1_
  10.3 0.5 shard_map.126
  10.8 0.1 collective-permute-start.2
  10.8 2.3 %collective-permute-start.3 = (bf16[176,128]{1,0:T(8,128)(2,1)S(1)}, bf16[176,128]{1,0:T(8,128)(2,1)S(1)}, u32[]{:S(2)}, u32[]{:S(2)}) collective-permute-start(bf16[176,128]{1,0:T(8,128)(2,1)S(1)} %get-tuple-element.62), channel_id=1, source_target_pairs={{0,7},{1,2},{2,1},{3,4},{4,3},{5,6},{6,5},{7,0},{8,15},{9,10},{10,... | collective-permute-start | bytes 135176 | tf_op jit(solution)/shard_map/ppermute | solution.py:925
  13.2 0.5 %shard_map.127.refs_0_.refs_4_ = f32[768,128]{1,0:T(8,128)S(1)} custom-call(f32[768,128]{1,0:T(8,128)S(1)} %get-tuple-element.58.refs_0_.refs_1_, f32[768,128]{1,0:T(8,128)S(1)} %get-tuple-element.44.refs_0_.refs_1_, f32[768,128]{1,0:T(8,128)S(1)} %get-tuple-element.47.refs_1_.refs_2_, bf16[352,352]{1,0:T(8,128)(2,1)S(1)} %get-tuple-element.48.refs_2_.refs_3_.refs_4_, ...), custom_call_target="tpu_custom_call" | custom-call | bytes 6000000 | tf_op jit(solution)/shard_map/pallas_call | solution.py:327
  13.7 0.0 collective-permute-done.2.refs_1_
  13.7 2.5 %collective-permute-done.3.refs_2_ = bf16[176,128]{1,0:T(8,128)(2,1)S(1)} collective-permute-done((bf16[176,128]{1,0:T(8,128)(2,1)S(1)}, bf16[176,128]{1,0:T(8,128)(2,1)S(1)}, u32[]{:S(2)}, u32[]{:S(2)}) %collective-permute-start.3) | collective-permute-done | bytes 45088 | tf_op jit(solution)/shard_map/ppermute | solution.py:925
  16.2 0.5 shard_map.128
  16.6 0.1 collective-permute-start.4
  16.7 2.3 %collective-permute-start.5 = (bf16[176,128]{1,0:T(8,128)(2,1)S(1)}, bf16[176,128]{1,0:T(8,128)(2,1)S(1)}, u32[]{:S(2)}, u32[]{:S(2)}) collective-permute-start(bf16[176,128]{1,0:T(8,128)(2,1)S(1)} %get-tuple-element.65), channel_id=1, source_target_pairs={{0,7},{1,2},{2,1},{3,4},{4,3},{5,6},{6,5},{7,0},{8,15},{9,10},{10,... | collective-permute-start | bytes 135176 | tf_op jit(solution)/shard_map/ppermute | solution.py:925
  19.1 0.5 %shard_map.130.refs_8_ = f32[4,8,128]{2,1,0:T(8,128)S(1)} custom-call(s32[2,729]{1,0:T(2,128)S(1)} %get-tuple-element.67.refs_0_, s32[1,81]{1,0:T(1,128)S(1)} %get-tuple-element.68.refs_1_, s32[1,8]{1,0:T(1,128)S(1)} %get-tuple-element.69.refs_2_, f32[6,128]{1,0:T(8,128)S(1)} %get-tuple-element.70.refs_3_, f32[768,128]{1,0:T(8,128)S(1)} %shard_map.127.refs_0_.refs_4_), custom_call_target="tpu_custom_call" | custom-call | bytes 3000000 | tf_op jit(solution)/shard_map/pallas_call | solution.py:597
  19.6 0.5 %shard_map.129.refs_0_ = f32[768,128]{1,0:T(8,128)S(1)} custom-call(f32[768,128]{1,0:T(8,128)S(1)} %get-tuple-element.63.refs_0_, f32[768,128]{1,0:T(8,128)S(1)} %get-tuple-element.58.refs_0_.refs_1_, f32[768,128]{1,0:T(8,128)S(1)} %get-tuple-element.47.refs_1_.refs_2_, bf16[352,352]{1,0:T(8,128)(2,1)S(1)} %get-tuple-element.48.refs_2_.refs_3_.refs_4_, ...), custom_call_target="tpu_custom_call" | custom-call | bytes 6000000 | tf_op jit(solution)/shard_map/pallas_call | solution.py:327
  20.1 0.0 collective-permute-done.4.refs_1_
  20.1 2.0 %collective-permute-done.5.refs_2_ = bf16[176,128]{1,0:T(8,128)(2,1)S(1)} collective-permute-done((bf16[176,128]{1,0:T(8,128)(2,1)S(1)}, bf16[176,128]{1,0:T(8,128)(2,1)S(1)}, u32[]{:S(2)}, u32[]{:S(2)}) %collective-permute-start.5) | collective-permute-done | bytes 45088 | tf_op jit(solution)/shard_map/ppermute | solution.py:925
  22.1 1.2 %shard_map.131 = (f32[768,128]{1,0:T(8,128)S(1)}, bf16[176,128]{1,0:T(8,128)(2,1)S(1)}, bf16[176,128]{1,0:T(8,128)(2,1)S(1)}, f32[32,1,1408]{2,1,0:T(1,128)}) custom-call(f32[768,128]{1,0:T(8,128)S(1)} %shard_map.129.refs_0_, bf16[176,128]{1,0:T(8,128)(2,1)S(1)} %collective-permute-done.4.refs_1_, bf16[176,128]{1,0:T(8,128)(2,1)S(1)} %collective-permute-done.5.refs_2_, ...), custom_call_target="tpu_custom_call" | custom-call | bytes 3000000 | tf_op jit(solution)/shard_map/pallas_call | solution.py:492
  23.2 4.5 %all-to-all-start = ((f32[32,1,1408]{2,1,0:T(1,128)}), f32[32,1,1408]{2,1,0:T(1,128)S(1)}, u32[]{:S(2)}, u32[]{:S(2)}) async-start(f32[32,1,1408]{2,1,0:T(1,128)} %get-tuple-element.71), calls=%async_computation | async-start | bytes 360448 | tf_op jit(solution)/shard_map/all_to_all | solution.py:896
  27.8 0.3 collective-permute-start.6
  28.1 3.5 %collective-permute-start.7 = (bf16[176,128]{1,0:T(8,128)(2,1)S(1)}, bf16[176,128]{1,0:T(8,128)(2,1)S(1)}, u32[]{:S(2)}, u32[]{:S(2)}) collective-permute-start(bf16[176,128]{1,0:T(8,128)(2,1)S(1)} %get-tuple-element.74), channel_id=1, source_target_pairs={{0,7},{1,2},{2,1},{3,4},{4,3},{5,6},{6,5},{7,0},{8,15},{9,10},{10,... | collective-permute-start | bytes 135176 | tf_op jit(solution)/shard_map/ppermute | solution.py:925
  31.6 0.5 %shard_map.132.base_ref = f32[768,128]{1,0:T(8,128)S(1)} custom-call(f32[768,128]{1,0:T(8,128)S(1)} %get-tuple-element.72.refs_0_.y_ref.refs_1_, f32[768,128]{1,0:T(8,128)S(1)} %get-tuple-element.47.refs_1_.refs_2_, bf16[352,352]{1,0:T(8,128)(2,1)S(1)} %get-tuple-element.48.refs_2_.refs_3_.refs_4_, ...), custom_call_target="tpu_custom_call" | custom-call | bytes 6000000 | tf_op jit(solution)/shard_map/pallas_call | solution.py:327
  32.1 0.0 collective-permute-done.6.near_ref
  32.1 3.7 %collective-permute-done.7.far_ref = bf16[176,128]{1,0:T(8,128)(2,1)S(1)} collective-permute-done((bf16[176,128]{1,0:T(8,128)(2,1)S(1)}, bf16[176,128]{1,0:T(8,128)(2,1)S(1)}, u32[]{:S(2)}, u32[]{:S(2)}) %collective-permute-start.7) | collective-permute-done | bytes 45088 | tf_op jit(solution)/shard_map/ppermute | solution.py:925
  35.8 0.7 %all-to-all-done = f32[32,1,1408]{2,1,0:T(1,128)S(1)} async-done(((f32[32,1,1408]{2,1,0:T(1,128)}), f32[32,1,1408]{2,1,0:T(1,128)S(1)}, u32[]{:S(2)}, u32[]{:S(2)}) %all-to-all-start) | async-done | bytes 180256 | tf_op jit(solution)/shard_map/all_to_all | solution.py:896
  36.5 3.8 %shard_map.133 = (f32[768,128]{1,0:T(8,128)S(1)}, bf16[176,128]{1,0:T(8,128)(2,1)S(1)}, bf16[176,128]{1,0:T(8,128)(2,1)S(1)}, f32[768,128]{1,0:T(8,128)S(1)}, f32[6,128]{1,0:T(8,128)S(1)}) custom-call(f32[352,128]{1,0:T(8,128)S(1)} %bitcast.5, f32[729,729]{1,0:T(8,128)} %matrix_hbm.1, f32[768,128]{1,0:T(8,128)S(1)} %shard_map.132.base_ref, ...), custom_call_target="tpu_custom_call" | custom-call | bytes 12000000 | tf_op jit(solution)/shard_map/pallas_call | solution.py:762
  40.3 1.1 %collective-permute-start.8 = (bf16[176,128]{1,0:T(8,128)(2,1)S(1)}, bf16[176,128]{1,0:T(8,128)(2,1)S(1)}, u32[]{:S(2)}, u32[]{:S(2)}) collective-permute-start(bf16[176,128]{1,0:T(8,128)(2,1)S(1)} %get-tuple-element.77), channel_id=1, source_target_pairs={{0,1},{1,0},{2,3},{3,2},{4,5},{5,4},{6,7},{7,6},{8,9},{9,8},{10,11... | collective-permute-start | bytes 135176 | tf_op jit(solution)/shard_map/ppermute | solution.py:926
  41.4 0.4 collective-permute-start.9
  41.8 0.5 %shard_map.134.refs_0_ = f32[768,128]{1,0:T(8,128)S(1)} custom-call(f32[768,128]{1,0:T(8,128)S(1)} %get-tuple-element.75.refs_0_, f32[768,128]{1,0:T(8,128)S(1)} %get-tuple-element.72.refs_0_.y_ref.refs_1_, f32[768,128]{1,0:T(8,128)S(1)} %get-tuple-element.47.refs_1_.refs_2_, f32[768,128]{1,0:T(8,128)S(1)} %get-tuple-element.76.refs_3_, ...), custom_call_target="tpu_custom_call" | custom-call | bytes 6000000 | tf_op jit(solution)/shard_map/pallas_call | solution.py:327
  42.3 0.0 collective-permute-done.8.refs_1_
  42.3 4.4 %collective-permute-done.9.refs_2_ = bf16[176,128]{1,0:T(8,128)(2,1)S(1)} collective-permute-done((bf16[176,128]{1,0:T(8,128)(2,1)S(1)}, bf16[176,128]{1,0:T(8,128)(2,1)S(1)}, u32[]{:S(2)}, u32[]{:S(2)}) %collective-permute-start.9) | collective-permute-done | bytes 45088 | tf_op jit(solution)/shard_map/ppermute | solution.py:925
  46.7 1.0 %shard_map.135 = (f32[768,128]{1,0:T(8,128)}, f32[6,128]{1,0:T(8,128)}) custom-call(f32[768,128]{1,0:T(8,128)S(1)} %shard_map.134.refs_0_, bf16[176,128]{1,0:T(8,128)(2,1)S(1)} %collective-permute-done.8.refs_1_, bf16[176,128]{1,0:T(8,128)(2,1)S(1)} %collective-permute-done.9.refs_2_, bf16[304,176]{1,0:T(8,128)(2,1)S(1)} %get-tuple-element.54.refs_2_.refs_3_.refs_0_, ...), custom_call_target="tpu_custom_call" | custom-call | bytes 3000000 | tf_op jit(solution)/shard_map/pallas_call | solution.py:492
Async XLA Ops:
  1.9 7.3 %collective-permute-start = (bf16[464,128]{1,0:T(8,128)(2,1)S(1)}, bf16[464,128]{1,0:T(8,128)(2,1)S(1)}, u32[]{:S(2)}, u32[]{:S(2)}) collective-permute-start(bf16[464,128]{1,0:T(8,128)(2,1)S(1)} %get-tuple-element.42), channel_id=1, source_target_pairs={{0,1},{1,2},{2,3},{3,4},{4,5},{5,6},{6,7},{7,0},{8,9},{9,10},{10,1... | collective-permute-start | bytes 356360 | tf_op jit(solution)/shard_map/ppermute | solution.py:32
  2.5 7.8 %collective-permute-start.1 = (bf16[176,128]{1,0:T(8,128)(2,1)S(1)}, bf16[176,128]{1,0:T(8,128)(2,1)S(1)}, u32[]{:S(2)}, u32[]{:S(2)}) collective-permute-start(bf16[176,128]{1,0:T(8,128)(2,1)S(1)} %get-tuple-element.52.own_up_ref), channel_id=1, source_target_pairs={{0,7},{1,0},{2,1},{3,2},{4,3},{5,4},{6,5},{7,6},{8,15},{9,8},{10,9... | collective-permute-start | bytes 135176 | tf_op jit(solution)/shard_map/ppermute | solution.py:32
  10.8 2.9 %collective-permute-start.2 = (bf16[176,128]{1,0:T(8,128)(2,1)S(1)}, bf16[176,128]{1,0:T(8,128)(2,1)S(1)}, u32[]{:S(2)}, u32[]{:S(2)}) collective-permute-start(bf16[176,128]{1,0:T(8,128)(2,1)S(1)} %get-tuple-element.61), channel_id=1, source_target_pairs={{0,1},{1,0},{2,3},{3,2},{4,5},{5,4},{6,7},{7,6},{8,9},{9,8},{10,11... | collective-permute-start | bytes 135176 | tf_op jit(solution)/shard_map/ppermute | solution.py:926
  10.8 5.3 %collective-permute-start.3 = (bf16[176,128]{1,0:T(8,128)(2,1)S(1)}, bf16[176,128]{1,0:T(8,128)(2,1)S(1)}, u32[]{:S(2)}, u32[]{:S(2)}) collective-permute-start(bf16[176,128]{1,0:T(8,128)(2,1)S(1)} %get-tuple-element.62), channel_id=1, source_target_pairs={{0,7},{1,2},{2,1},{3,4},{4,3},{5,6},{6,5},{7,0},{8,15},{9,10},{10,... | collective-permute-start | bytes 135176 | tf_op jit(solution)/shard_map/ppermute | solution.py:925
  16.6 3.5 %collective-permute-start.4 = (bf16[176,128]{1,0:T(8,128)(2,1)S(1)}, bf16[176,128]{1,0:T(8,128)(2,1)S(1)}, u32[]{:S(2)}, u32[]{:S(2)}) collective-permute-start(bf16[176,128]{1,0:T(8,128)(2,1)S(1)} %get-tuple-element.64), channel_id=1, source_target_pairs={{0,1},{1,0},{2,3},{3,2},{4,5},{5,4},{6,7},{7,6},{8,9},{9,8},{10,11... | collective-permute-start | bytes 135176 | tf_op jit(solution)/shard_map/ppermute | solution.py:926
  16.7 5.3 %collective-permute-start.5 = (bf16[176,128]{1,0:T(8,128)(2,1)S(1)}, bf16[176,128]{1,0:T(8,128)(2,1)S(1)}, u32[]{:S(2)}, u32[]{:S(2)}) collective-permute-start(bf16[176,128]{1,0:T(8,128)(2,1)S(1)} %get-tuple-element.65), channel_id=1, source_target_pairs={{0,7},{1,2},{2,1},{3,4},{4,3},{5,6},{6,5},{7,0},{8,15},{9,10},{10,... | collective-permute-start | bytes 135176 | tf_op jit(solution)/shard_map/ppermute | solution.py:925
  23.2 13.2 %all-to-all-start = ((f32[32,1,1408]{2,1,0:T(1,128)}), f32[32,1,1408]{2,1,0:T(1,128)S(1)}, u32[]{:S(2)}, u32[]{:S(2)}) async-start(f32[32,1,1408]{2,1,0:T(1,128)} %get-tuple-element.71), calls=%async_computation | async-start | bytes 360448 | tf_op jit(solution)/shard_map/all_to_all | solution.py:896
  27.8 4.3 %collective-permute-start.6 = (bf16[176,128]{1,0:T(8,128)(2,1)S(1)}, bf16[176,128]{1,0:T(8,128)(2,1)S(1)}, u32[]{:S(2)}, u32[]{:S(2)}) collective-permute-start(bf16[176,128]{1,0:T(8,128)(2,1)S(1)} %get-tuple-element.73), channel_id=1, source_target_pairs={{0,1},{1,0},{2,3},{3,2},{4,5},{5,4},{6,7},{7,6},{8,9},{9,8},{10,11... | collective-permute-start | bytes 135176 | tf_op jit(solution)/shard_map/ppermute | solution.py:926
  28.1 7.7 %collective-permute-start.7 = (bf16[176,128]{1,0:T(8,128)(2,1)S(1)}, bf16[176,128]{1,0:T(8,128)(2,1)S(1)}, u32[]{:S(2)}, u32[]{:S(2)}) collective-permute-start(bf16[176,128]{1,0:T(8,128)(2,1)S(1)} %get-tuple-element.74), channel_id=1, source_target_pairs={{0,7},{1,2},{2,1},{3,4},{4,3},{5,6},{6,5},{7,0},{8,15},{9,10},{10,... | collective-permute-start | bytes 135176 | tf_op jit(solution)/shard_map/ppermute | solution.py:925
  40.3 2.0 %collective-permute-start.8 = (bf16[176,128]{1,0:T(8,128)(2,1)S(1)}, bf16[176,128]{1,0:T(8,128)(2,1)S(1)}, u32[]{:S(2)}, u32[]{:S(2)}) collective-permute-start(bf16[176,128]{1,0:T(8,128)(2,1)S(1)} %get-tuple-element.77), channel_id=1, source_target_pairs={{0,1},{1,0},{2,3},{3,2},{4,5},{5,4},{6,7},{7,6},{8,9},{9,8},{10,11... | collective-permute-start | bytes 135176 | tf_op jit(solution)/shard_map/ppermute | solution.py:926
  41.4 5.3 %collective-permute-start.9 = (bf16[176,128]{1,0:T(8,128)(2,1)S(1)}, bf16[176,128]{1,0:T(8,128)(2,1)S(1)}, u32[]{:S(2)}, u32[]{:S(2)}) collective-permute-start(bf16[176,128]{1,0:T(8,128)(2,1)S(1)} %get-tuple-element.78), channel_id=1, source_target_pairs={{0,7},{1,2},{2,1},{3,4},{4,3},{5,6},{6,5},{7,0},{8,15},{9,10},{10,... | collective-permute-start | bytes 135176 | tf_op jit(solution)/shard_map/ppermute | solution.py:925

commit v4 on v3

--- a/solution.py
+++ b/solution.py
@@ -288,14 +288,22 @@
     return (dn, up), y, table, others
 
 
-def owned_part_kernel(geo, scale, has_prev, has_field, has_upper, *refs):
+def owned_part_kernel(geo, scale, has_prev, has_field, has_upper, far, *refs):
     refs = list(refs)
+    if far:
+        places, sems = refs[-2 - geo.cells : -1], refs[-1]
+        refs = refs[: -2 - geo.cells]
     base_ref = refs.pop()
     y_ref = refs.pop(0)
     prev_ref = refs.pop(0) if has_prev else None
     pot_ref = refs.pop(0)
     field_ref = refs.pop(0) if has_field else None
     mats = [refs.pop(0) for _ in range(geo.cells)]
+    if far:
+        copies = fetch(list(zip([pot_ref, *mats], places)), sems)
+        pot_ref, mats = places[0], places[1:]
+        for copy in copies:
+            copy.wait()
     y = y_ref[...]
     factor = pot_ref[...]
     if has_field:
@@ -320,15 +328,27 @@
             base_ref[0 : geo.sp, :] += dot(upper[...], x[0 : geo.sp, :]) * scale
 
 
-def owned_part(geo, scale, y, prev, pot, field, mats, uppers):
+def owned_part(geo, scale, y, prev, pot, field, mats, uppers, far=False):
+    vmem, hbm = pl.BlockSpec(memory_space=pltpu.VMEM), pl.BlockSpec(memory_space=pltpu.HBM)
+    place, scratch = vmem, []
+    if far:
+        place = hbm
+        scratch = [pltpu.VMEM(a.shape, a.dtype) for a in [pot, *mats]]
+        scratch.append(pltpu.SemaphoreType.DMA((1 + len(mats),)))
+        pot, *mats = in_hbm(pot, *mats)
     args = [y] + ([prev] if prev is not None else []) + [pot]
     args += [field] if field is not None else []
     args += list(mats) + list(uppers)
+    specs = [vmem] * (2 if prev is not None else 1) + [place]
+    specs += [vmem] * (0 if field is None else 1)
+    specs += [place] * len(mats) + [vmem] * len(uppers)
     return vmem_call(
         functools.partial(
-            owned_part_kernel, geo, scale, prev is not None, field is not None, bool(uppers)
+            owned_part_kernel, geo, scale, prev is not None, field is not None, bool(uppers), far
         ),
         sds(y.shape, F32),
+        scratch,
+        in_specs=specs,
         cost=cost_of(2.0),
     )(*args)
 
@@ -689,18 +709,16 @@
             for c in range(cells):
                 sources = [(t, local[t]) for t in fg.touched[c]]
                 rows[c * domains : (c + 1) * domains, r * LANES : (r + 1) * LANES] = lookup(sources, codes[c * fg.rows + r])
-            if copies:
-                copies.pop(0).wait()
-                span = slice(r * LANES, min((r + 1) * LANES, fg.npc))
-                full = matrix_ref[span, :]
-                top = full.astype(BF)
-                high_ref[span, :] = top
-                low_ref[span, :] = (full - top.astype(F32)).astype(BF)
         picked = rows[:, 0 : fg.npc]
         high = picked.astype(BF)
         low = (picked - high.astype(F32)).astype(BF)
         both = dot(jnp.concatenate([high, low], axis=0), high_ref[...])
         half_rows = cells * domains
+        for r in range(fg.rows if copies else 0):
+            copies.pop(0).wait()
+            span = slice(r * LANES, min((r + 1) * LANES, fg.npc))
+            rest = matrix_ref[span, :] - high_ref[span, :].astype(F32)
+            low_ref[span, :] = rest.astype(BF)
         rows[:, 0 : fg.npc] = both[:half_rows] + (both[half_rows:] + dot(high, low_ref[...]))
         out = [None] * fg.tiles
         for c in range(cells):
@@ -727,11 +745,31 @@
     return [(x + y) + z for x, y, z in zip(step_one, step_two, step_three)]
 
 
-def field_kernel(geo, fg, scale, got_ref, matrix_hbm, base_ref, near_ref, far_ref, y_ref, *refs):
+def field_top_kernel(fg, matrix_hbm, after_ref, top_ref, matrix_ref, sems):
+    del after_ref
+    spans = [pl.ds(r * LANES, min(LANES, fg.npc - r * LANES)) for r in range(fg.rows)]
+    copies = fetch([(matrix_hbm.at[span], matrix_ref.at[span]) for span in spans], sems)
+    for r, copy in enumerate(copies):
+        copy.wait()
+        span = slice(r * LANES, min((r + 1) * LANES, fg.npc))
+        top_ref[span, :] = matrix_ref[span, :].astype(BF)
+
+
+def field_top(fg, matrix, after):
+    return vmem_call(
+        functools.partial(field_top_kernel, fg),
+        sds(matrix.shape, BF),
+        [pltpu.VMEM(matrix.shape, F32), pltpu.SemaphoreType.DMA((fg.rows,))],
+        in_specs=[pl.BlockSpec(memory_space=pltpu.HBM), pl.BlockSpec(memory_space=pl.ANY)],
+        cost=cost_of(1.5),
+    )(*in_hbm(matrix), after)
+
+
+def field_kernel(geo, fg, scale, got_ref, matrix_hbm, high_ref, base_ref, near_ref, far_ref, y_ref, *refs):
     n = len(geo.touching)
     crosses, reaches, refs = refs[:n], refs[n : 2 * n], refs[2 * n :]
     z_ref, near_out, far_out, column_ref, hartree_ref = refs[:5]
-    codes, rows, mine, matrix_ref, high_ref, low_ref, sems = refs[5:]
+    codes, rows, mine, matrix_ref, low_ref, sems = refs[5:]
     spans = [pl.ds(r * LANES, min(LANES, fg.npc - r * LANES)) for r in range(fg.rows)]
     copies = fetch([(matrix_hbm.at[span], matrix_ref.at[span]) for span in spans], sems)
     z_ref[...] = base_ref[...]
@@ -752,11 +790,11 @@
         hartree_ref[row : row + 1, start : start + count] = mine[j : j + 1, offset : offset + count]
 
 
-def field_step(geo, fg, scale, got, matrix, base, halo, y, crosses, reaches):
+def field_step(geo, fg, scale, got, matrix, top, base, halo, y, crosses, reaches):
     tile = (fg.domains, LANES)
     vmem = pl.BlockSpec(memory_space=pltpu.VMEM)
     got = got.reshape(got.shape[0] * fg.width // LANES, LANES)
-    args = [got, *in_hbm(matrix), base, *halo, y, *crosses, *reaches]
+    args = [got, *in_hbm(matrix), top, base, *halo, y, *crosses, *reaches]
     specs = [vmem] * len(args)
     specs[1] = pl.BlockSpec(memory_space=pltpu.HBM)
     z, near, far, column, lines = vmem_call(
@@ -772,7 +810,6 @@
             pltpu.VMEM((fg.cells * fg.domains, fg.size), F32),
             pltpu.VMEM(tile, F32),
             pltpu.VMEM(matrix.shape, F32),
-            pltpu.VMEM(matrix.shape, BF),
             pltpu.VMEM(matrix.shape, BF),
             pltpu.SemaphoreType.DMA((fg.rows,)),
         ],
@@ -896,8 +933,9 @@
         dens = lax.all_to_all(spread, ("band", "domain"), 0, 0, tiled=True)
         halo = swap((dn, up))
         base = owned_part(geo, first, y3, None, pot, None, mats, uppers)
+        top = field_top(fg, pois_matrix, base)
         z1, sends4, column, packed = field_step(
-            geo, fg, first, dens, pois_matrix, base, halo, y3, crosses, reaches
+            geo, fg, first, dens, pois_matrix, top, base, halo, y3, crosses, reaches
         )
     else:
         y3, *sends3 = finish(geo, later, base, halo, crosses, reaches)
@@ -910,7 +948,7 @@
         z1, *sends4 = finish(geo, first, base, halo, crosses, reaches)
 
     halo = swap(sends4)
-    base = owned_part(geo, later, z1, y3, pot, column, mats, uppers)
+    base = owned_part(geo, later, z1, y3, pot, column, mats, uppers, far=fg.fits)
     last = [packed] if fg.fits else []
     filtered, *rest = finish(geo, later, base, halo, crosses, last=last)
     if fg.fits:

time: 47.9 us -> 48.2 us (level)
  Pallas kernels: 14.4 us -> 17.5 us
  waiting for transfers between devices: 13.2 us -> 10.2 us
    ppermute x4, waiting for transfers between devices: 12.5 us -> 9.53 us  [swap(): far = lax.ppermute(far, 'domain', turns)]
    pallas_call x0 -> x1, Pallas kernels: none -> 1.63 us  [field_top(): vmem_call(functools.partial(field_top_kernel, fg), sds(matrix.shape, BF),...]
    pallas_call x5, Pallas kernels: 2.42 us -> 3.72 us  [owned_part(): vmem_call(functools.partial(owned_part_kernel, geo, scale, prev is not No...]
  transfers between devices with their start and end apart: 11 -> 11, of which waited for: 5 -> 5; matrix products, arithmetic and copies ran while one was open for 0% -> 0% of each run, Pallas kernels for 13% -> 19%
where the time goes in v4:
time: 48.2 us; the launch traced here: 47.9 us
  starting transfers between devices  19.3 us (40%)
  Pallas kernels  17.5 us (36%)
  waiting for transfers between devices  10.2 us (21%)
  between operations  0.86 us (2%)
    ppermute x4, waiting for transfers between devices, swap(): far = lax.ppermute(far, 'domain', turns)  9.53 us
    ppermute x4, starting transfers between devices, swap(): far = lax.ppermute(far, 'domain', turns)  8.55 us
    ppermute x2, starting transfers between devices, from_behind(): lax.ppermute(array, axis, [(i, (i + by) % length) for i in range(length)])  4.64 us
    all_to_all x1, starting transfers between devices, on_device(): dens = lax.all_to_all(spread, ('band', 'domain'), 0, 0, tiled=True)  4.52 us
    pallas_call x1, Pallas kernels, field_step(): vmem_call(functools.partial(field_kernel, geo, fg, scale), [sds(y.shape,...  4 us
    pallas_call x5, Pallas kernels, owned_part(): vmem_call(functools.partial(owned_part_kernel, geo, scale, prev is not No...  3.72 us
    pallas_call x3, Pallas kernels, finish(): vmem_call(functools.partial(finish_kernel, geo, scale, mode, part_rows),...  2.61 us
    pallas_call x1, Pallas kernels, own_matrices(): vmem_call(functools.partial(own_matrices_kernel, geo), shapes, [matrix_sc...  2.25 us
  transfers between devices with their start and end apart: 11, of which 5 were waited for; matrix products, arithmetic and copies ran while one was open for 0% of the time, Pallas kernels for 19%

profile of v4, /device:TPU:0, one launch (start us, length us, event | category | flops | bytes accessed | tf_op | source)
XLA Modules:
  0.0 47.9 jit_solution(17513583894113525355)
XLA Ops:
  0.6 1.3 %shard_map.122 = (bf16[464,128]{1,0:T(8,128)(2,1)S(1)}, bf16[176,128]{1,0:T(8,128)(2,1)S(1)}, f32[768,128]{1,0:T(8,128)S(1)}, s32[8,384]{1,0:T(8,128)S(1)}, bf16...) custom-call(f32[768,128]{1,0:T(8,128)} %y_hbm.1, ...), custom_call_target="tpu_custom_call" | custom-call | bytes 3000000 | tf_op jit(solution)/shard_map/pallas_call | solution.py:270
  1.9 0.5 %collective-permute-start = (bf16[464,128]{1,0:T(8,128)(2,1)S(1)}, bf16[464,128]{1,0:T(8,128)(2,1)S(1)}, u32[]{:S(2)}, u32[]{:S(2)}) collective-permute-start(bf16[464,128]{1,0:T(8,128)(2,1)S(1)} %get-tuple-element.42), channel_id=1, source_target_pairs={{0,1},{1,2},{2,3},{3,4},{4,5},{5,6},{6,7},{7,0},{8,9},{9,10},{10,1... | collective-permute-start | bytes 356360 | tf_op jit(solution)/shard_map/ppermute | solution.py:32
  2.5 4.1 %collective-permute-start.1 = (bf16[176,128]{1,0:T(8,128)(2,1)S(1)}, bf16[176,128]{1,0:T(8,128)(2,1)S(1)}, u32[]{:S(2)}, u32[]{:S(2)}) collective-permute-start(bf16[176,128]{1,0:T(8,128)(2,1)S(1)} %get-tuple-element.52.own_up_ref), channel_id=1, source_target_pairs={{0,7},{1,0},{2,1},{3,2},{4,3},{5,4},{6,5},{7,6},{8,15},{9,8},{10,9... | collective-permute-start | bytes 135176 | tf_op jit(solution)/shard_map/ppermute | solution.py:32
  6.6 2.3 %shard_map.123 = (bf16[352,352]{1,0:T(8,128)(2,1)S(1)}, bf16[368,368]{1,0:T(8,128)(2,1)S(1)}, bf16[304,304]{1,0:T(8,128)(2,1)S(1)}, bf16[192,192]{1,0:T(8,128)(2...) custom-call(s32[8,384]{1,0:T(8,128)S(1)} %get-tuple-element.45.refs_, ...), custom_call_target="tpu_custom_call" | custom-call | bytes 6000000 | tf_op jit(solution)/shard_map/pallas_call | solution.py:172
  8.8 0.0 copy-start
  8.9 0.0 copy-start.1
  8.9 0.0 copy-start.2
  8.9 0.0 copy-start.3
  8.9 0.0 copy-start.4
  8.9 0.4 shard_map.124.base_ref
  9.3 0.0 collective-permute-done.sent_ref
  9.4 1.0 %shard_map.125 = (bf16[176,176]{1,0:T(8,128)(2,1)S(1)}, bf16[176,176]{1,0:T(8,128)(2,1)S(1)}, f32[768,128]{1,0:T(8,128)S(1)}) custom-call(bf16[464,128]{1,0:T(8,128)(2,1)S(1)} %collective-permute-done.sent_ref, bf16[343,343]{1,0:T(8,128)(2,1)S(1)} %get-tuple-element.43.refs_1_.matrix_ref, f32[768,128]{1,0:T(8,128)S(1)} %shard_map.124.base_ref, ...), custom_call_target="tpu_custom_call" | custom-call | bytes 3000000 | tf_op jit(solution)/shard_map/pallas_call | solution.py:409
  10.4 0.0 collective-permute-done.1.refs_1_
  10.4 0.5 shard_map.126
  10.8 0.1 collective-permute-start.2
  10.9 2.3 %collective-permute-start.3 = (bf16[176,128]{1,0:T(8,128)(2,1)S(1)}, bf16[176,128]{1,0:T(8,128)(2,1)S(1)}, u32[]{:S(2)}, u32[]{:S(2)}) collective-permute-start(bf16[176,128]{1,0:T(8,128)(2,1)S(1)} %get-tuple-element.62), channel_id=1, source_target_pairs={{0,7},{1,2},{2,1},{3,4},{4,3},{5,6},{6,5},{7,0},{8,15},{9,10},{10,... | collective-permute-start | bytes 135176 | tf_op jit(solution)/shard_map/ppermute | solution.py:963
  13.2 0.5 %shard_map.127.refs_0_.refs_4_ = f32[768,128]{1,0:T(8,128)S(1)} custom-call(f32[768,128]{1,0:T(8,128)S(1)} %get-tuple-element.58.refs_0_.refs_1_, f32[768,128]{1,0:T(8,128)S(1)} %get-tuple-element.44.refs_0_.refs_1_, f32[768,128]{1,0:T(8,128)S(1)} %get-tuple-element.47.refs_1_.refs_2_, bf16[352,352]{1,0:T(8,128)(2,1)S(1)} %get-tuple-element.48.refs_2_.refs_3_.refs_4_, ...), custom_call_target="tpu_custom_call" | custom-call | bytes 6000000 | tf_op jit(solution)/shard_map/pallas_call | solution.py:345
  13.7 0.0 collective-permute-done.2.refs_1_
  13.8 2.5 %collective-permute-done.3.refs_2_ = bf16[176,128]{1,0:T(8,128)(2,1)S(1)} collective-permute-done((bf16[176,128]{1,0:T(8,128)(2,1)S(1)}, bf16[176,128]{1,0:T(8,128)(2,1)S(1)}, u32[]{:S(2)}, u32[]{:S(2)}) %collective-permute-start.3) | collective-permute-done | bytes 45088 | tf_op jit(solution)/shard_map/ppermute | solution.py:963
  16.2 0.5 shard_map.128
  16.7 0.1 collective-permute-start.4
  16.8 2.3 %collective-permute-start.5 = (bf16[176,128]{1,0:T(8,128)(2,1)S(1)}, bf16[176,128]{1,0:T(8,128)(2,1)S(1)}, u32[]{:S(2)}, u32[]{:S(2)}) collective-permute-start(bf16[176,128]{1,0:T(8,128)(2,1)S(1)} %get-tuple-element.65), channel_id=1, source_target_pairs={{0,7},{1,2},{2,1},{3,4},{4,3},{5,6},{6,5},{7,0},{8,15},{9,10},{10,... | collective-permute-start | bytes 135176 | tf_op jit(solution)/shard_map/ppermute | solution.py:963
  19.1 0.5 %shard_map.130.refs_8_ = f32[4,8,128]{2,1,0:T(8,128)S(1)} custom-call(s32[2,729]{1,0:T(2,128)S(1)} %get-tuple-element.67.refs_0_, s32[1,81]{1,0:T(1,128)S(1)} %get-tuple-element.68.refs_1_, s32[1,8]{1,0:T(1,128)S(1)} %get-tuple-element.69.refs_2_, f32[6,128]{1,0:T(8,128)S(1)} %get-tuple-element.70.refs_3_, f32[768,128]{1,0:T(8,128)S(1)} %shard_map.127.refs_0_.refs_4_), custom_call_target="tpu_custom_call" | custom-call | bytes 3000000 | tf_op jit(solution)/shard_map/pallas_call | solution.py:617
  19.7 0.5 %shard_map.129.refs_0_ = f32[768,128]{1,0:T(8,128)S(1)} custom-call(f32[768,128]{1,0:T(8,128)S(1)} %get-tuple-element.63.refs_0_, f32[768,128]{1,0:T(8,128)S(1)} %get-tuple-element.58.refs_0_.refs_1_, f32[768,128]{1,0:T(8,128)S(1)} %get-tuple-element.47.refs_1_.refs_2_, bf16[352,352]{1,0:T(8,128)(2,1)S(1)} %get-tuple-element.48.refs_2_.refs_3_.refs_4_, ...), custom_call_target="tpu_custom_call" | custom-call | bytes 6000000 | tf_op jit(solution)/shard_map/pallas_call | solution.py:345
  20.2 0.0 collective-permute-done.4.refs_1_
  20.2 2.0 %collective-permute-done.5.refs_2_ = bf16[176,128]{1,0:T(8,128)(2,1)S(1)} collective-permute-done((bf16[176,128]{1,0:T(8,128)(2,1)S(1)}, bf16[176,128]{1,0:T(8,128)(2,1)S(1)}, u32[]{:S(2)}, u32[]{:S(2)}) %collective-permute-start.5) | collective-permute-done | bytes 45088 | tf_op jit(solution)/shard_map/ppermute | solution.py:963
  22.1 1.2 %shard_map.131 = (f32[768,128]{1,0:T(8,128)S(1)}, bf16[176,128]{1,0:T(8,128)(2,1)S(1)}, bf16[176,128]{1,0:T(8,128)(2,1)S(1)}, f32[32,1,1408]{2,1,0:T(1,128)}) custom-call(f32[768,128]{1,0:T(8,128)S(1)} %shard_map.129.refs_0_, bf16[176,128]{1,0:T(8,128)(2,1)S(1)} %collective-permute-done.4.refs_1_, bf16[176,128]{1,0:T(8,128)(2,1)S(1)} %collective-permute-done.5.refs_2_, ...), custom_call_target="tpu_custom_call" | custom-call | bytes 3000000 | tf_op jit(solution)/shard_map/pallas_call | solution.py:512
  23.3 4.5 %all-to-all-start = ((f32[32,1,1408]{2,1,0:T(1,128)}), f32[32,1,1408]{2,1,0:T(1,128)S(1)}, u32[]{:S(2)}, u32[]{:S(2)}) async-start(f32[32,1,1408]{2,1,0:T(1,128)} %get-tuple-element.71), calls=%async_computation | async-start | bytes 360448 | tf_op jit(solution)/shard_map/all_to_all | solution.py:933
  27.8 0.3 collective-permute-start.6
  28.2 3.5 %collective-permute-start.7 = (bf16[176,128]{1,0:T(8,128)(2,1)S(1)}, bf16[176,128]{1,0:T(8,128)(2,1)S(1)}, u32[]{:S(2)}, u32[]{:S(2)}) collective-permute-start(bf16[176,128]{1,0:T(8,128)(2,1)S(1)} %get-tuple-element.74), channel_id=1, source_target_pairs={{0,7},{1,2},{2,1},{3,4},{4,3},{5,6},{6,5},{7,0},{8,15},{9,10},{10,... | collective-permute-start | bytes 135176 | tf_op jit(solution)/shard_map/ppermute | solution.py:963
  31.6 0.0 copy-done
  31.6 0.0 copy-done.1
  31.6 0.0 copy-done.2
  31.6 0.0 copy-done.3
  31.6 0.0 copy-done.4
  31.7 0.5 %shard_map.132.after_ref.base_ref = f32[768,128]{1,0:T(8,128)S(1)} custom-call(f32[768,128]{1,0:T(8,128)S(1)} %get-tuple-element.72.refs_0_.y_ref.refs_1_, f32[768,128]{1,0:T(8,128)S(1)} %get-tuple-element.47.refs_1_.refs_2_, bf16[352,352]{1,0:T(8,128)(2,1)S(1)} %get-tuple-element.48.refs_2_.refs_3_.refs_4_, ...), custom_call_target="tpu_custom_call" | custom-call | bytes 6000000 | tf_op jit(solution)/shard_map/pallas_call | solution.py:345
  32.1 1.6 %shard_map.133.high_ref = bf16[729,729]{1,0:T(8,128)(2,1)S(1)} custom-call(f32[729,729]{1,0:T(8,128)} %matrix_hbm.3, f32[768,128]{1,0:T(8,128)S(1)} %shard_map.132.after_ref.base_ref), custom_call_target="tpu_custom_call" | custom-call | bytes 4500000 | tf_op jit(solution)/shard_map/pallas_call | solution.py:759
  33.8 0.0 collective-permute-done.6.near_ref
  33.8 2.0 %collective-permute-done.7.far_ref = bf16[176,128]{1,0:T(8,128)(2,1)S(1)} collective-permute-done((bf16[176,128]{1,0:T(8,128)(2,1)S(1)}, bf16[176,128]{1,0:T(8,128)(2,1)S(1)}, u32[]{:S(2)}, u32[]{:S(2)}) %collective-permute-start.7) | collective-permute-done | bytes 45088 | tf_op jit(solution)/shard_map/ppermute | solution.py:963
  35.8 0.7 %all-to-all-done = f32[32,1,1408]{2,1,0:T(1,128)S(1)} async-done(((f32[32,1,1408]{2,1,0:T(1,128)}), f32[32,1,1408]{2,1,0:T(1,128)S(1)}, u32[]{:S(2)}, u32[]{:S(2)}) %all-to-all-start) | async-done | bytes 180256 | tf_op jit(solution)/shard_map/all_to_all | solution.py:933
  36.5 4.0 %shard_map.134 = (f32[768,128]{1,0:T(8,128)S(1)}, bf16[176,128]{1,0:T(8,128)(2,1)S(1)}, bf16[176,128]{1,0:T(8,128)(2,1)S(1)}, f32[768,128]{1,0:T(8,128)S(1)}, f32[6,128]{1,0:T(8,128)S(1)}) custom-call(f32[352,128]{1,0:T(8,128)S(1)} %bitcast.5, f32[729,729]{1,0:T(8,128)} %matrix_hbm.3, bf16[729,729]{1,0:T(8,128)(2,1)S(1)} %shard_map.133.high_ref, ...), custom_call_target="tpu_custom_call" | custom-call | bytes 12000000 | tf_op jit(solution)/shard_map/pallas_call | solution.py:800
  40.5 1.1 %collective-permute-start.8 = (bf16[176,128]{1,0:T(8,128)(2,1)S(1)}, bf16[176,128]{1,0:T(8,128)(2,1)S(1)}, u32[]{:S(2)}, u32[]{:S(2)}) collective-permute-start(bf16[176,128]{1,0:T(8,128)(2,1)S(1)} %get-tuple-element.77), channel_id=1, source_target_pairs={{0,1},{1,0},{2,3},{3,2},{4,5},{5,4},{6,7},{7,6},{8,9},{9,8},{10,11... | collective-permute-start | bytes 135176 | tf_op jit(solution)/shard_map/ppermute | solution.py:964
  41.6 0.4 collective-permute-start.9
  42.0 1.8 %shard_map.135.refs_0_ = f32[768,128]{1,0:T(8,128)S(1)} custom-call(f32[768,128]{1,0:T(8,128)S(1)} %get-tuple-element.75.refs_0_, f32[768,128]{1,0:T(8,128)S(1)} %get-tuple-element.72.refs_0_.y_ref.refs_1_, f32[768,128]{1,0:T(8,128)} %copy-done, f32[768,128]{1,0:T(8,128)S(1)} %get-tuple-element.76.refs_3_, bf16[352,352]{1,0:T(8,128)(2,1)} %copy-done.2, ...), custom_call_target="tpu_custom_call" | custom-call | bytes 6000000 | tf_op jit(solution)/shard_map/pallas_call | solution.py:345
  43.8 0.0 collective-permute-done.8.refs_1_
  43.8 3.1 %collective-permute-done.9.refs_2_ = bf16[176,128]{1,0:T(8,128)(2,1)S(1)} collective-permute-done((bf16[176,128]{1,0:T(8,128)(2,1)S(1)}, bf16[176,128]{1,0:T(8,128)(2,1)S(1)}, u32[]{:S(2)}, u32[]{:S(2)}) %collective-permute-start.9) | collective-permute-done | bytes 45088 | tf_op jit(solution)/shard_map/ppermute | solution.py:963
  46.9 1.0 %shard_map.136 = (f32[768,128]{1,0:T(8,128)}, f32[6,128]{1,0:T(8,128)}) custom-call(f32[768,128]{1,0:T(8,128)S(1)} %shard_map.135.refs_0_, bf16[176,128]{1,0:T(8,128)(2,1)S(1)} %collective-permute-done.8.refs_1_, bf16[176,128]{1,0:T(8,128)(2,1)S(1)} %collective-permute-done.9.refs_2_, bf16[304,176]{1,0:T(8,128)(2,1)S(1)} %get-tuple-element.54.refs_2_.refs_3_.refs_0_, ...), custom_call_target="tpu_custom_call" | custom-call | bytes 3000000 | tf_op jit(solution)/shard_map/pallas_call | solution.py:512
Async XLA Ops:
  1.9 7.4 %collective-permute-start = (bf16[464,128]{1,0:T(8,128)(2,1)S(1)}, bf16[464,128]{1,0:T(8,128)(2,1)S(1)}, u32[]{:S(2)}, u32[]{:S(2)}) collective-permute-start(bf16[464,128]{1,0:T(8,128)(2,1)S(1)} %get-tuple-element.42), channel_id=1, source_target_pairs={{0,1},{1,2},{2,3},{3,4},{4,5},{5,6},{6,7},{7,0},{8,9},{9,10},{10,1... | collective-permute-start | bytes 356360 | tf_op jit(solution)/shard_map/ppermute | solution.py:32
  2.5 7.9 %collective-permute-start.1 = (bf16[176,128]{1,0:T(8,128)(2,1)S(1)}, bf16[176,128]{1,0:T(8,128)(2,1)S(1)}, u32[]{:S(2)}, u32[]{:S(2)}) collective-permute-start(bf16[176,128]{1,0:T(8,128)(2,1)S(1)} %get-tuple-element.52.own_up_ref), channel_id=1, source_target_pairs={{0,7},{1,0},{2,1},{3,2},{4,3},{5,4},{6,5},{7,6},{8,15},{9,8},{10,9... | collective-permute-start | bytes 135176 | tf_op jit(solution)/shard_map/ppermute | solution.py:32
  8.8 22.8 %copy-start = (f32[768,128]{1,0:T(8,128)}, f32[768,128]{1,0:T(8,128)S(1)}, u32[]{:S(2)}) copy-start(f32[768,128]{1,0:T(8,128)S(1)} %get-tuple-element.47.refs_1_.refs_2_) | copy-start | bytes 1179652
  8.9 22.8 %copy-start.1 = (bf16[368,368]{1,0:T(8,128)(2,1)}, bf16[368,368]{1,0:T(8,128)(2,1)S(1)}, u32[]{:S(2)}) copy-start(bf16[368,368]{1,0:T(8,128)(2,1)S(1)} %get-tuple-element.49.refs_3_.refs_4_.refs_5_) | copy-start | bytes 812548
  8.9 22.8 %copy-start.2 = (bf16[352,352]{1,0:T(8,128)(2,1)}, bf16[352,352]{1,0:T(8,128)(2,1)S(1)}, u32[]{:S(2)}) copy-start(bf16[352,352]{1,0:T(8,128)(2,1)S(1)} %get-tuple-element.48.refs_2_.refs_3_.refs_4_) | copy-start | bytes 743428
  8.9 22.8 %copy-start.3 = (bf16[304,304]{1,0:T(8,128)(2,1)}, bf16[304,304]{1,0:T(8,128)(2,1)S(1)}, u32[]{:S(2)}) copy-start(bf16[304,304]{1,0:T(8,128)(2,1)S(1)} %get-tuple-element.50.refs_4_.refs_5_.refs_6_) | copy-start | bytes 554500
  8.9 22.8 %copy-start.4 = (bf16[192,192]{1,0:T(8,128)(2,1)}, bf16[192,192]{1,0:T(8,128)(2,1)S(1)}, u32[]{:S(2)}) copy-start(bf16[192,192]{1,0:T(8,128)(2,1)S(1)} %get-tuple-element.51.refs_5_.refs_6_.refs_7_) | copy-start | bytes 221188
  10.8 2.9 %collective-permute-start.2 = (bf16[176,128]{1,0:T(8,128)(2,1)S(1)}, bf16[176,128]{1,0:T(8,128)(2,1)S(1)}, u32[]{:S(2)}, u32[]{:S(2)}) collective-permute-start(bf16[176,128]{1,0:T(8,128)(2,1)S(1)} %get-tuple-element.61), channel_id=1, source_target_pairs={{0,1},{1,0},{2,3},{3,2},{4,5},{5,4},{6,7},{7,6},{8,9},{9,8},{10,11... | collective-permute-start | bytes 135176 | tf_op jit(solution)/shard_map/ppermute | solution.py:964
  10.9 5.3 %collective-permute-start.3 = (bf16[176,128]{1,0:T(8,128)(2,1)S(1)}, bf16[176,128]{1,0:T(8,128)(2,1)S(1)}, u32[]{:S(2)}, u32[]{:S(2)}) collective-permute-start(bf16[176,128]{1,0:T(8,128)(2,1)S(1)} %get-tuple-element.62), channel_id=1, source_target_pairs={{0,7},{1,2},{2,1},{3,4},{4,3},{5,6},{6,5},{7,0},{8,15},{9,10},{10,... | collective-permute-start | bytes 135176 | tf_op jit(solution)/shard_map/ppermute | solution.py:963
  16.7 3.5 %collective-permute-start.4 = (bf16[176,128]{1,0:T(8,128)(2,1)S(1)}, bf16[176,128]{1,0:T(8,128)(2,1)S(1)}, u32[]{:S(2)}, u32[]{:S(2)}) collective-permute-start(bf16[176,128]{1,0:T(8,128)(2,1)S(1)} %get-tuple-element.64), channel_id=1, source_target_pairs={{0,1},{1,0},{2,3},{3,2},{4,5},{5,4},{6,7},{7,6},{8,9},{9,8},{10,11... | collective-permute-start | bytes 135176 | tf_op jit(solution)/shard_map/ppermute | solution.py:964
  16.8 5.3 %collective-permute-start.5 = (bf16[176,128]{1,0:T(8,128)(2,1)S(1)}, bf16[176,128]{1,0:T(8,128)(2,1)S(1)}, u32[]{:S(2)}, u32[]{:S(2)}) collective-permute-start(bf16[176,128]{1,0:T(8,128)(2,1)S(1)} %get-tuple-element.65), channel_id=1, source_target_pairs={{0,7},{1,2},{2,1},{3,4},{4,3},{5,6},{6,5},{7,0},{8,15},{9,10},{10,... | collective-permute-start | bytes 135176 | tf_op jit(solution)/shard_map/ppermute | solution.py:963
  23.3 13.2 %all-to-all-start = ((f32[32,1,1408]{2,1,0:T(1,128)}), f32[32,1,1408]{2,1,0:T(1,128)S(1)}, u32[]{:S(2)}, u32[]{:S(2)}) async-start(f32[32,1,1408]{2,1,0:T(1,128)} %get-tuple-element.71), calls=%async_computation | async-start | bytes 360448 | tf_op jit(solution)/shard_map/all_to_all | solution.py:933
  27.8 5.9 %collective-permute-start.6 = (bf16[176,128]{1,0:T(8,128)(2,1)S(1)}, bf16[176,128]{1,0:T(8,128)(2,1)S(1)}, u32[]{:S(2)}, u32[]{:S(2)}) collective-permute-start(bf16[176,128]{1,0:T(8,128)(2,1)S(1)} %get-tuple-element.73), channel_id=1, source_target_pairs={{0,1},{1,0},{2,3},{3,2},{4,5},{5,4},{6,7},{7,6},{8,9},{9,8},{10,11... | collective-permute-start | bytes 135176 | tf_op jit(solution)/shard_map/ppermute | solution.py:964
  28.2 7.7 %collective-permute-start.7 = (bf16[176,128]{1,0:T(8,128)(2,1)S(1)}, bf16[176,128]{1,0:T(8,128)(2,1)S(1)}, u32[]{:S(2)}, u32[]{:S(2)}) collective-permute-start(bf16[176,128]{1,0:T(8,128)(2,1)S(1)} %get-tuple-element.74), channel_id=1, source_target_pairs={{0,7},{1,2},{2,1},{3,4},{4,3},{5,6},{6,5},{7,0},{8,15},{9,10},{10,... | collective-permute-start | bytes 135176 | tf_op jit(solution)/shard_map/ppermute | solution.py:963
  40.5 3.3 %collective-permute-start.8 = (bf16[176,128]{1,0:T(8,128)(2,1)S(1)}, bf16[176,128]{1,0:T(8,128)(2,1)S(1)}, u32[]{:S(2)}, u32[]{:S(2)}) collective-permute-start(bf16[176,128]{1,0:T(8,128)(2,1)S(1)} %get-tuple-element.77), channel_id=1, source_target_pairs={{0,1},{1,0},{2,3},{3,2},{4,5},{5,4},{6,7},{7,6},{8,9},{9,8},{10,11... | collective-permute-start | bytes 135176 | tf_op jit(solution)/shard_map/ppermute | solution.py:964
  41.6 5.3 %collective-permute-start.9 = (bf16[176,128]{1,0:T(8,128)(2,1)S(1)}, bf16[176,128]{1,0:T(8,128)(2,1)S(1)}, u32[]{:S(2)}, u32[]{:S(2)}) collective-permute-start(bf16[176,128]{1,0:T(8,128)(2,1)S(1)} %get-tuple-element.78), channel_id=1, source_target_pairs={{0,7},{1,2},{2,1},{3,4},{4,3},{5,6},{6,5},{7,0},{8,15},{9,10},{10,... | collective-permute-start | bytes 135176 | tf_op jit(solution)/shard_map/ppermute | solution.py:963

commit v5 on v4

--- a/solution.py
+++ b/solution.py
@@ -699,7 +699,7 @@
     return source
 
 
-def field_solve(fg, source, codes, screen, matrix_ref, high_ref, low_ref, rows, copies):
+def field_solve(fg, source, codes, screen, high_ref, low_ref, rows, copies):
     domains, cells = fg.domains, fg.cells
 
     def operator(field):
@@ -714,11 +714,8 @@
         low = (picked - high.astype(F32)).astype(BF)
         both = dot(jnp.concatenate([high, low], axis=0), high_ref[...])
         half_rows = cells * domains
-        for r in range(fg.rows if copies else 0):
-            copies.pop(0).wait()
-            span = slice(r * LANES, min((r + 1) * LANES, fg.npc))
-            rest = matrix_ref[span, :] - high_ref[span, :].astype(F32)
-            low_ref[span, :] = rest.astype(BF)
+        if copies:
+            copies.pop().wait()
         rows[:, 0 : fg.npc] = both[:half_rows] + (both[half_rows:] + dot(high, low_ref[...]))
         out = [None] * fg.tiles
         for c in range(cells):
@@ -745,38 +742,44 @@
     return [(x + y) + z for x, y, z in zip(step_one, step_two, step_three)]
 
 
-def field_top_kernel(fg, matrix_hbm, after_ref, top_ref, matrix_ref, sems):
+def field_parts_kernel(fg, matrix_hbm, after_ref, top_ref, low_ref, matrix_ref, sems):
     del after_ref
     spans = [pl.ds(r * LANES, min(LANES, fg.npc - r * LANES)) for r in range(fg.rows)]
     copies = fetch([(matrix_hbm.at[span], matrix_ref.at[span]) for span in spans], sems)
     for r, copy in enumerate(copies):
         copy.wait()
         span = slice(r * LANES, min((r + 1) * LANES, fg.npc))
-        top_ref[span, :] = matrix_ref[span, :].astype(BF)
-
-
-def field_top(fg, matrix, after):
+        full = matrix_ref[span, :]
+        top = full.astype(BF)
+        top_ref[span, :] = top
+        low_ref[span, :] = (full - top.astype(F32)).astype(BF)
+
+
+def field_parts(fg, matrix, after):
+    hbm = pl.BlockSpec(memory_space=pltpu.HBM)
     return vmem_call(
-        functools.partial(field_top_kernel, fg),
-        sds(matrix.shape, BF),
-        [pltpu.VMEM(matrix.shape, F32), pltpu.SemaphoreType.DMA((fg.rows,))],
-        in_specs=[pl.BlockSpec(memory_space=pltpu.HBM), pl.BlockSpec(memory_space=pl.ANY)],
-        cost=cost_of(1.5),
+        functools.partial(field_parts_kernel, fg),
+        [sds(matrix.shape, BF), sds(matrix.shape, BF)],
+        [
+            pltpu.VMEM(matrix.shape, F32),
+            pltpu.SemaphoreType.DMA((fg.rows,)),
+        ],
+        in_specs=[hbm, pl.BlockSpec(memory_space=pl.ANY)],
+        cost=cost_of(2.5),
     )(*in_hbm(matrix), after)
 
 
-def field_kernel(geo, fg, scale, got_ref, matrix_hbm, high_ref, base_ref, near_ref, far_ref, y_ref, *refs):
+def field_kernel(geo, fg, scale, got_ref, low_hbm, high_ref, base_ref, near_ref, far_ref, y_ref, *refs):
     n = len(geo.touching)
     crosses, reaches, refs = refs[:n], refs[n : 2 * n], refs[2 * n :]
     z_ref, near_out, far_out, column_ref, hartree_ref = refs[:5]
-    codes, rows, mine, matrix_ref, low_ref, sems = refs[5:]
-    spans = [pl.ds(r * LANES, min(LANES, fg.npc - r * LANES)) for r in range(fg.rows)]
-    copies = fetch([(matrix_hbm.at[span], matrix_ref.at[span]) for span in spans], sems)
+    codes, rows, mine, low_ref, sems = refs[5:]
+    copies = fetch([(low_hbm, low_ref)], sems)
     z_ref[...] = base_ref[...]
     add_halo(geo, scale, z_ref, near_ref, far_ref, crosses)
     places, owner, screens = decode(fg, got_ref, codes)
     source = field_source(fg, got_ref, places)
-    solved = field_solve(fg, source, codes, screens, matrix_ref, high_ref, low_ref, rows, copies)
+    solved = field_solve(fg, source, codes, screens, high_ref, low_ref, rows, copies)
     lane = lax.broadcasted_iota(I32, (fg.domains, LANES), 1)
     block = lookup(list(enumerate(solved)), lane + lax.axis_index("domain") * fg.block)
     mine[...] = rows_of(block, owner)
@@ -790,11 +793,11 @@
         hartree_ref[row : row + 1, start : start + count] = mine[j : j + 1, offset : offset + count]
 
 
-def field_step(geo, fg, scale, got, matrix, top, base, halo, y, crosses, reaches):
+def field_step(geo, fg, scale, got, top, rest, base, halo, y, crosses, reaches):
     tile = (fg.domains, LANES)
     vmem = pl.BlockSpec(memory_space=pltpu.VMEM)
     got = got.reshape(got.shape[0] * fg.width // LANES, LANES)
-    args = [got, *in_hbm(matrix), top, base, *halo, y, *crosses, *reaches]
+    args = [got, *in_hbm(rest), top, base, *halo, y, *crosses, *reaches]
     specs = [vmem] * len(args)
     specs[1] = pl.BlockSpec(memory_space=pltpu.HBM)
     z, near, far, column, lines = vmem_call(
@@ -809,9 +812,8 @@
             pltpu.VMEM((2 * fg.at_screen, *tile), I32),
             pltpu.VMEM((fg.cells * fg.domains, fg.size), F32),
             pltpu.VMEM(tile, F32),
-            pltpu.VMEM(matrix.shape, F32),
-            pltpu.VMEM(matrix.shape, BF),
-            pltpu.SemaphoreType.DMA((fg.rows,)),
+            pltpu.VMEM(rest.shape, BF),
+            pltpu.SemaphoreType.DMA((1,)),
         ],
         in_specs=specs,
         cost=cost_of(4.0),
@@ -933,9 +935,9 @@
         dens = lax.all_to_all(spread, ("band", "domain"), 0, 0, tiled=True)
         halo = swap((dn, up))
         base = owned_part(geo, first, y3, None, pot, None, mats, uppers)
-        top = field_top(fg, pois_matrix, base)
+        top, rest = field_parts(fg, pois_matrix, base)
         z1, sends4, column, packed = field_step(
-            geo, fg, first, dens, pois_matrix, top, base, halo, y3, crosses, reaches
+            geo, fg, first, dens, top, rest, base, halo, y3, crosses, reaches
         )
     else:
         y3, *sends3 = finish(geo, later, base, halo, crosses, reaches)

time: 48.2 us -> 47.5 us (0.985)
  local copies, waits for them, and re-layouts: 0.02 us -> 1.03 us
  waiting for transfers between devices: 10.2 us -> 9.2 us
  Pallas kernels: 17.5 us -> 16.9 us
    ppermute x4, waiting for transfers between devices: 9.53 us -> 8.49 us  [swap(): far = lax.ppermute(far, 'domain', turns)]
    unnamed x10 -> x12, local copies, waits for them, and re-layouts: 0.02 us -> 1.03 us
    pallas_call x1, Pallas kernels: 4 us -> 3.38 us  [field_step(): vmem_call(functools.partial(field_kernel, geo, fg, scale), [sds(y.shape,...]
where the time goes in v5:
time: 47.5 us; the launch traced here: 47.3 us
  starting transfers between devices  19.3 us (41%)
  Pallas kernels  16.9 us (36%)
  waiting for transfers between devices  9.2 us (19%)
  local copies, waits for them, and re-layouts  1.03 us (2%)
  between operations  0.86 us (2%)
    ppermute x4, starting transfers between devices, swap(): far = lax.ppermute(far, 'domain', turns)  8.54 us
    ppermute x4, waiting for transfers between devices, swap(): far = lax.ppermute(far, 'domain', turns)  8.49 us
    ppermute x2, starting transfers between devices, from_behind(): lax.ppermute(array, axis, [(i, (i + by) % length) for i in range(length)])  4.64 us
    all_to_all x1, starting transfers between devices, on_device(): dens = lax.all_to_all(spread, ('band', 'domain'), 0, 0, tiled=True)  4.52 us
    pallas_call x5, Pallas kernels, owned_part(): vmem_call(functools.partial(owned_part_kernel, geo, scale, prev is not No...  3.72 us
    pallas_call x1, Pallas kernels, field_step(): vmem_call(functools.partial(field_kernel, geo, fg, scale), [sds(y.shape,...  3.38 us
    pallas_call x3, Pallas kernels, finish(): vmem_call(functools.partial(finish_kernel, geo, scale, mode, part_rows),...  2.59 us
    pallas_call x1, Pallas kernels, own_matrices(): vmem_call(functools.partial(own_matrices_kernel, geo), shapes, [matrix_sc...  2.25 us
  transfers between devices with their start and end apart: 11, of which 5 were waited for; matrix products, arithmetic and copies ran while one was open for 0% of the time, Pallas kernels for 19%

profile of v5, /device:TPU:0, one launch (start us, length us, event | category | flops | bytes accessed | tf_op | source)
XLA Modules:
  0.0 47.3 jit_solution(5799621389417260150)
XLA Ops:
  0.6 1.3 %shard_map.122 = (bf16[464,128]{1,0:T(8,128)(2,1)S(1)}, bf16[176,128]{1,0:T(8,128)(2,1)S(1)}, f32[768,128]{1,0:T(8,128)S(1)}, s32[8,384]{1,0:T(8,128)S(1)}, bf16...) custom-call(f32[768,128]{1,0:T(8,128)} %y_hbm.1, ...), custom_call_target="tpu_custom_call" | custom-call | bytes 3000000 | tf_op jit(solution)/shard_map/pallas_call | solution.py:270
  1.9 0.5 %collective-permute-start = (bf16[464,128]{1,0:T(8,128)(2,1)S(1)}, bf16[464,128]{1,0:T(8,128)(2,1)S(1)}, u32[]{:S(2)}, u32[]{:S(2)}) collective-permute-start(bf16[464,128]{1,0:T(8,128)(2,1)S(1)} %get-tuple-element.44), channel_id=1, source_target_pairs={{0,1},{1,2},{2,3},{3,4},{4,5},{5,6},{6,7},{7,0},{8,9},{9,10},{10,1... | collective-permute-start | bytes 356360 | tf_op jit(solution)/shard_map/ppermute | solution.py:32
  2.5 4.1 %collective-permute-start.1 = (bf16[176,128]{1,0:T(8,128)(2,1)S(1)}, bf16[176,128]{1,0:T(8,128)(2,1)S(1)}, u32[]{:S(2)}, u32[]{:S(2)}) collective-permute-start(bf16[176,128]{1,0:T(8,128)(2,1)S(1)} %get-tuple-element.54.own_up_ref), channel_id=1, source_target_pairs={{0,7},{1,0},{2,1},{3,2},{4,3},{5,4},{6,5},{7,6},{8,15},{9,8},{10,9... | collective-permute-start | bytes 135176 | tf_op jit(solution)/shard_map/ppermute | solution.py:32
  6.6 2.3 %shard_map.123 = (bf16[352,352]{1,0:T(8,128)(2,1)S(1)}, bf16[368,368]{1,0:T(8,128)(2,1)S(1)}, bf16[304,304]{1,0:T(8,128)(2,1)S(1)}, bf16[192,192]{1,0:T(8,128)(2...) custom-call(s32[8,384]{1,0:T(8,128)S(1)} %get-tuple-element.47.refs_, ...), custom_call_target="tpu_custom_call" | custom-call | bytes 6000000 | tf_op jit(solution)/shard_map/pallas_call | solution.py:172
  8.8 0.0 copy-start
  8.9 0.0 copy-start.1
  8.9 0.0 copy-start.2
  8.9 0.0 copy-start.3
  8.9 0.0 copy-start.4
  8.9 0.4 shard_map.124.base_ref
  9.3 0.0 collective-permute-done.sent_ref
  9.4 1.0 %shard_map.125 = (bf16[176,176]{1,0:T(8,128)(2,1)S(1)}, bf16[176,176]{1,0:T(8,128)(2,1)S(1)}, f32[768,128]{1,0:T(8,128)S(1)}) custom-call(bf16[464,128]{1,0:T(8,128)(2,1)S(1)} %collective-permute-done.sent_ref, bf16[343,343]{1,0:T(8,128)(2,1)S(1)} %get-tuple-element.45.refs_1_.matrix_ref, f32[768,128]{1,0:T(8,128)S(1)} %shard_map.124.base_ref, ...), custom_call_target="tpu_custom_call" | custom-call | bytes 3000000 | tf_op jit(solution)/shard_map/pallas_call | solution.py:409
  10.4 0.0 collective-permute-done.1.refs_1_
  10.4 0.5 shard_map.126
  10.8 0.1 collective-permute-start.2
  10.9 2.3 %collective-permute-start.3 = (bf16[176,128]{1,0:T(8,128)(2,1)S(1)}, bf16[176,128]{1,0:T(8,128)(2,1)S(1)}, u32[]{:S(2)}, u32[]{:S(2)}) collective-permute-start(bf16[176,128]{1,0:T(8,128)(2,1)S(1)} %get-tuple-element.64), channel_id=1, source_target_pairs={{0,7},{1,2},{2,1},{3,4},{4,3},{5,6},{6,5},{7,0},{8,15},{9,10},{10,... | collective-permute-start | bytes 135176 | tf_op jit(solution)/shard_map/ppermute | solution.py:965
  13.2 0.5 %shard_map.127.refs_0_.refs_4_ = f32[768,128]{1,0:T(8,128)S(1)} custom-call(f32[768,128]{1,0:T(8,128)S(1)} %get-tuple-element.60.refs_0_.refs_1_, f32[768,128]{1,0:T(8,128)S(1)} %get-tuple-element.46.refs_0_.refs_1_, f32[768,128]{1,0:T(8,128)S(1)} %get-tuple-element.49.refs_1_.refs_2_, bf16[352,352]{1,0:T(8,128)(2,1)S(1)} %get-tuple-element.50.refs_2_.refs_3_.refs_4_, ...), custom_call_target="tpu_custom_call" | custom-call | bytes 6000000 | tf_op jit(solution)/shard_map/pallas_call | solution.py:345
  13.7 0.0 collective-permute-done.2.refs_1_
  13.8 2.5 %collective-permute-done.3.refs_2_ = bf16[176,128]{1,0:T(8,128)(2,1)S(1)} collective-permute-done((bf16[176,128]{1,0:T(8,128)(2,1)S(1)}, bf16[176,128]{1,0:T(8,128)(2,1)S(1)}, u32[]{:S(2)}, u32[]{:S(2)}) %collective-permute-start.3) | collective-permute-done | bytes 45088 | tf_op jit(solution)/shard_map/ppermute | solution.py:965
  16.2 0.5 shard_map.128
  16.7 0.1 collective-permute-start.4
  16.8 2.3 %collective-permute-start.5 = (bf16[176,128]{1,0:T(8,128)(2,1)S(1)}, bf16[176,128]{1,0:T(8,128)(2,1)S(1)}, u32[]{:S(2)}, u32[]{:S(2)}) collective-permute-start(bf16[176,128]{1,0:T(8,128)(2,1)S(1)} %get-tuple-element.67), channel_id=1, source_target_pairs={{0,7},{1,2},{2,1},{3,4},{4,3},{5,6},{6,5},{7,0},{8,15},{9,10},{10,... | collective-permute-start | bytes 135176 | tf_op jit(solution)/shard_map/ppermute | solution.py:965
  19.1 0.5 %shard_map.130.refs_8_ = f32[4,8,128]{2,1,0:T(8,128)S(1)} custom-call(s32[2,729]{1,0:T(2,128)S(1)} %get-tuple-element.69.refs_0_, s32[1,81]{1,0:T(1,128)S(1)} %get-tuple-element.70.refs_1_, s32[1,8]{1,0:T(1,128)S(1)} %get-tuple-element.71.refs_2_, f32[6,128]{1,0:T(8,128)S(1)} %get-tuple-element.72.refs_3_, f32[768,128]{1,0:T(8,128)S(1)} %shard_map.127.refs_0_.refs_4_), custom_call_target="tpu_custom_call" | custom-call | bytes 3000000 | tf_op jit(solution)/shard_map/pallas_call | solution.py:617
  19.7 0.5 %shard_map.129.refs_0_ = f32[768,128]{1,0:T(8,128)S(1)} custom-call(f32[768,128]{1,0:T(8,128)S(1)} %get-tuple-element.65.refs_0_, f32[768,128]{1,0:T(8,128)S(1)} %get-tuple-element.60.refs_0_.refs_1_, f32[768,128]{1,0:T(8,128)S(1)} %get-tuple-element.49.refs_1_.refs_2_, bf16[352,352]{1,0:T(8,128)(2,1)S(1)} %get-tuple-element.50.refs_2_.refs_3_.refs_4_, ...), custom_call_target="tpu_custom_call" | custom-call | bytes 6000000 | tf_op jit(solution)/shard_map/pallas_call | solution.py:345
  20.2 0.0 collective-permute-done.4.refs_1_
  20.2 2.0 %collective-permute-done.5.refs_2_ = bf16[176,128]{1,0:T(8,128)(2,1)S(1)} collective-permute-done((bf16[176,128]{1,0:T(8,128)(2,1)S(1)}, bf16[176,128]{1,0:T(8,128)(2,1)S(1)}, u32[]{:S(2)}, u32[]{:S(2)}) %collective-permute-start.5) | collective-permute-done | bytes 45088 | tf_op jit(solution)/shard_map/ppermute | solution.py:965
  22.1 1.2 %shard_map.131 = (f32[768,128]{1,0:T(8,128)S(1)}, bf16[176,128]{1,0:T(8,128)(2,1)S(1)}, bf16[176,128]{1,0:T(8,128)(2,1)S(1)}, f32[32,1,1408]{2,1,0:T(1,128)}) custom-call(f32[768,128]{1,0:T(8,128)S(1)} %shard_map.129.refs_0_, bf16[176,128]{1,0:T(8,128)(2,1)S(1)} %collective-permute-done.4.refs_1_, bf16[176,128]{1,0:T(8,128)(2,1)S(1)} %collective-permute-done.5.refs_2_, ...), custom_call_target="tpu_custom_call" | custom-call | bytes 3000000 | tf_op jit(solution)/shard_map/pallas_call | solution.py:512
  23.3 4.5 %all-to-all-start = ((f32[32,1,1408]{2,1,0:T(1,128)}), f32[32,1,1408]{2,1,0:T(1,128)S(1)}, u32[]{:S(2)}, u32[]{:S(2)}) async-start(f32[32,1,1408]{2,1,0:T(1,128)} %get-tuple-element.73), calls=%async_computation | async-start | bytes 360448 | tf_op jit(solution)/shard_map/all_to_all | solution.py:935
  27.8 0.3 collective-permute-start.6
  28.1 3.5 %collective-permute-start.7 = (bf16[176,128]{1,0:T(8,128)(2,1)S(1)}, bf16[176,128]{1,0:T(8,128)(2,1)S(1)}, u32[]{:S(2)}, u32[]{:S(2)}) collective-permute-start(bf16[176,128]{1,0:T(8,128)(2,1)S(1)} %get-tuple-element.78), channel_id=1, source_target_pairs={{0,7},{1,2},{2,1},{3,4},{4,3},{5,6},{6,5},{7,0},{8,15},{9,10},{10,... | collective-permute-start | bytes 135176 | tf_op jit(solution)/shard_map/ppermute | solution.py:965
  31.6 0.0 copy-done
  31.6 0.0 copy-done.1
  31.6 0.0 copy-done.2
  31.6 0.0 copy-done.3
  31.6 0.0 copy-done.4
  31.6 0.5 %shard_map.132.after_ref.base_ref = f32[768,128]{1,0:T(8,128)S(1)} custom-call(f32[768,128]{1,0:T(8,128)S(1)} %get-tuple-element.74.refs_0_.y_ref.refs_1_, f32[768,128]{1,0:T(8,128)S(1)} %get-tuple-element.49.refs_1_.refs_2_, bf16[352,352]{1,0:T(8,128)(2,1)S(1)} %get-tuple-element.50.refs_2_.refs_3_.refs_4_, ...), custom_call_target="tpu_custom_call" | custom-call | bytes 6000000 | tf_op jit(solution)/shard_map/pallas_call | solution.py:345
  32.1 1.7 %shard_map.133 = (bf16[729,729]{1,0:T(8,128)(2,1)S(1)}, bf16[729,729]{1,0:T(8,128)(2,1)S(1)}) custom-call(f32[729,729]{1,0:T(8,128)} %matrix_hbm.1, f32[768,128]{1,0:T(8,128)S(1)} %shard_map.132.after_ref.base_ref), custom_call_target="tpu_custom_call" | custom-call | bytes 7500000 | tf_op jit(solution)/shard_map/pallas_call | solution.py:760
  33.8 1.0 %copy-done.5 = bf16[729,729]{1,0:T(8,128)(2,1)} copy-done((bf16[729,729]{1,0:T(8,128)(2,1)}, bf16[729,729]{1,0:T(8,128)(2,1)S(1)}, u32[]{:S(2)}) %copy-start.5) | copy-done | bytes 1062906
  34.8 0.0 collective-permute-done.6.near_ref
  34.8 1.0 %collective-permute-done.7.far_ref = bf16[176,128]{1,0:T(8,128)(2,1)S(1)} collective-permute-done((bf16[176,128]{1,0:T(8,128)(2,1)S(1)}, bf16[176,128]{1,0:T(8,128)(2,1)S(1)}, u32[]{:S(2)}, u32[]{:S(2)}) %collective-permute-start.7) | collective-permute-done | bytes 45088 | tf_op jit(solution)/shard_map/ppermute | solution.py:965
  35.8 0.7 %all-to-all-done = f32[32,1,1408]{2,1,0:T(1,128)S(1)} async-done(((f32[32,1,1408]{2,1,0:T(1,128)}), f32[32,1,1408]{2,1,0:T(1,128)S(1)}, u32[]{:S(2)}, u32[]{:S(2)}) %all-to-all-start) | async-done | bytes 180256 | tf_op jit(solution)/shard_map/all_to_all | solution.py:935
  36.5 3.4 %shard_map.134 = (f32[768,128]{1,0:T(8,128)S(1)}, bf16[176,128]{1,0:T(8,128)(2,1)S(1)}, bf16[176,128]{1,0:T(8,128)(2,1)S(1)}, f32[768,128]{1,0:T(8,128)S(1)}, f32[6,128]{1,0:T(8,128)S(1)}) custom-call(f32[352,128]{1,0:T(8,128)S(1)} %bitcast.5, bf16[729,729]{1,0:T(8,128)(2,1)} %copy-done.5, bf16[729,729]{1,0:T(8,128)(2,1)S(1)} %get-tuple-element.76.high_ref, ...), custom_call_target="tpu_custom_call" | custom-call | bytes 12000000 | tf_op jit(solution)/shard_map/pallas_call | solution.py:803
  39.9 1.1 %collective-permute-start.8 = (bf16[176,128]{1,0:T(8,128)(2,1)S(1)}, bf16[176,128]{1,0:T(8,128)(2,1)S(1)}, u32[]{:S(2)}, u32[]{:S(2)}) collective-permute-start(bf16[176,128]{1,0:T(8,128)(2,1)S(1)} %get-tuple-element.81), channel_id=1, source_target_pairs={{0,1},{1,0},{2,3},{3,2},{4,5},{5,4},{6,7},{7,6},{8,9},{9,8},{10,11... | collective-permute-start | bytes 135176 | tf_op jit(solution)/shard_map/ppermute | solution.py:966
  41.0 0.4 collective-permute-start.9
  41.4 1.8 %shard_map.135.refs_0_ = f32[768,128]{1,0:T(8,128)S(1)} custom-call(f32[768,128]{1,0:T(8,128)S(1)} %get-tuple-element.79.refs_0_, f32[768,128]{1,0:T(8,128)S(1)} %get-tuple-element.74.refs_0_.y_ref.refs_1_, f32[768,128]{1,0:T(8,128)} %copy-done, f32[768,128]{1,0:T(8,128)S(1)} %get-tuple-element.80.refs_3_, bf16[352,352]{1,0:T(8,128)(2,1)} %copy-done.2, ...), custom_call_target="tpu_custom_call" | custom-call | bytes 6000000 | tf_op jit(solution)/shard_map/pallas_call | solution.py:345
  43.2 0.0 collective-permute-done.8.refs_1_
  43.2 3.1 %collective-permute-done.9.refs_2_ = bf16[176,128]{1,0:T(8,128)(2,1)S(1)} collective-permute-done((bf16[176,128]{1,0:T(8,128)(2,1)S(1)}, bf16[176,128]{1,0:T(8,128)(2,1)S(1)}, u32[]{:S(2)}, u32[]{:S(2)}) %collective-permute-start.9) | collective-permute-done | bytes 45088 | tf_op jit(solution)/shard_map/ppermute | solution.py:965
  46.3 1.0 %shard_map.136 = (f32[768,128]{1,0:T(8,128)}, f32[6,128]{1,0:T(8,128)}) custom-call(f32[768,128]{1,0:T(8,128)S(1)} %shard_map.135.refs_0_, bf16[176,128]{1,0:T(8,128)(2,1)S(1)} %collective-permute-done.8.refs_1_, bf16[176,128]{1,0:T(8,128)(2,1)S(1)} %collective-permute-done.9.refs_2_, bf16[304,176]{1,0:T(8,128)(2,1)S(1)} %get-tuple-element.56.refs_2_.refs_3_.refs_0_, ...), custom_call_target="tpu_custom_call" | custom-call | bytes 3000000 | tf_op jit(solution)/shard_map/pallas_call | solution.py:512
  (1 shorter events, 0.0 us)
Async XLA Ops:
  1.9 7.4 %collective-permute-start = (bf16[464,128]{1,0:T(8,128)(2,1)S(1)}, bf16[464,128]{1,0:T(8,128)(2,1)S(1)}, u32[]{:S(2)}, u32[]{:S(2)}) collective-permute-start(bf16[464,128]{1,0:T(8,128)(2,1)S(1)} %get-tuple-element.44), channel_id=1, source_target_pairs={{0,1},{1,2},{2,3},{3,4},{4,5},{5,6},{6,7},{7,0},{8,9},{9,10},{10,1... | collective-permute-start | bytes 356360 | tf_op jit(solution)/shard_map/ppermute | solution.py:32
  2.5 7.9 %collective-permute-start.1 = (bf16[176,128]{1,0:T(8,128)(2,1)S(1)}, bf16[176,128]{1,0:T(8,128)(2,1)S(1)}, u32[]{:S(2)}, u32[]{:S(2)}) collective-permute-start(bf16[176,128]{1,0:T(8,128)(2,1)S(1)} %get-tuple-element.54.own_up_ref), channel_id=1, source_target_pairs={{0,7},{1,0},{2,1},{3,2},{4,3},{5,4},{6,5},{7,6},{8,15},{9,8},{10,9... | collective-permute-start | bytes 135176 | tf_op jit(solution)/shard_map/ppermute | solution.py:32
  8.8 22.8 %copy-start = (f32[768,128]{1,0:T(8,128)}, f32[768,128]{1,0:T(8,128)S(1)}, u32[]{:S(2)}) copy-start(f32[768,128]{1,0:T(8,128)S(1)} %get-tuple-element.49.refs_1_.refs_2_) | copy-start | bytes 1179652
  8.9 22.8 %copy-start.1 = (bf16[368,368]{1,0:T(8,128)(2,1)}, bf16[368,368]{1,0:T(8,128)(2,1)S(1)}, u32[]{:S(2)}) copy-start(bf16[368,368]{1,0:T(8,128)(2,1)S(1)} %get-tuple-element.51.refs_3_.refs_4_.refs_5_) | copy-start | bytes 812548
  8.9 22.8 %copy-start.2 = (bf16[352,352]{1,0:T(8,128)(2,1)}, bf16[352,352]{1,0:T(8,128)(2,1)S(1)}, u32[]{:S(2)}) copy-start(bf16[352,352]{1,0:T(8,128)(2,1)S(1)} %get-tuple-element.50.refs_2_.refs_3_.refs_4_) | copy-start | bytes 743428
  8.9 22.8 %copy-start.3 = (bf16[304,304]{1,0:T(8,128)(2,1)}, bf16[304,304]{1,0:T(8,128)(2,1)S(1)}, u32[]{:S(2)}) copy-start(bf16[304,304]{1,0:T(8,128)(2,1)S(1)} %get-tuple-element.52.refs_4_.refs_5_.refs_6_) | copy-start | bytes 554500
  8.9 22.8 %copy-start.4 = (bf16[192,192]{1,0:T(8,128)(2,1)}, bf16[192,192]{1,0:T(8,128)(2,1)S(1)}, u32[]{:S(2)}) copy-start(bf16[192,192]{1,0:T(8,128)(2,1)S(1)} %get-tuple-element.53.refs_5_.refs_6_.refs_7_) | copy-start | bytes 221188
  10.8 2.9 %collective-permute-start.2 = (bf16[176,128]{1,0:T(8,128)(2,1)S(1)}, bf16[176,128]{1,0:T(8,128)(2,1)S(1)}, u32[]{:S(2)}, u32[]{:S(2)}) collective-permute-start(bf16[176,128]{1,0:T(8,128)(2,1)S(1)} %get-tuple-element.63), channel_id=1, source_target_pairs={{0,1},{1,0},{2,3},{3,2},{4,5},{5,4},{6,7},{7,6},{8,9},{9,8},{10,11... | collective-permute-start | bytes 135176 | tf_op jit(solution)/shard_map/ppermute | solution.py:966
  10.9 5.3 %collective-permute-start.3 = (bf16[176,128]{1,0:T(8,128)(2,1)S(1)}, bf16[176,128]{1,0:T(8,128)(2,1)S(1)}, u32[]{:S(2)}, u32[]{:S(2)}) collective-permute-start(bf16[176,128]{1,0:T(8,128)(2,1)S(1)} %get-tuple-element.64), channel_id=1, source_target_pairs={{0,7},{1,2},{2,1},{3,4},{4,3},{5,6},{6,5},{7,0},{8,15},{9,10},{10,... | collective-permute-start | bytes 135176 | tf_op jit(solution)/shard_map/ppermute | solution.py:965
  16.7 3.5 %collective-permute-start.4 = (bf16[176,128]{1,0:T(8,128)(2,1)S(1)}, bf16[176,128]{1,0:T(8,128)(2,1)S(1)}, u32[]{:S(2)}, u32[]{:S(2)}) collective-permute-start(bf16[176,128]{1,0:T(8,128)(2,1)S(1)} %get-tuple-element.66), channel_id=1, source_target_pairs={{0,1},{1,0},{2,3},{3,2},{4,5},{5,4},{6,7},{7,6},{8,9},{9,8},{10,11... | collective-permute-start | bytes 135176 | tf_op jit(solution)/shard_map/ppermute | solution.py:966
  16.8 5.3 %collective-permute-start.5 = (bf16[176,128]{1,0:T(8,128)(2,1)S(1)}, bf16[176,128]{1,0:T(8,128)(2,1)S(1)}, u32[]{:S(2)}, u32[]{:S(2)}) collective-permute-start(bf16[176,128]{1,0:T(8,128)(2,1)S(1)} %get-tuple-element.67), channel_id=1, source_target_pairs={{0,7},{1,2},{2,1},{3,4},{4,3},{5,6},{6,5},{7,0},{8,15},{9,10},{10,... | collective-permute-start | bytes 135176 | tf_op jit(solution)/shard_map/ppermute | solution.py:965
  23.3 13.2 %all-to-all-start = ((f32[32,1,1408]{2,1,0:T(1,128)}), f32[32,1,1408]{2,1,0:T(1,128)S(1)}, u32[]{:S(2)}, u32[]{:S(2)}) async-start(f32[32,1,1408]{2,1,0:T(1,128)} %get-tuple-element.73), calls=%async_computation | async-start | bytes 360448 | tf_op jit(solution)/shard_map/all_to_all | solution.py:935
  27.8 7.0 %collective-permute-start.6 = (bf16[176,128]{1,0:T(8,128)(2,1)S(1)}, bf16[176,128]{1,0:T(8,128)(2,1)S(1)}, u32[]{:S(2)}, u32[]{:S(2)}) collective-permute-start(bf16[176,128]{1,0:T(8,128)(2,1)S(1)} %get-tuple-element.77), channel_id=1, source_target_pairs={{0,1},{1,0},{2,3},{3,2},{4,5},{5,4},{6,7},{7,6},{8,9},{9,8},{10,11... | collective-permute-start | bytes 135176 | tf_op jit(solution)/shard_map/ppermute | solution.py:966
  28.1 7.7 %collective-permute-start.7 = (bf16[176,128]{1,0:T(8,128)(2,1)S(1)}, bf16[176,128]{1,0:T(8,128)(2,1)S(1)}, u32[]{:S(2)}, u32[]{:S(2)}) collective-permute-start(bf16[176,128]{1,0:T(8,128)(2,1)S(1)} %get-tuple-element.78), channel_id=1, source_target_pairs={{0,7},{1,2},{2,1},{3,4},{4,3},{5,6},{6,5},{7,0},{8,15},{9,10},{10,... | collective-permute-start | bytes 135176 | tf_op jit(solution)/shard_map/ppermute | solution.py:965
  33.8 1.0 %copy-start.5 = (bf16[729,729]{1,0:T(8,128)(2,1)}, bf16[729,729]{1,0:T(8,128)(2,1)S(1)}, u32[]{:S(2)}) copy-start(bf16[729,729]{1,0:T(8,128)(2,1)S(1)} %get-tuple-element.75.low_hbm) | copy-start | bytes 3188650
  39.9 3.3 %collective-permute-start.8 = (bf16[176,128]{1,0:T(8,128)(2,1)S(1)}, bf16[176,128]{1,0:T(8,128)(2,1)S(1)}, u32[]{:S(2)}, u32[]{:S(2)}) collective-permute-start(bf16[176,128]{1,0:T(8,128)(2,1)S(1)} %get-tuple-element.81), channel_id=1, source_target_pairs={{0,1},{1,0},{2,3},{3,2},{4,5},{5,4},{6,7},{7,6},{8,9},{9,8},{10,11... | collective-permute-start | bytes 135176 | tf_op jit(solution)/shard_map/ppermute | solution.py:966
  41.0 5.3 %collective-permute-start.9 = (bf16[176,128]{1,0:T(8,128)(2,1)S(1)}, bf16[176,128]{1,0:T(8,128)(2,1)S(1)}, u32[]{:S(2)}, u32[]{:S(2)}) collective-permute-start(bf16[176,128]{1,0:T(8,128)(2,1)S(1)} %get-tuple-element.82), channel_id=1, source_target_pairs={{0,7},{1,2},{2,1},{3,4},{4,3},{5,6},{6,5},{7,0},{8,15},{9,10},{10,... | collective-permute-start | bytes 135176 | tf_op jit(solution)/shard_map/ppermute | solution.py:965

commit v6 on v5

--- a/solution.py
+++ b/solution.py
@@ -381,7 +381,15 @@
     add_upper(geo, scale, y_ref, jnp.where(even, near, far).astype(BF), crosses)
 
 
-def write_density(y_ref, occ_ref, table_ref, part_rows, dens_ref):
+def write_tables(own, table_ref, part_rows, dens_ref):
+    parts = dens_ref.shape[0]
+    band = lax.axis_index("band")
+    for r in range(part_rows):
+        row = table_ref[band, r : r + 1, :]
+        dens_ref[:, 0, own + r * LANES : own + (r + 1) * LANES] = jnp.broadcast_to(row, (parts, LANES))
+
+
+def write_density(y_ref, occ_ref, dens_ref):
     parts = dens_ref.shape[0]
     own = y_ref.shape[0]
     y = y_ref[...]
@@ -391,10 +399,6 @@
     ones = jnp.ones((SUBLANES, terms.shape[1]), BF)
     summed = dot_t(ones, high) + dot_t(ones, low)
     dens_ref[:, 0, 0:own] = jnp.broadcast_to(summed[0:1, :], (parts, own))
-    band = lax.axis_index("band")
-    for r in range(part_rows):
-        row = table_ref[band, r : r + 1, :]
-        dens_ref[:, 0, own + r * LANES : own + (r + 1) * LANES] = jnp.broadcast_to(row, (parts, LANES))
 
 
 def behind_kernel(geo, scale, sent_ref, matrix_ref, base_ref, own_up_ref, *refs):
@@ -452,16 +456,24 @@
     if mode == "density":
         occ_ref, table_ref = refs.pop(0), refs.pop(0)
     y_ref = refs.pop(0)
+    if mode == "density":
+        _, _, out_hbm, dens, sems = refs
+        spans = [pl.ds(geo.own, part_rows * LANES), pl.ds(0, geo.own)]
+        copies = [
+            pltpu.make_async_copy(dens.at[:, :, span], out_hbm.at[:, :, span], sems.at[i])
+            for i, span in enumerate(spans)
+        ]
+        write_tables(geo.own, table_ref, part_rows, dens)
+        copies[0].start()
     y_ref[...] = base_ref[...]
     add_halo(geo, scale, y_ref, *halo)
     if mode == "density":
-        _, _, out_hbm, dens, sem = refs
-        write_density(y_ref, occ_ref, table_ref, part_rows, dens)
-        copy = pltpu.make_async_copy(dens, out_hbm, sem)
-        copy.start()
+        write_density(y_ref, occ_ref, dens)
+        copies[1].start()
     write_sends(geo, y_ref, reaches, refs[0], refs[1])
     if mode == "density":
-        copy.wait()
+        for copy in copies:
+            copy.wait()
 
 
 def finish_last(geo, scale, base_ref, halo, *refs):
@@ -508,7 +520,7 @@
         spread = (fg.bands * fg.domains, 1, fg.width)
         shapes.append(sds(spread, F32))
         out_specs.append(hbm)
-        scratch = [pltpu.VMEM(spread, F32), pltpu.SemaphoreType.DMA(())]
+        scratch = [pltpu.VMEM(spread, F32), pltpu.SemaphoreType.DMA((2,))]
     return vmem_call(
         functools.partial(finish_kernel, geo, scale, mode, part_rows),
         shapes,

time: 47.5 us -> 47.5 us (level)
  no operation moved by 1% of the time
where the time goes in v6:
time: 47.5 us; the launch traced here: 47.2 us
  starting transfers between devices  19.3 us (41%)
  Pallas kernels  16.9 us (36%)
  waiting for transfers between devices  9.2 us (19%)
  local copies, waits for them, and re-layouts  1.03 us (2%)
  between operations  0.86 us (2%)
    ppermute x4, starting transfers between devices, swap(): far = lax.ppermute(far, 'domain', turns)  8.54 us
    ppermute x4, waiting for transfers between devices, swap(): far = lax.ppermute(far, 'domain', turns)  8.49 us
    ppermute x2, starting transfers between devices, from_behind(): lax.ppermute(array, axis, [(i, (i + by) % length) for i in range(length)])  4.64 us
    all_to_all x1, starting transfers between devices, on_device(): dens = lax.all_to_all(spread, ('band', 'domain'), 0, 0, tiled=True)  4.52 us
    pallas_call x5, Pallas kernels, owned_part(): vmem_call(functools.partial(owned_part_kernel, geo, scale, prev is not No...  3.72 us
    pallas_call x1, Pallas kernels, field_step(): vmem_call(functools.partial(field_kernel, geo, fg, scale), [sds(y.shape,...  3.37 us
    pallas_call x3, Pallas kernels, finish(): vmem_call(functools.partial(finish_kernel, geo, scale, mode, part_rows),...  2.59 us
    pallas_call x1, Pallas kernels, own_matrices(): vmem_call(functools.partial(own_matrices_kernel, geo), shapes, [matrix_sc...  2.25 us
  transfers between devices with their start and end apart: 11, of which 5 were waited for; matrix products, arithmetic and copies ran while one was open for 0% of the time, Pallas kernels for 19%

profile of v6, /device:TPU:0, one launch (start us, length us, event | category | flops | bytes accessed | tf_op | source)
XLA Modules:
  0.0 47.2 jit_solution(17470784666167924294)
XLA Ops:
  0.6 1.3 %shard_map.122 = (bf16[464,128]{1,0:T(8,128)(2,1)S(1)}, bf16[176,128]{1,0:T(8,128)(2,1)S(1)}, f32[768,128]{1,0:T(8,128)S(1)}, s32[8,384]{1,0:T(8,128)S(1)}, bf16...) custom-call(f32[768,128]{1,0:T(8,128)} %y_hbm.1, ...), custom_call_target="tpu_custom_call" | custom-call | bytes 3000000 | tf_op jit(solution)/shard_map/pallas_call | solution.py:270
  1.9 0.5 %collective-permute-start = (bf16[464,128]{1,0:T(8,128)(2,1)S(1)}, bf16[464,128]{1,0:T(8,128)(2,1)S(1)}, u32[]{:S(2)}, u32[]{:S(2)}) collective-permute-start(bf16[464,128]{1,0:T(8,128)(2,1)S(1)} %get-tuple-element.44), channel_id=1, source_target_pairs={{0,1},{1,2},{2,3},{3,4},{4,5},{5,6},{6,7},{7,0},{8,9},{9,10},{10,1... | collective-permute-start | bytes 356360 | tf_op jit(solution)/shard_map/ppermute | solution.py:32
  2.5 4.1 %collective-permute-start.1 = (bf16[176,128]{1,0:T(8,128)(2,1)S(1)}, bf16[176,128]{1,0:T(8,128)(2,1)S(1)}, u32[]{:S(2)}, u32[]{:S(2)}) collective-permute-start(bf16[176,128]{1,0:T(8,128)(2,1)S(1)} %get-tuple-element.54.own_up_ref), channel_id=1, source_target_pairs={{0,7},{1,0},{2,1},{3,2},{4,3},{5,4},{6,5},{7,6},{8,15},{9,8},{10,9... | collective-permute-start | bytes 135176 | tf_op jit(solution)/shard_map/ppermute | solution.py:32
  6.6 2.3 %shard_map.123 = (bf16[352,352]{1,0:T(8,128)(2,1)S(1)}, bf16[368,368]{1,0:T(8,128)(2,1)S(1)}, bf16[304,304]{1,0:T(8,128)(2,1)S(1)}, bf16[192,192]{1,0:T(8,128)(2...) custom-call(s32[8,384]{1,0:T(8,128)S(1)} %get-tuple-element.47.refs_, ...), custom_call_target="tpu_custom_call" | custom-call | bytes 6000000 | tf_op jit(solution)/shard_map/pallas_call | solution.py:172
  8.8 0.0 copy-start
  8.9 0.0 copy-start.1
  8.9 0.0 copy-start.2
  8.9 0.0 copy-start.3
  8.9 0.0 copy-start.4
  8.9 0.4 shard_map.124.base_ref
  9.3 0.0 collective-permute-done.sent_ref
  9.4 1.0 %shard_map.125 = (bf16[176,176]{1,0:T(8,128)(2,1)S(1)}, bf16[176,176]{1,0:T(8,128)(2,1)S(1)}, f32[768,128]{1,0:T(8,128)S(1)}) custom-call(bf16[464,128]{1,0:T(8,128)(2,1)S(1)} %collective-permute-done.sent_ref, bf16[343,343]{1,0:T(8,128)(2,1)S(1)} %get-tuple-element.45.refs_1_.matrix_ref, f32[768,128]{1,0:T(8,128)S(1)} %shard_map.124.base_ref, ...), custom_call_target="tpu_custom_call" | custom-call | bytes 3000000 | tf_op jit(solution)/shard_map/pallas_call | solution.py:413
  10.4 0.0 collective-permute-done.1.refs_1_
  10.4 0.5 shard_map.126
  10.8 0.1 collective-permute-start.2
  10.9 2.3 %collective-permute-start.3 = (bf16[176,128]{1,0:T(8,128)(2,1)S(1)}, bf16[176,128]{1,0:T(8,128)(2,1)S(1)}, u32[]{:S(2)}, u32[]{:S(2)}) collective-permute-start(bf16[176,128]{1,0:T(8,128)(2,1)S(1)} %get-tuple-element.64), channel_id=1, source_target_pairs={{0,7},{1,2},{2,1},{3,4},{4,3},{5,6},{6,5},{7,0},{8,15},{9,10},{10,... | collective-permute-start | bytes 135176 | tf_op jit(solution)/shard_map/ppermute | solution.py:977
  13.2 0.5 %shard_map.127.refs_0_.refs_4_ = f32[768,128]{1,0:T(8,128)S(1)} custom-call(f32[768,128]{1,0:T(8,128)S(1)} %get-tuple-element.60.refs_0_.refs_1_, f32[768,128]{1,0:T(8,128)S(1)} %get-tuple-element.46.refs_0_.refs_1_, f32[768,128]{1,0:T(8,128)S(1)} %get-tuple-element.49.refs_1_.refs_2_, bf16[352,352]{1,0:T(8,128)(2,1)S(1)} %get-tuple-element.50.refs_2_.refs_3_.refs_4_, ...), custom_call_target="tpu_custom_call" | custom-call | bytes 6000000 | tf_op jit(solution)/shard_map/pallas_call | solution.py:345
  13.7 0.0 collective-permute-done.2.refs_1_
  13.8 2.5 %collective-permute-done.3.refs_2_ = bf16[176,128]{1,0:T(8,128)(2,1)S(1)} collective-permute-done((bf16[176,128]{1,0:T(8,128)(2,1)S(1)}, bf16[176,128]{1,0:T(8,128)(2,1)S(1)}, u32[]{:S(2)}, u32[]{:S(2)}) %collective-permute-start.3) | collective-permute-done | bytes 45088 | tf_op jit(solution)/shard_map/ppermute | solution.py:977
  16.2 0.5 shard_map.128
  16.7 0.1 collective-permute-start.4
  16.8 2.3 %collective-permute-start.5 = (bf16[176,128]{1,0:T(8,128)(2,1)S(1)}, bf16[176,128]{1,0:T(8,128)(2,1)S(1)}, u32[]{:S(2)}, u32[]{:S(2)}) collective-permute-start(bf16[176,128]{1,0:T(8,128)(2,1)S(1)} %get-tuple-element.67), channel_id=1, source_target_pairs={{0,7},{1,2},{2,1},{3,4},{4,3},{5,6},{6,5},{7,0},{8,15},{9,10},{10,... | collective-permute-start | bytes 135176 | tf_op jit(solution)/shard_map/ppermute | solution.py:977
  19.1 0.5 %shard_map.130.refs_8_ = f32[4,8,128]{2,1,0:T(8,128)S(1)} custom-call(s32[2,729]{1,0:T(2,128)S(1)} %get-tuple-element.69.refs_0_, s32[1,81]{1,0:T(1,128)S(1)} %get-tuple-element.70.refs_1_, s32[1,8]{1,0:T(1,128)S(1)} %get-tuple-element.71.refs_2_, f32[6,128]{1,0:T(8,128)S(1)} %get-tuple-element.72.refs_3_, f32[768,128]{1,0:T(8,128)S(1)} %shard_map.127.refs_0_.refs_4_), custom_call_target="tpu_custom_call" | custom-call | bytes 3000000 | tf_op jit(solution)/shard_map/pallas_call | solution.py:629
  19.7 0.5 %shard_map.129.refs_0_ = f32[768,128]{1,0:T(8,128)S(1)} custom-call(f32[768,128]{1,0:T(8,128)S(1)} %get-tuple-element.65.refs_0_, f32[768,128]{1,0:T(8,128)S(1)} %get-tuple-element.60.refs_0_.refs_1_, f32[768,128]{1,0:T(8,128)S(1)} %get-tuple-element.49.refs_1_.refs_2_, bf16[352,352]{1,0:T(8,128)(2,1)S(1)} %get-tuple-element.50.refs_2_.refs_3_.refs_4_, ...), custom_call_target="tpu_custom_call" | custom-call | bytes 6000000 | tf_op jit(solution)/shard_map/pallas_call | solution.py:345
  20.2 0.0 collective-permute-done.4.refs_1_
  20.2 2.0 %collective-permute-done.5.refs_2_ = bf16[176,128]{1,0:T(8,128)(2,1)S(1)} collective-permute-done((bf16[176,128]{1,0:T(8,128)(2,1)S(1)}, bf16[176,128]{1,0:T(8,128)(2,1)S(1)}, u32[]{:S(2)}, u32[]{:S(2)}) %collective-permute-start.5) | collective-permute-done | bytes 45088 | tf_op jit(solution)/shard_map/ppermute | solution.py:977
  22.1 1.2 %shard_map.131 = (f32[768,128]{1,0:T(8,128)S(1)}, bf16[176,128]{1,0:T(8,128)(2,1)S(1)}, bf16[176,128]{1,0:T(8,128)(2,1)S(1)}, f32[32,1,1408]{2,1,0:T(1,128)}) custom-call(f32[768,128]{1,0:T(8,128)S(1)} %shard_map.129.refs_0_, bf16[176,128]{1,0:T(8,128)(2,1)S(1)} %collective-permute-done.4.refs_1_, bf16[176,128]{1,0:T(8,128)(2,1)S(1)} %collective-permute-done.5.refs_2_, ...), custom_call_target="tpu_custom_call" | custom-call | bytes 3000000 | tf_op jit(solution)/shard_map/pallas_call | solution.py:524
  23.3 4.5 %all-to-all-start = ((f32[32,1,1408]{2,1,0:T(1,128)}), f32[32,1,1408]{2,1,0:T(1,128)S(1)}, u32[]{:S(2)}, u32[]{:S(2)}) async-start(f32[32,1,1408]{2,1,0:T(1,128)} %get-tuple-element.73), calls=%async_computation | async-start | bytes 360448 | tf_op jit(solution)/shard_map/all_to_all | solution.py:947
  27.8 0.3 collective-permute-start.6
  28.1 3.5 %collective-permute-start.7 = (bf16[176,128]{1,0:T(8,128)(2,1)S(1)}, bf16[176,128]{1,0:T(8,128)(2,1)S(1)}, u32[]{:S(2)}, u32[]{:S(2)}) collective-permute-start(bf16[176,128]{1,0:T(8,128)(2,1)S(1)} %get-tuple-element.78), channel_id=1, source_target_pairs={{0,7},{1,2},{2,1},{3,4},{4,3},{5,6},{6,5},{7,0},{8,15},{9,10},{10,... | collective-permute-start | bytes 135176 | tf_op jit(solution)/shard_map/ppermute | solution.py:977
  31.6 0.0 copy-done
  31.6 0.0 copy-done.1
  31.6 0.0 copy-done.2
  31.6 0.0 copy-done.3
  31.6 0.0 copy-done.4
  31.6 0.5 %shard_map.132.after_ref.base_ref = f32[768,128]{1,0:T(8,128)S(1)} custom-call(f32[768,128]{1,0:T(8,128)S(1)} %get-tuple-element.74.refs_0_.y_ref.refs_1_, f32[768,128]{1,0:T(8,128)S(1)} %get-tuple-element.49.refs_1_.refs_2_, bf16[352,352]{1,0:T(8,128)(2,1)S(1)} %get-tuple-element.50.refs_2_.refs_3_.refs_4_, ...), custom_call_target="tpu_custom_call" | custom-call | bytes 6000000 | tf_op jit(solution)/shard_map/pallas_call | solution.py:345
  32.1 1.7 %shard_map.133 = (bf16[729,729]{1,0:T(8,128)(2,1)S(1)}, bf16[729,729]{1,0:T(8,128)(2,1)S(1)}) custom-call(f32[729,729]{1,0:T(8,128)} %matrix_hbm.1, f32[768,128]{1,0:T(8,128)S(1)} %shard_map.132.after_ref.base_ref), custom_call_target="tpu_custom_call" | custom-call | bytes 7500000 | tf_op jit(solution)/shard_map/pallas_call | solution.py:772
  33.8 1.0 %copy-done.5 = bf16[729,729]{1,0:T(8,128)(2,1)} copy-done((bf16[729,729]{1,0:T(8,128)(2,1)}, bf16[729,729]{1,0:T(8,128)(2,1)S(1)}, u32[]{:S(2)}) %copy-start.5) | copy-done | bytes 1062906
  34.8 0.0 collective-permute-done.6.near_ref
  34.8 1.0 %collective-permute-done.7.far_ref = bf16[176,128]{1,0:T(8,128)(2,1)S(1)} collective-permute-done((bf16[176,128]{1,0:T(8,128)(2,1)S(1)}, bf16[176,128]{1,0:T(8,128)(2,1)S(1)}, u32[]{:S(2)}, u32[]{:S(2)}) %collective-permute-start.7) | collective-permute-done | bytes 45088 | tf_op jit(solution)/shard_map/ppermute | solution.py:977
  35.8 0.7 %all-to-all-done = f32[32,1,1408]{2,1,0:T(1,128)S(1)} async-done(((f32[32,1,1408]{2,1,0:T(1,128)}), f32[32,1,1408]{2,1,0:T(1,128)S(1)}, u32[]{:S(2)}, u32[]{:S(2)}) %all-to-all-start) | async-done | bytes 180256 | tf_op jit(solution)/shard_map/all_to_all | solution.py:947
  36.5 3.4 %shard_map.134 = (f32[768,128]{1,0:T(8,128)S(1)}, bf16[176,128]{1,0:T(8,128)(2,1)S(1)}, bf16[176,128]{1,0:T(8,128)(2,1)S(1)}, f32[768,128]{1,0:T(8,128)S(1)}, f32[6,128]{1,0:T(8,128)S(1)}) custom-call(f32[352,128]{1,0:T(8,128)S(1)} %bitcast.5, bf16[729,729]{1,0:T(8,128)(2,1)} %copy-done.5, bf16[729,729]{1,0:T(8,128)(2,1)S(1)} %get-tuple-element.76.high_ref, ...), custom_call_target="tpu_custom_call" | custom-call | bytes 12000000 | tf_op jit(solution)/shard_map/pallas_call | solution.py:815
  39.9 1.1 %collective-permute-start.8 = (bf16[176,128]{1,0:T(8,128)(2,1)S(1)}, bf16[176,128]{1,0:T(8,128)(2,1)S(1)}, u32[]{:S(2)}, u32[]{:S(2)}) collective-permute-start(bf16[176,128]{1,0:T(8,128)(2,1)S(1)} %get-tuple-element.81), channel_id=1, source_target_pairs={{0,1},{1,0},{2,3},{3,2},{4,5},{5,4},{6,7},{7,6},{8,9},{9,8},{10,11... | collective-permute-start | bytes 135176 | tf_op jit(solution)/shard_map/ppermute | solution.py:978
  41.0 0.4 collective-permute-start.9
  41.4 1.8 %shard_map.135.refs_0_ = f32[768,128]{1,0:T(8,128)S(1)} custom-call(f32[768,128]{1,0:T(8,128)S(1)} %get-tuple-element.79.refs_0_, f32[768,128]{1,0:T(8,128)S(1)} %get-tuple-element.74.refs_0_.y_ref.refs_1_, f32[768,128]{1,0:T(8,128)} %copy-done, f32[768,128]{1,0:T(8,128)S(1)} %get-tuple-element.80.refs_3_, bf16[352,352]{1,0:T(8,128)(2,1)} %copy-done.2, ...), custom_call_target="tpu_custom_call" | custom-call | bytes 6000000 | tf_op jit(solution)/shard_map/pallas_call | solution.py:345
  43.2 0.0 collective-permute-done.8.refs_1_
  43.2 3.1 %collective-permute-done.9.refs_2_ = bf16[176,128]{1,0:T(8,128)(2,1)S(1)} collective-permute-done((bf16[176,128]{1,0:T(8,128)(2,1)S(1)}, bf16[176,128]{1,0:T(8,128)(2,1)S(1)}, u32[]{:S(2)}, u32[]{:S(2)}) %collective-permute-start.9) | collective-permute-done | bytes 45088 | tf_op jit(solution)/shard_map/ppermute | solution.py:977
  46.3 1.0 %shard_map.136 = (f32[768,128]{1,0:T(8,128)}, f32[6,128]{1,0:T(8,128)}) custom-call(f32[768,128]{1,0:T(8,128)S(1)} %shard_map.135.refs_0_, bf16[176,128]{1,0:T(8,128)(2,1)S(1)} %collective-permute-done.8.refs_1_, bf16[176,128]{1,0:T(8,128)(2,1)S(1)} %collective-permute-done.9.refs_2_, bf16[304,176]{1,0:T(8,128)(2,1)S(1)} %get-tuple-element.56.refs_2_.refs_3_.refs_0_, ...), custom_call_target="tpu_custom_call" | custom-call | bytes 3000000 | tf_op jit(solution)/shard_map/pallas_call | solution.py:524
  (1 shorter events, 0.0 us)
Async XLA Ops:
  1.9 7.4 %collective-permute-start = (bf16[464,128]{1,0:T(8,128)(2,1)S(1)}, bf16[464,128]{1,0:T(8,128)(2,1)S(1)}, u32[]{:S(2)}, u32[]{:S(2)}) collective-permute-start(bf16[464,128]{1,0:T(8,128)(2,1)S(1)} %get-tuple-element.44), channel_id=1, source_target_pairs={{0,1},{1,2},{2,3},{3,4},{4,5},{5,6},{6,7},{7,0},{8,9},{9,10},{10,1... | collective-permute-start | bytes 356360 | tf_op jit(solution)/shard_map/ppermute | solution.py:32
  2.5 7.9 %collective-permute-start.1 = (bf16[176,128]{1,0:T(8,128)(2,1)S(1)}, bf16[176,128]{1,0:T(8,128)(2,1)S(1)}, u32[]{:S(2)}, u32[]{:S(2)}) collective-permute-start(bf16[176,128]{1,0:T(8,128)(2,1)S(1)} %get-tuple-element.54.own_up_ref), channel_id=1, source_target_pairs={{0,7},{1,0},{2,1},{3,2},{4,3},{5,4},{6,5},{7,6},{8,15},{9,8},{10,9... | collective-permute-start | bytes 135176 | tf_op jit(solution)/shard_map/ppermute | solution.py:32
  8.8 22.8 %copy-start = (f32[768,128]{1,0:T(8,128)}, f32[768,128]{1,0:T(8,128)S(1)}, u32[]{:S(2)}) copy-start(f32[768,128]{1,0:T(8,128)S(1)} %get-tuple-element.49.refs_1_.refs_2_) | copy-start | bytes 1179652
  8.9 22.8 %copy-start.1 = (bf16[368,368]{1,0:T(8,128)(2,1)}, bf16[368,368]{1,0:T(8,128)(2,1)S(1)}, u32[]{:S(2)}) copy-start(bf16[368,368]{1,0:T(8,128)(2,1)S(1)} %get-tuple-element.51.refs_3_.refs_4_.refs_5_) | copy-start | bytes 812548
  8.9 22.8 %copy-start.2 = (bf16[352,352]{1,0:T(8,128)(2,1)}, bf16[352,352]{1,0:T(8,128)(2,1)S(1)}, u32[]{:S(2)}) copy-start(bf16[352,352]{1,0:T(8,128)(2,1)S(1)} %get-tuple-element.50.refs_2_.refs_3_.refs_4_) | copy-start | bytes 743428
  8.9 22.7 %copy-start.3 = (bf16[304,304]{1,0:T(8,128)(2,1)}, bf16[304,304]{1,0:T(8,128)(2,1)S(1)}, u32[]{:S(2)}) copy-start(bf16[304,304]{1,0:T(8,128)(2,1)S(1)} %get-tuple-element.52.refs_4_.refs_5_.refs_6_) | copy-start | bytes 554500
  8.9 22.7 %copy-start.4 = (bf16[192,192]{1,0:T(8,128)(2,1)}, bf16[192,192]{1,0:T(8,128)(2,1)S(1)}, u32[]{:S(2)}) copy-start(bf16[192,192]{1,0:T(8,128)(2,1)S(1)} %get-tuple-element.53.refs_5_.refs_6_.refs_7_) | copy-start | bytes 221188
  10.8 2.9 %collective-permute-start.2 = (bf16[176,128]{1,0:T(8,128)(2,1)S(1)}, bf16[176,128]{1,0:T(8,128)(2,1)S(1)}, u32[]{:S(2)}, u32[]{:S(2)}) collective-permute-start(bf16[176,128]{1,0:T(8,128)(2,1)S(1)} %get-tuple-element.63), channel_id=1, source_target_pairs={{0,1},{1,0},{2,3},{3,2},{4,5},{5,4},{6,7},{7,6},{8,9},{9,8},{10,11... | collective-permute-start | bytes 135176 | tf_op jit(solution)/shard_map/ppermute | solution.py:978
  10.9 5.3 %collective-permute-start.3 = (bf16[176,128]{1,0:T(8,128)(2,1)S(1)}, bf16[176,128]{1,0:T(8,128)(2,1)S(1)}, u32[]{:S(2)}, u32[]{:S(2)}) collective-permute-start(bf16[176,128]{1,0:T(8,128)(2,1)S(1)} %get-tuple-element.64), channel_id=1, source_target_pairs={{0,7},{1,2},{2,1},{3,4},{4,3},{5,6},{6,5},{7,0},{8,15},{9,10},{10,... | collective-permute-start | bytes 135176 | tf_op jit(solution)/shard_map/ppermute | solution.py:977
  16.7 3.5 %collective-permute-start.4 = (bf16[176,128]{1,0:T(8,128)(2,1)S(1)}, bf16[176,128]{1,0:T(8,128)(2,1)S(1)}, u32[]{:S(2)}, u32[]{:S(2)}) collective-permute-start(bf16[176,128]{1,0:T(8,128)(2,1)S(1)} %get-tuple-element.66), channel_id=1, source_target_pairs={{0,1},{1,0},{2,3},{3,2},{4,5},{5,4},{6,7},{7,6},{8,9},{9,8},{10,11... | collective-permute-start | bytes 135176 | tf_op jit(solution)/shard_map/ppermute | solution.py:978
  16.8 5.3 %collective-permute-start.5 = (bf16[176,128]{1,0:T(8,128)(2,1)S(1)}, bf16[176,128]{1,0:T(8,128)(2,1)S(1)}, u32[]{:S(2)}, u32[]{:S(2)}) collective-permute-start(bf16[176,128]{1,0:T(8,128)(2,1)S(1)} %get-tuple-element.67), channel_id=1, source_target_pairs={{0,7},{1,2},{2,1},{3,4},{4,3},{5,6},{6,5},{7,0},{8,15},{9,10},{10,... | collective-permute-start | bytes 135176 | tf_op jit(solution)/shard_map/ppermute | solution.py:977
  23.3 13.2 %all-to-all-start = ((f32[32,1,1408]{2,1,0:T(1,128)}), f32[32,1,1408]{2,1,0:T(1,128)S(1)}, u32[]{:S(2)}, u32[]{:S(2)}) async-start(f32[32,1,1408]{2,1,0:T(1,128)} %get-tuple-element.73), calls=%async_computation | async-start | bytes 360448 | tf_op jit(solution)/shard_map/all_to_all | solution.py:947
  27.8 7.0 %collective-permute-start.6 = (bf16[176,128]{1,0:T(8,128)(2,1)S(1)}, bf16[176,128]{1,0:T(8,128)(2,1)S(1)}, u32[]{:S(2)}, u32[]{:S(2)}) collective-permute-start(bf16[176,128]{1,0:T(8,128)(2,1)S(1)} %get-tuple-element.77), channel_id=1, source_target_pairs={{0,1},{1,0},{2,3},{3,2},{4,5},{5,4},{6,7},{7,6},{8,9},{9,8},{10,11... | collective-permute-start | bytes 135176 | tf_op jit(solution)/shard_map/ppermute | solution.py:978
  28.1 7.7 %collective-permute-start.7 = (bf16[176,128]{1,0:T(8,128)(2,1)S(1)}, bf16[176,128]{1,0:T(8,128)(2,1)S(1)}, u32[]{:S(2)}, u32[]{:S(2)}) collective-permute-start(bf16[176,128]{1,0:T(8,128)(2,1)S(1)} %get-tuple-element.78), channel_id=1, source_target_pairs={{0,7},{1,2},{2,1},{3,4},{4,3},{5,6},{6,5},{7,0},{8,15},{9,10},{10,... | collective-permute-start | bytes 135176 | tf_op jit(solution)/shard_map/ppermute | solution.py:977
  33.8 1.0 %copy-start.5 = (bf16[729,729]{1,0:T(8,128)(2,1)}, bf16[729,729]{1,0:T(8,128)(2,1)S(1)}, u32[]{:S(2)}) copy-start(bf16[729,729]{1,0:T(8,128)(2,1)S(1)} %get-tuple-element.75.low_hbm) | copy-start | bytes 3188650
  39.9 3.3 %collective-permute-start.8 = (bf16[176,128]{1,0:T(8,128)(2,1)S(1)}, bf16[176,128]{1,0:T(8,128)(2,1)S(1)}, u32[]{:S(2)}, u32[]{:S(2)}) collective-permute-start(bf16[176,128]{1,0:T(8,128)(2,1)S(1)} %get-tuple-element.81), channel_id=1, source_target_pairs={{0,1},{1,0},{2,3},{3,2},{4,5},{5,4},{6,7},{7,6},{8,9},{9,8},{10,11... | collective-permute-start | bytes 135176 | tf_op jit(solution)/shard_map/ppermute | solution.py:978
  41.0 5.3 %collective-permute-start.9 = (bf16[176,128]{1,0:T(8,128)(2,1)S(1)}, bf16[176,128]{1,0:T(8,128)(2,1)S(1)}, u32[]{:S(2)}, u32[]{:S(2)}) collective-permute-start(bf16[176,128]{1,0:T(8,128)(2,1)S(1)} %get-tuple-element.82), channel_id=1, source_target_pairs={{0,7},{1,2},{2,1},{3,4},{4,3},{5,6},{6,5},{7,0},{8,15},{9,10},{10,... | collective-permute-start | bytes 135176 | tf_op jit(solution)/shard_map/ppermute | solution.py:977

commit v7 on v6

--- a/solution.py
+++ b/solution.py
@@ -245,12 +245,16 @@
     kept, (nodes, face, faces, sems) = refs[4 : 4 + extra], refs[4 + extra :]
     cuts = sorted({0, max(geo.sp, geo.low), geo.dn_lo, geo.own})
     spans = list(zip(cuts[:-1], cuts[1:]))
-    pairs = [(nodes_hbm, nodes), (face_hbm, face)]
-    pairs += [(y_hbm.at[pl.ds(a, b - a)], y.at[pl.ds(a, b - a)]) for a, b in spans]
+    pairs = [(y_hbm.at[pl.ds(a, b - a)], y.at[pl.ds(a, b - a)]) for a, b in spans]
+    pairs += [(nodes_hbm, nodes), (face_hbm, face)]
     pairs += list(zip(sources, kept))
     copies = fetch(pairs, sems)
-    copies[0].wait()
-    copies[1].wait()
+    first = len(spans)
+    for copy in copies[:first]:
+        copy.wait()
+    write_rows(geo, y, dn_ref, up_ref)
+    for copy in copies[first : first + 2]:
+        copy.wait()
     place_table(geo, nodes, face, table, faces)
     for t in range(geo.table_tiles):
         at = geo.dn_rows + 2 * t * geo.table_rows
@@ -259,9 +263,8 @@
         low = jnp.bitwise_and(value, LANES - 1).astype(F32)
         digits = jnp.concatenate([high, low], axis=0).astype(BF)
         dn_ref[at : at + 2 * geo.table_rows, :] = digits
-    for copy in copies[2:]:
+    for copy in copies[first + 2 :]:
         copy.wait()
-    write_rows(geo, y, dn_ref, up_ref)
 
 
 def pack(geo, y, cell_nodes, face_order, *others):

time: 47.5 us -> 47.5 us (level)
  no operation moved by 1% of the time
where the time goes in v7:
time: 47.5 us; the launch traced here: 47.2 us
  starting transfers between devices  19.3 us (41%)
  Pallas kernels  16.9 us (36%)
  waiting for transfers between devices  9.2 us (19%)
  local copies, waits for them, and re-layouts  1.03 us (2%)
  between operations  0.86 us (2%)
    ppermute x4, starting transfers between devices, swap(): far = lax.ppermute(far, 'domain', turns)  8.54 us
    ppermute x4, waiting for transfers between devices, swap(): far = lax.ppermute(far, 'domain', turns)  8.49 us
    ppermute x2, starting transfers between devices, from_behind(): lax.ppermute(array, axis, [(i, (i + by) % length) for i in range(length)])  4.64 us
    all_to_all x1, starting transfers between devices, on_device(): dens = lax.all_to_all(spread, ('band', 'domain'), 0, 0, tiled=True)  4.5 us
    pallas_call x5, Pallas kernels, owned_part(): vmem_call(functools.partial(owned_part_kernel, geo, scale, prev is not No...  3.72 us
    pallas_call x1, Pallas kernels, field_step(): vmem_call(functools.partial(field_kernel, geo, fg, scale), [sds(y.shape,...  3.37 us
    pallas_call x3, Pallas kernels, finish(): vmem_call(functools.partial(finish_kernel, geo, scale, mode, part_rows),...  2.59 us
    pallas_call x1, Pallas kernels, own_matrices(): vmem_call(functools.partial(own_matrices_kernel, geo), shapes, [matrix_sc...  2.26 us
  transfers between devices with their start and end apart: 11, of which 5 were waited for; matrix products, arithmetic and copies ran while one was open for 0% of the time, Pallas kernels for 19%

profile of v7, /device:TPU:0, one launch (start us, length us, event | category | flops | bytes accessed | tf_op | source)
XLA Modules:
  0.0 47.2 jit_solution(5160919515203978492)
XLA Ops:
  0.6 1.3 %shard_map.122 = (bf16[464,128]{1,0:T(8,128)(2,1)S(1)}, bf16[176,128]{1,0:T(8,128)(2,1)S(1)}, f32[768,128]{1,0:T(8,128)S(1)}, s32[8,384]{1,0:T(8,128)S(1)}, bf16...) custom-call(f32[768,128]{1,0:T(8,128)} %y_hbm.1, ...), custom_call_target="tpu_custom_call" | custom-call | bytes 3000000 | tf_op jit(solution)/shard_map/pallas_call | solution.py:273
  1.9 0.5 %collective-permute-start = (bf16[464,128]{1,0:T(8,128)(2,1)S(1)}, bf16[464,128]{1,0:T(8,128)(2,1)S(1)}, u32[]{:S(2)}, u32[]{:S(2)}) collective-permute-start(bf16[464,128]{1,0:T(8,128)(2,1)S(1)} %get-tuple-element.44), channel_id=1, source_target_pairs={{0,1},{1,2},{2,3},{3,4},{4,5},{5,6},{6,7},{7,0},{8,9},{9,10},{10,1... | collective-permute-start | bytes 356360 | tf_op jit(solution)/shard_map/ppermute | solution.py:32
  2.5 4.1 %collective-permute-start.1 = (bf16[176,128]{1,0:T(8,128)(2,1)S(1)}, bf16[176,128]{1,0:T(8,128)(2,1)S(1)}, u32[]{:S(2)}, u32[]{:S(2)}) collective-permute-start(bf16[176,128]{1,0:T(8,128)(2,1)S(1)} %get-tuple-element.54.own_up_ref), channel_id=1, source_target_pairs={{0,7},{1,0},{2,1},{3,2},{4,3},{5,4},{6,5},{7,6},{8,15},{9,8},{10,9... | collective-permute-start | bytes 135176 | tf_op jit(solution)/shard_map/ppermute | solution.py:32
  6.6 2.3 %shard_map.123 = (bf16[352,352]{1,0:T(8,128)(2,1)S(1)}, bf16[368,368]{1,0:T(8,128)(2,1)S(1)}, bf16[304,304]{1,0:T(8,128)(2,1)S(1)}, bf16[192,192]{1,0:T(8,128)(2...) custom-call(s32[8,384]{1,0:T(8,128)S(1)} %get-tuple-element.47.refs_, ...), custom_call_target="tpu_custom_call" | custom-call | bytes 6000000 | tf_op jit(solution)/shard_map/pallas_call | solution.py:172
  8.8 0.0 copy-start
  8.9 0.0 copy-start.1
  8.9 0.0 copy-start.2
  8.9 0.0 copy-start.3
  8.9 0.0 copy-start.4
  8.9 0.4 shard_map.124.base_ref
  9.3 0.0 collective-permute-done.sent_ref
  9.4 1.0 %shard_map.125 = (bf16[176,176]{1,0:T(8,128)(2,1)S(1)}, bf16[176,176]{1,0:T(8,128)(2,1)S(1)}, f32[768,128]{1,0:T(8,128)S(1)}) custom-call(bf16[464,128]{1,0:T(8,128)(2,1)S(1)} %collective-permute-done.sent_ref, bf16[343,343]{1,0:T(8,128)(2,1)S(1)} %get-tuple-element.45.refs_1_.matrix_ref, f32[768,128]{1,0:T(8,128)S(1)} %shard_map.124.base_ref, ...), custom_call_target="tpu_custom_call" | custom-call | bytes 3000000 | tf_op jit(solution)/shard_map/pallas_call | solution.py:416
  10.4 0.0 collective-permute-done.1.refs_1_
  10.4 0.5 shard_map.126
  10.8 0.1 collective-permute-start.2
  10.9 2.3 %collective-permute-start.3 = (bf16[176,128]{1,0:T(8,128)(2,1)S(1)}, bf16[176,128]{1,0:T(8,128)(2,1)S(1)}, u32[]{:S(2)}, u32[]{:S(2)}) collective-permute-start(bf16[176,128]{1,0:T(8,128)(2,1)S(1)} %get-tuple-element.64), channel_id=1, source_target_pairs={{0,7},{1,2},{2,1},{3,4},{4,3},{5,6},{6,5},{7,0},{8,15},{9,10},{10,... | collective-permute-start | bytes 135176 | tf_op jit(solution)/shard_map/ppermute | solution.py:980
  13.2 0.5 %shard_map.127.refs_0_.refs_4_ = f32[768,128]{1,0:T(8,128)S(1)} custom-call(f32[768,128]{1,0:T(8,128)S(1)} %get-tuple-element.60.refs_0_.refs_1_, f32[768,128]{1,0:T(8,128)S(1)} %get-tuple-element.46.refs_0_.refs_1_, f32[768,128]{1,0:T(8,128)S(1)} %get-tuple-element.49.refs_1_.refs_2_, bf16[352,352]{1,0:T(8,128)(2,1)S(1)} %get-tuple-element.50.refs_2_.refs_3_.refs_4_, ...), custom_call_target="tpu_custom_call" | custom-call | bytes 6000000 | tf_op jit(solution)/shard_map/pallas_call | solution.py:348
  13.7 0.0 collective-permute-done.2.refs_1_
  13.8 2.5 %collective-permute-done.3.refs_2_ = bf16[176,128]{1,0:T(8,128)(2,1)S(1)} collective-permute-done((bf16[176,128]{1,0:T(8,128)(2,1)S(1)}, bf16[176,128]{1,0:T(8,128)(2,1)S(1)}, u32[]{:S(2)}, u32[]{:S(2)}) %collective-permute-start.3) | collective-permute-done | bytes 45088 | tf_op jit(solution)/shard_map/ppermute | solution.py:980
  16.2 0.5 shard_map.128
  16.7 0.1 collective-permute-start.4
  16.8 2.3 %collective-permute-start.5 = (bf16[176,128]{1,0:T(8,128)(2,1)S(1)}, bf16[176,128]{1,0:T(8,128)(2,1)S(1)}, u32[]{:S(2)}, u32[]{:S(2)}) collective-permute-start(bf16[176,128]{1,0:T(8,128)(2,1)S(1)} %get-tuple-element.67), channel_id=1, source_target_pairs={{0,7},{1,2},{2,1},{3,4},{4,3},{5,6},{6,5},{7,0},{8,15},{9,10},{10,... | collective-permute-start | bytes 135176 | tf_op jit(solution)/shard_map/ppermute | solution.py:980
  19.1 0.5 %shard_map.130.refs_8_ = f32[4,8,128]{2,1,0:T(8,128)S(1)} custom-call(s32[2,729]{1,0:T(2,128)S(1)} %get-tuple-element.69.refs_0_, s32[1,81]{1,0:T(1,128)S(1)} %get-tuple-element.70.refs_1_, s32[1,8]{1,0:T(1,128)S(1)} %get-tuple-element.71.refs_2_, f32[6,128]{1,0:T(8,128)S(1)} %get-tuple-element.72.refs_3_, f32[768,128]{1,0:T(8,128)S(1)} %shard_map.127.refs_0_.refs_4_), custom_call_target="tpu_custom_call" | custom-call | bytes 3000000 | tf_op jit(solution)/shard_map/pallas_call | solution.py:632
  19.7 0.5 %shard_map.129.refs_0_ = f32[768,128]{1,0:T(8,128)S(1)} custom-call(f32[768,128]{1,0:T(8,128)S(1)} %get-tuple-element.65.refs_0_, f32[768,128]{1,0:T(8,128)S(1)} %get-tuple-element.60.refs_0_.refs_1_, f32[768,128]{1,0:T(8,128)S(1)} %get-tuple-element.49.refs_1_.refs_2_, bf16[352,352]{1,0:T(8,128)(2,1)S(1)} %get-tuple-element.50.refs_2_.refs_3_.refs_4_, ...), custom_call_target="tpu_custom_call" | custom-call | bytes 6000000 | tf_op jit(solution)/shard_map/pallas_call | solution.py:348
  20.2 0.0 collective-permute-done.4.refs_1_
  20.2 2.0 %collective-permute-done.5.refs_2_ = bf16[176,128]{1,0:T(8,128)(2,1)S(1)} collective-permute-done((bf16[176,128]{1,0:T(8,128)(2,1)S(1)}, bf16[176,128]{1,0:T(8,128)(2,1)S(1)}, u32[]{:S(2)}, u32[]{:S(2)}) %collective-permute-start.5) | collective-permute-done | bytes 45088 | tf_op jit(solution)/shard_map/ppermute | solution.py:980
  22.1 1.2 %shard_map.131 = (f32[768,128]{1,0:T(8,128)S(1)}, bf16[176,128]{1,0:T(8,128)(2,1)S(1)}, bf16[176,128]{1,0:T(8,128)(2,1)S(1)}, f32[32,1,1408]{2,1,0:T(1,128)}) custom-call(f32[768,128]{1,0:T(8,128)S(1)} %shard_map.129.refs_0_, bf16[176,128]{1,0:T(8,128)(2,1)S(1)} %collective-permute-done.4.refs_1_, bf16[176,128]{1,0:T(8,128)(2,1)S(1)} %collective-permute-done.5.refs_2_, ...), custom_call_target="tpu_custom_call" | custom-call | bytes 3000000 | tf_op jit(solution)/shard_map/pallas_call | solution.py:527
  23.3 4.5 %all-to-all-start = ((f32[32,1,1408]{2,1,0:T(1,128)}), f32[32,1,1408]{2,1,0:T(1,128)S(1)}, u32[]{:S(2)}, u32[]{:S(2)}) async-start(f32[32,1,1408]{2,1,0:T(1,128)} %get-tuple-element.73), calls=%async_computation | async-start | bytes 360448 | tf_op jit(solution)/shard_map/all_to_all | solution.py:950
  27.8 0.3 collective-permute-start.6
  28.1 3.5 %collective-permute-start.7 = (bf16[176,128]{1,0:T(8,128)(2,1)S(1)}, bf16[176,128]{1,0:T(8,128)(2,1)S(1)}, u32[]{:S(2)}, u32[]{:S(2)}) collective-permute-start(bf16[176,128]{1,0:T(8,128)(2,1)S(1)} %get-tuple-element.78), channel_id=1, source_target_pairs={{0,7},{1,2},{2,1},{3,4},{4,3},{5,6},{6,5},{7,0},{8,15},{9,10},{10,... | collective-permute-start | bytes 135176 | tf_op jit(solution)/shard_map/ppermute | solution.py:980
  31.6 0.0 copy-done
  31.6 0.0 copy-done.1
  31.6 0.0 copy-done.2
  31.6 0.0 copy-done.3
  31.6 0.0 copy-done.4
  31.6 0.5 %shard_map.132.after_ref.base_ref = f32[768,128]{1,0:T(8,128)S(1)} custom-call(f32[768,128]{1,0:T(8,128)S(1)} %get-tuple-element.74.refs_0_.y_ref.refs_1_, f32[768,128]{1,0:T(8,128)S(1)} %get-tuple-element.49.refs_1_.refs_2_, bf16[352,352]{1,0:T(8,128)(2,1)S(1)} %get-tuple-element.50.refs_2_.refs_3_.refs_4_, ...), custom_call_target="tpu_custom_call" | custom-call | bytes 6000000 | tf_op jit(solution)/shard_map/pallas_call | solution.py:348
  32.1 1.7 %shard_map.133 = (bf16[729,729]{1,0:T(8,128)(2,1)S(1)}, bf16[729,729]{1,0:T(8,128)(2,1)S(1)}) custom-call(f32[729,729]{1,0:T(8,128)} %matrix_hbm.1, f32[768,128]{1,0:T(8,128)S(1)} %shard_map.132.after_ref.base_ref), custom_call_target="tpu_custom_call" | custom-call | bytes 7500000 | tf_op jit(solution)/shard_map/pallas_call | solution.py:775
  33.8 1.0 %copy-done.5 = bf16[729,729]{1,0:T(8,128)(2,1)} copy-done((bf16[729,729]{1,0:T(8,128)(2,1)}, bf16[729,729]{1,0:T(8,128)(2,1)S(1)}, u32[]{:S(2)}) %copy-start.5) | copy-done | bytes 1062906
  34.8 0.0 collective-permute-done.6.near_ref
  34.8 1.0 %collective-permute-done.7.far_ref = bf16[176,128]{1,0:T(8,128)(2,1)S(1)} collective-permute-done((bf16[176,128]{1,0:T(8,128)(2,1)S(1)}, bf16[176,128]{1,0:T(8,128)(2,1)S(1)}, u32[]{:S(2)}, u32[]{:S(2)}) %collective-permute-start.7) | collective-permute-done | bytes 45088 | tf_op jit(solution)/shard_map/ppermute | solution.py:980
  35.8 0.7 %all-to-all-done = f32[32,1,1408]{2,1,0:T(1,128)S(1)} async-done(((f32[32,1,1408]{2,1,0:T(1,128)}), f32[32,1,1408]{2,1,0:T(1,128)S(1)}, u32[]{:S(2)}, u32[]{:S(2)}) %all-to-all-start) | async-done | bytes 180256 | tf_op jit(solution)/shard_map/all_to_all | solution.py:950
  36.5 3.4 %shard_map.134 = (f32[768,128]{1,0:T(8,128)S(1)}, bf16[176,128]{1,0:T(8,128)(2,1)S(1)}, bf16[176,128]{1,0:T(8,128)(2,1)S(1)}, f32[768,128]{1,0:T(8,128)S(1)}, f32[6,128]{1,0:T(8,128)S(1)}) custom-call(f32[352,128]{1,0:T(8,128)S(1)} %bitcast.5, bf16[729,729]{1,0:T(8,128)(2,1)} %copy-done.5, bf16[729,729]{1,0:T(8,128)(2,1)S(1)} %get-tuple-element.76.high_ref, ...), custom_call_target="tpu_custom_call" | custom-call | bytes 12000000 | tf_op jit(solution)/shard_map/pallas_call | solution.py:818
  39.9 1.1 %collective-permute-start.8 = (bf16[176,128]{1,0:T(8,128)(2,1)S(1)}, bf16[176,128]{1,0:T(8,128)(2,1)S(1)}, u32[]{:S(2)}, u32[]{:S(2)}) collective-permute-start(bf16[176,128]{1,0:T(8,128)(2,1)S(1)} %get-tuple-element.81), channel_id=1, source_target_pairs={{0,1},{1,0},{2,3},{3,2},{4,5},{5,4},{6,7},{7,6},{8,9},{9,8},{10,11... | collective-permute-start | bytes 135176 | tf_op jit(solution)/shard_map/ppermute | solution.py:981
  41.0 0.4 collective-permute-start.9
  41.4 1.8 %shard_map.135.refs_0_ = f32[768,128]{1,0:T(8,128)S(1)} custom-call(f32[768,128]{1,0:T(8,128)S(1)} %get-tuple-element.79.refs_0_, f32[768,128]{1,0:T(8,128)S(1)} %get-tuple-element.74.refs_0_.y_ref.refs_1_, f32[768,128]{1,0:T(8,128)} %copy-done, f32[768,128]{1,0:T(8,128)S(1)} %get-tuple-element.80.refs_3_, bf16[352,352]{1,0:T(8,128)(2,1)} %copy-done.2, ...), custom_call_target="tpu_custom_call" | custom-call | bytes 6000000 | tf_op jit(solution)/shard_map/pallas_call | solution.py:348
  43.2 0.0 collective-permute-done.8.refs_1_
  43.2 3.1 %collective-permute-done.9.refs_2_ = bf16[176,128]{1,0:T(8,128)(2,1)S(1)} collective-permute-done((bf16[176,128]{1,0:T(8,128)(2,1)S(1)}, bf16[176,128]{1,0:T(8,128)(2,1)S(1)}, u32[]{:S(2)}, u32[]{:S(2)}) %collective-permute-start.9) | collective-permute-done | bytes 45088 | tf_op jit(solution)/shard_map/ppermute | solution.py:980
  46.3 1.0 %shard_map.136 = (f32[768,128]{1,0:T(8,128)}, f32[6,128]{1,0:T(8,128)}) custom-call(f32[768,128]{1,0:T(8,128)S(1)} %shard_map.135.refs_0_, bf16[176,128]{1,0:T(8,128)(2,1)S(1)} %collective-permute-done.8.refs_1_, bf16[176,128]{1,0:T(8,128)(2,1)S(1)} %collective-permute-done.9.refs_2_, bf16[304,176]{1,0:T(8,128)(2,1)S(1)} %get-tuple-element.56.refs_2_.refs_3_.refs_0_, ...), custom_call_target="tpu_custom_call" | custom-call | bytes 3000000 | tf_op jit(solution)/shard_map/pallas_call | solution.py:527
  (1 shorter events, 0.0 us)
Async XLA Ops:
  1.9 7.4 %collective-permute-start = (bf16[464,128]{1,0:T(8,128)(2,1)S(1)}, bf16[464,128]{1,0:T(8,128)(2,1)S(1)}, u32[]{:S(2)}, u32[]{:S(2)}) collective-permute-start(bf16[464,128]{1,0:T(8,128)(2,1)S(1)} %get-tuple-element.44), channel_id=1, source_target_pairs={{0,1},{1,2},{2,3},{3,4},{4,5},{5,6},{6,7},{7,0},{8,9},{9,10},{10,1... | collective-permute-start | bytes 356360 | tf_op jit(solution)/shard_map/ppermute | solution.py:32
  2.5 7.9 %collective-permute-start.1 = (bf16[176,128]{1,0:T(8,128)(2,1)S(1)}, bf16[176,128]{1,0:T(8,128)(2,1)S(1)}, u32[]{:S(2)}, u32[]{:S(2)}) collective-permute-start(bf16[176,128]{1,0:T(8,128)(2,1)S(1)} %get-tuple-element.54.own_up_ref), channel_id=1, source_target_pairs={{0,7},{1,0},{2,1},{3,2},{4,3},{5,4},{6,5},{7,6},{8,15},{9,8},{10,9... | collective-permute-start | bytes 135176 | tf_op jit(solution)/shard_map/ppermute | solution.py:32
  8.8 22.8 %copy-start = (f32[768,128]{1,0:T(8,128)}, f32[768,128]{1,0:T(8,128)S(1)}, u32[]{:S(2)}) copy-start(f32[768,128]{1,0:T(8,128)S(1)} %get-tuple-element.49.refs_1_.refs_2_) | copy-start | bytes 1179652
  8.9 22.7 %copy-start.1 = (bf16[368,368]{1,0:T(8,128)(2,1)}, bf16[368,368]{1,0:T(8,128)(2,1)S(1)}, u32[]{:S(2)}) copy-start(bf16[368,368]{1,0:T(8,128)(2,1)S(1)} %get-tuple-element.51.refs_3_.refs_4_.refs_5_) | copy-start | bytes 812548
  8.9 22.7 %copy-start.2 = (bf16[352,352]{1,0:T(8,128)(2,1)}, bf16[352,352]{1,0:T(8,128)(2,1)S(1)}, u32[]{:S(2)}) copy-start(bf16[352,352]{1,0:T(8,128)(2,1)S(1)} %get-tuple-element.50.refs_2_.refs_3_.refs_4_) | copy-start | bytes 743428
  8.9 22.7 %copy-start.3 = (bf16[304,304]{1,0:T(8,128)(2,1)}, bf16[304,304]{1,0:T(8,128)(2,1)S(1)}, u32[]{:S(2)}) copy-start(bf16[304,304]{1,0:T(8,128)(2,1)S(1)} %get-tuple-element.52.refs_4_.refs_5_.refs_6_) | copy-start | bytes 554500
  8.9 22.7 %copy-start.4 = (bf16[192,192]{1,0:T(8,128)(2,1)}, bf16[192,192]{1,0:T(8,128)(2,1)S(1)}, u32[]{:S(2)}) copy-start(bf16[192,192]{1,0:T(8,128)(2,1)S(1)} %get-tuple-element.53.refs_5_.refs_6_.refs_7_) | copy-start | bytes 221188
  10.8 2.9 %collective-permute-start.2 = (bf16[176,128]{1,0:T(8,128)(2,1)S(1)}, bf16[176,128]{1,0:T(8,128)(2,1)S(1)}, u32[]{:S(2)}, u32[]{:S(2)}) collective-permute-start(bf16[176,128]{1,0:T(8,128)(2,1)S(1)} %get-tuple-element.63), channel_id=1, source_target_pairs={{0,1},{1,0},{2,3},{3,2},{4,5},{5,4},{6,7},{7,6},{8,9},{9,8},{10,11... | collective-permute-start | bytes 135176 | tf_op jit(solution)/shard_map/ppermute | solution.py:981
  10.9 5.3 %collective-permute-start.3 = (bf16[176,128]{1,0:T(8,128)(2,1)S(1)}, bf16[176,128]{1,0:T(8,128)(2,1)S(1)}, u32[]{:S(2)}, u32[]{:S(2)}) collective-permute-start(bf16[176,128]{1,0:T(8,128)(2,1)S(1)} %get-tuple-element.64), channel_id=1, source_target_pairs={{0,7},{1,2},{2,1},{3,4},{4,3},{5,6},{6,5},{7,0},{8,15},{9,10},{10,... | collective-permute-start | bytes 135176 | tf_op jit(solution)/shard_map/ppermute | solution.py:980
  16.7 3.5 %collective-permute-start.4 = (bf16[176,128]{1,0:T(8,128)(2,1)S(1)}, bf16[176,128]{1,0:T(8,128)(2,1)S(1)}, u32[]{:S(2)}, u32[]{:S(2)}) collective-permute-start(bf16[176,128]{1,0:T(8,128)(2,1)S(1)} %get-tuple-element.66), channel_id=1, source_target_pairs={{0,1},{1,0},{2,3},{3,2},{4,5},{5,4},{6,7},{7,6},{8,9},{9,8},{10,11... | collective-permute-start | bytes 135176 | tf_op jit(solution)/shard_map/ppermute | solution.py:981
  16.8 5.3 %collective-permute-start.5 = (bf16[176,128]{1,0:T(8,128)(2,1)S(1)}, bf16[176,128]{1,0:T(8,128)(2,1)S(1)}, u32[]{:S(2)}, u32[]{:S(2)}) collective-permute-start(bf16[176,128]{1,0:T(8,128)(2,1)S(1)} %get-tuple-element.67), channel_id=1, source_target_pairs={{0,7},{1,2},{2,1},{3,4},{4,3},{5,6},{6,5},{7,0},{8,15},{9,10},{10,... | collective-permute-start | bytes 135176 | tf_op jit(solution)/shard_map/ppermute | solution.py:980
  23.3 13.2 %all-to-all-start = ((f32[32,1,1408]{2,1,0:T(1,128)}), f32[32,1,1408]{2,1,0:T(1,128)S(1)}, u32[]{:S(2)}, u32[]{:S(2)}) async-start(f32[32,1,1408]{2,1,0:T(1,128)} %get-tuple-element.73), calls=%async_computation | async-start | bytes 360448 | tf_op jit(solution)/shard_map/all_to_all | solution.py:950
  27.8 7.0 %collective-permute-start.6 = (bf16[176,128]{1,0:T(8,128)(2,1)S(1)}, bf16[176,128]{1,0:T(8,128)(2,1)S(1)}, u32[]{:S(2)}, u32[]{:S(2)}) collective-permute-start(bf16[176,128]{1,0:T(8,128)(2,1)S(1)} %get-tuple-element.77), channel_id=1, source_target_pairs={{0,1},{1,0},{2,3},{3,2},{4,5},{5,4},{6,7},{7,6},{8,9},{9,8},{10,11... | collective-permute-start | bytes 135176 | tf_op jit(solution)/shard_map/ppermute | solution.py:981
  28.1 7.7 %collective-permute-start.7 = (bf16[176,128]{1,0:T(8,128)(2,1)S(1)}, bf16[176,128]{1,0:T(8,128)(2,1)S(1)}, u32[]{:S(2)}, u32[]{:S(2)}) collective-permute-start(bf16[176,128]{1,0:T(8,128)(2,1)S(1)} %get-tuple-element.78), channel_id=1, source_target_pairs={{0,7},{1,2},{2,1},{3,4},{4,3},{5,6},{6,5},{7,0},{8,15},{9,10},{10,... | collective-permute-start | bytes 135176 | tf_op jit(solution)/shard_map/ppermute | solution.py:980
  33.8 1.0 %copy-start.5 = (bf16[729,729]{1,0:T(8,128)(2,1)}, bf16[729,729]{1,0:T(8,128)(2,1)S(1)}, u32[]{:S(2)}) copy-start(bf16[729,729]{1,0:T(8,128)(2,1)S(1)} %get-tuple-element.75.low_hbm) | copy-start | bytes 3188650
  39.9 3.3 %collective-permute-start.8 = (bf16[176,128]{1,0:T(8,128)(2,1)S(1)}, bf16[176,128]{1,0:T(8,128)(2,1)S(1)}, u32[]{:S(2)}, u32[]{:S(2)}) collective-permute-start(bf16[176,128]{1,0:T(8,128)(2,1)S(1)} %get-tuple-element.81), channel_id=1, source_target_pairs={{0,1},{1,0},{2,3},{3,2},{4,5},{5,4},{6,7},{7,6},{8,9},{9,8},{10,11... | collective-permute-start | bytes 135176 | tf_op jit(solution)/shard_map/ppermute | solution.py:981
  41.0 5.3 %collective-permute-start.9 = (bf16[176,128]{1,0:T(8,128)(2,1)S(1)}, bf16[176,128]{1,0:T(8,128)(2,1)S(1)}, u32[]{:S(2)}, u32[]{:S(2)}) collective-permute-start(bf16[176,128]{1,0:T(8,128)(2,1)S(1)} %get-tuple-element.82), channel_id=1, source_target_pairs={{0,7},{1,2},{2,1},{3,4},{4,3},{5,6},{6,5},{7,0},{8,15},{9,10},{10,... | collective-permute-start | bytes 135176 | tf_op jit(solution)/shard_map/ppermute | solution.py:980
